TPU v7x, 32 devices: a whole 2x2x4 slice. The times are simulated.
32 devices in a mesh: chaos: 8 (over z, x), space: 4 (over y, core).
Axes of the slice: x: 2, y: 2, z: 4, core: 2. Of those that a mesh axis runs over, the one named last changes fastest.
Arguments:
- coeffs: float32 [64, 16, 32, 128], P('chaos', 'space'), may hold values from -6 to 6
- source: float32 [64, 16, 32, 128], P('chaos', 'space'), may hold values from -6 to 6
- mean_field: float32 [16, 32, 128], P('space'), may hold values from 0.5 to 2
- mode_bank: float32 [8, 16, 32, 128], P('chaos', 'space'), may hold values from -2.4 to 2.4
- mode_owner: int32 [2], replicated, may hold values from 0 to 7, as said below
- links: int32 [8, 32, 4], P('chaos'), may hold values from 0 to 63, as said below
Outputs:
- residual: float32 [64, 16, 32, 128], P('chaos', 'space')
- correction: float32 [64, 16, 32, 128], P('chaos', 'space')
Inputs may be any that keep to these rules, and one draw needn't show every extreme that they name: `mode_owner`: 2 distinct slots. Entry (s, p, k, L) of links[d]: s a coefficient among device d's 8, p a global destination coefficient, k a mode, L a level from 0 to 3, where level 0 marks a pair that is absent. Every pair appears in both directions with one level. One device's list names coefficients of one destination device at most 5 times, and some device's list does so exactly 5 times with all those entries present.
All inputs are finite; a program needn't handle non-finite values.
Results may differ from a plain program's by a relative error of at most 0.00015.
Values sent between devices are 32-bit elements; how exact they have to be, the bound alone decides.
No kernel may reach another device: no remote copies, remote signals or barrier semaphores. Data moves between devices by JAX's collectives and lax.ppermute only.
A program may use at most 128 MiB of HBM per device.

v0:
```python
import functools

import jax
import jax.numpy as jnp
from jax import lax
from jax.experimental import pallas as pl
from jax.experimental.pallas import tpu as pltpu
from jax.sharding import PartitionSpec as P


M = 2
ITERS = 4

REACTION = 0.5
BOUND_LOW = 0.04
BOUND_HIGH = 2.0

CHUNKS = 2
TABLE_ROWS = 8


VMEM = pl.BlockSpec(memory_space=pltpu.VMEM)
SMEM = pl.BlockSpec(memory_space=pltpu.SMEM)


def cost(planes, nx, ny, flops):
    return pl.CostEstimate(
        flops=flops * planes * nx * ny, bytes_accessed=8 * planes * nx * ny, transcendentals=0
    )


def shifted(values, axis, step):
    return pltpu.roll(values, step % values.shape[axis], axis)


def faces(below, own, above):
    nx, ny = own.shape
    ix = lax.broadcasted_iota(jnp.int32, (nx, ny), 0)
    iy = lax.broadcasted_iota(jnp.int32, (nx, ny), 1)
    half = 0.5 * own
    zero = jnp.zeros_like(own)
    xm = jnp.where(ix == 0, zero, half + shifted(half, 0, 1))
    xp = jnp.where(ix == nx - 1, zero, half + shifted(half, 0, -1))
    ym = jnp.where(iy == 0, zero, half + shifted(half, 1, 1))
    yp = jnp.where(iy == ny - 1, zero, half + shifted(half, 1, -1))
    up = half + 0.5 * above
    down = half + 0.5 * below
    total = up + down
    total = total + jnp.where(ix == 0, half, xm) + jnp.where(ix == nx - 1, half, xp)
    total = total + jnp.where(iy == 0, half, ym) + jnp.where(iy == ny - 1, half, yp)
    return xm, xp, ym, yp, down, up, total


def lateral(to_xm, to_xp, to_ym, to_yp):
    return (
        shifted(to_xm, 0, -1)
        + shifted(to_xp, 0, 1)
        + shifted(to_ym, 1, -1)
        + shifted(to_yp, 1, 1)
    )


def sum_kernel(n_blocks, coef_dev, entries, rows, slot_rows, scan, more, *refs):
    refs = list(refs)
    where = refs.pop(0) if scan else None
    given = None if scan else [refs.pop(0) for _ in range(3)]
    blocks = [refs.pop(0) for _ in range(n_blocks)]
    so_far = [refs.pop(0) for _ in range(2)] if more else [None] * 2
    own, other = refs.pop(0), refs.pop(0)
    lists, weights, counts = [refs.pop(0) for _ in range(3)] if scan else given
    outs = (own, other)
    targets = coef_dev * M

    def add(block, code, w, out):
        row, target = lax.div(code, targets), lax.rem(code, targets)
        at = pl.ds(pl.multiple_of(target * rows, rows), rows)
        src = block[pl.ds(pl.multiple_of(row * rows, rows), rows), :]
        out[at, :] = out[at, :] + w * src

    if scan:
        tables, sems = refs
        table_at = coef_dev * rows + slot_rows
        copies = [
            pltpu.make_async_copy(b.at[pl.ds(table_at, TABLE_ROWS)], tables.at[i], sems.at[i])
            for i, b in enumerate(blocks)
        ]
        for copy in copies:
            copy.start()
    for out, start in zip(outs, so_far):
        out[...] = start[...] if more else jnp.zeros_like(out)
    if scan:
        for copy in copies:
            copy.wait()
        names = [where[kind].astype(jnp.float32) for kind in range(2)]
    for i, b in enumerate(blocks):
        if scan:
            for kind in range(2):
                counts[2 * i + kind] = 0

            def look(e, carry, b=b, i=i):
                name = tables[i, 0, e]
                for kind, out in enumerate(outs):

                    @pl.when(name == names[kind])
                    def _(kind=kind, out=out):
                        slot = 2 * i + kind
                        code = tables[i, 1, e].astype(jnp.int32)
                        w = tables[i, 2, e]
                        at = counts[slot]
                        lists[slot * entries + at] = code
                        weights[slot * entries + at] = w
                        counts[slot] = at + 1
                        add(b, code, w, out)

                return carry

            lax.fori_loop(0, entries, look, 0)
            for k in range(M):

                @pl.when(where[2 + k] == where[2 + M + i])
                def _(b=b, k=k):
                    at = pl.ds(targets * rows + k * slot_rows, slot_rows)
                    slot = b[pl.ds(coef_dev * rows, slot_rows), :]
                    own[at, :] = own[at, :] + slot
                    other[at, :] = other[at, :] + slot

        else:
            for kind, out in enumerate(outs):
                slot = 2 * i + kind

                def listed(e, carry, b=b, out=out, slot=slot):
                    add(b, lists[slot * entries + e], weights[slot * entries + e], out)
                    return carry

                lax.fori_loop(0, counts[slot], listed, 0)


def sum_blocks(blocks, coef_dev, entries, rows, slot_rows, where, lists, so_far):
    scan, more, n = lists is None, so_far is not None, len(blocks)
    lanes = blocks[0].shape[1]
    size = coef_dev * M * rows + (M * slot_rows if scan else 0)
    total = jax.ShapeDtypeStruct((size, lanes), jnp.float32)
    out_shape, out_specs, scratch = [total, total], [VMEM, VMEM], []
    if scan:
        out_shape += [
            jax.ShapeDtypeStruct((2 * n * entries,), jnp.int32),
            jax.ShapeDtypeStruct((2 * n * entries,), jnp.float32),
            jax.ShapeDtypeStruct((2 * n,), jnp.int32),
        ]
        out_specs += [SMEM] * 3
        scratch = [
            pltpu.SMEM((n, TABLE_ROWS, lanes), jnp.float32),
            pltpu.SemaphoreType.DMA((n,)),
        ]
    small = [where] if scan else list(lists)
    operands = small + list(blocks) + (list(so_far) if more else [])
    got = pl.pallas_call(
        functools.partial(
            sum_kernel, n, coef_dev, entries, rows, slot_rows if scan else 0, scan, more
        ),
        out_shape=out_shape,
        in_specs=[SMEM] * len(small) + [VMEM] * (len(operands) - len(small)),
        out_specs=out_specs,
        scratch_shapes=scratch,
        compiler_params=pltpu.CompilerParams(vmem_limit_bytes=12 << 20),
        cost_estimate=cost(coef_dev * M, rows, lanes, 4),
    )(*operands)
    return got[:2], (lists if lists is not None else got[2:])


def exchange_pairs(count, inner, mask, keep=lambda o: True):
    return [
        (o * inner + i, (o ^ mask) * inner + i)
        for o in range(count)
        for i in range(inner)
        if keep(o)
    ]


def line_of_four(block, inner):
    middle = (1, 2)
    far = lax.ppermute(block, "chaos", exchange_pairs(4, inner, 2))
    near = lax.ppermute(block, "chaos", exchange_pairs(4, inner, 1))
    mid = lax.ppermute(block, "chaos", exchange_pairs(4, inner, 3, lambda o: o in middle))
    relay = lax.ppermute(far, "chaos", exchange_pairs(4, inner, 1, lambda o: o in middle))
    return near, far, mid, relay


def column_sums(coef_dev, entries, rows, slot_rows, wanted, owners):
    targets = coef_dev * M

    def sums(block, table, device):
        ids = table[:2, :entries].astype(jnp.int32)
        w = table[2, :entries]
        source_row, target = ids[1] // targets, ids[1] % targets
        picked = (source_row[:, None] == jnp.arange(coef_dev)[None, :]).astype(jnp.float32)
        found = []
        for who in wanted:
            mine = jnp.where(ids[0] == who + 1, w, 0.0)
            onehot = (jnp.arange(targets)[:, None] == target[None, :]).astype(jnp.float32)
            matrix = jnp.sum(
                (onehot * mine[None, :])[:, :, None] * picked[None, :, :], axis=1
            )
            data = block[: coef_dev * rows].reshape(coef_dev, -1)
            found.append(
                jnp.dot(matrix, data, precision=lax.Precision.HIGHEST).reshape(
                    targets * rows, -1
                )
            )
        if slot_rows:
            slot = block[coef_dev * rows : coef_dev * rows + slot_rows]
            part = jnp.concatenate(
                [jnp.where(owners[k] == device, slot, 0.0) for k in range(M)], axis=0
            )
            found = [jnp.concatenate([f, part], axis=0) for f in found]
        return found

    return sums


def grid_of(count):
    inner = 2 if count % 2 == 0 else 1
    return count // inner, inner


def chaos_sums(chunks, coef_dev, entries, rows_of, slot_rows, mode_owner):
    outer, inner = grid_of(lax.axis_size("chaos"))
    me = lax.axis_index("chaos")
    my_outer, my_inner = me // inner, me % inner
    neighbour = my_outer * inner + (inner - 1 - my_inner)
    found = []
    if outer == 4:
        where = jnp.stack(
            [me + 1, neighbour + 1]
            + [mode_owner[k] for k in range(M)]
            + [(my_outer ^ mask) * inner + my_inner for mask in (0, 1, 2, 3, 3)]
        ).astype(jnp.int32)
        head = 2 + M
        relay_where = jnp.concatenate([where[:head], where[head + 4 :]])
        lists = late_lists = None
        gathered = [line_of_four(c, inner) for c in chunks]
        for j, (chunk, (near, far, mid, relay)) in enumerate(zip(chunks, gathered)):
            args = (coef_dev, entries, rows_of[j], slot_rows)
            sums, lists = sum_blocks([chunk, near, far, mid], *args, where, lists, None)
            sums, late_lists = sum_blocks([relay], *args, relay_where, late_lists, sums)
            found.append(sums)
    else:
        ring = [
            (o * inner + i, ((o + 1) % outer) * inner + i)
            for o in range(outer)
            for i in range(inner)
        ]
        table_at = coef_dev * rows_of[0] + slot_rows

        def at_step(step, blocks):
            device = ((my_outer - step) % outer) * inner + my_inner
            table = blocks[0][table_at : table_at + TABLE_ROWS]
            return [
                tuple(
                    column_sums(
                        coef_dev,
                        entries,
                        rows_of[j],
                        slot_rows if j == 0 else 0,
                        (me, neighbour),
                        mode_owner,
                    )(block, table, device)
                )
                for j, block in enumerate(blocks)
            ]

        def body(step, carry):
            blocks, sums = carry
            blocks = [lax.ppermute(b, "chaos", ring) for b in blocks]
            return blocks, jax.tree.map(jnp.add, sums, at_step(step, blocks))

        _, found = lax.fori_loop(1, outer, body, (list(chunks), at_step(0, chunks)))
    if inner == 1:
        return [own for own, _ in found]
    across = [
        (o * inner + i, o * inner + inner - 1 - i) for o in range(outer) for i in range(inner)
    ]
    full = []
    for own, other in found:
        got = lax.ppermute(other, "chaos", across)
        full.append(own + got)
    return full


def depth_pair(values):
    count = lax.axis_size("space")
    first = [(i, i ^ 1) for i in range(count) if i ^ 1 < count]
    second = [
        (i, j)
        for i in range(count)
        for j in [i - 1 if i % 2 == 0 else i + 1]
        if 0 <= j < count
    ]
    other = lax.ppermute(values, "space", second)
    pair = lax.ppermute(values, "space", first)
    return other, pair


def base_kernel(coef_dev, depth, n_space, space_ref, coeffs, source, mean, *refs):
    other, pair, known, face, coef_ext, mean_ext = refs
    index = space_ref[0]
    even = lax.rem(index, 2) == 0
    pair_at = jnp.where(even, 2 * depth, 0)
    other_at = jnp.where(even, 0, 2 * depth)
    total_layers = 3 * depth
    planes = coef_dev * depth

    for at, part in ((pair_at, pair), (other_at, other)):
        for c in range(coef_dev):
            coef_ext[c, pl.ds(at, depth)] = part[c * depth : (c + 1) * depth]
        mean_ext[pl.ds(at, depth)] = part[2 * planes : 2 * planes + depth]
    for c in range(coef_dev):
        coef_ext[c, depth : 2 * depth] = coeffs[c]
    mean_ext[depth : 2 * depth] = mean[...]

    def layer(l, source_of):
        xm, xp, ym, yp, down, up, total = faces(mean_ext[l - 1], mean_ext[l], mean_ext[l + 1])
        diagonal = REACTION + total
        absolute = index * depth + l - depth
        inside = (absolute >= 0) & (absolute < n_space * depth)
        face[0, l], face[1, l], face[2, l], face[3, l] = xm, xp, ym, yp
        face[4, l], face[5, l] = down, up
        face[6, l] = jnp.where(inside, 1.0 / diagonal, 0.0)

        def coefficient(c, carry):
            v = coef_ext[c, l]
            spread = lateral(xm * v, xp * v, ym * v, yp * v)
            spread = spread + down * coef_ext[c, l - 1] + up * coef_ext[c, l + 1]
            known[c, l] = source_of(c) - (diagonal * v - spread)
            return carry

        for c in range(coef_dev):
            coefficient(c, 0)

    def from_part(part, at):
        def body(l, carry):
            layer(l, lambda c: part[planes + c * depth + l - at])
            return carry

        lax.fori_loop(jnp.maximum(at, 1), jnp.minimum(at + depth, total_layers - 1), body, 0)

    from_part(pair, pair_at)
    from_part(other, other_at)

    def body(l, carry):
        layer(l, lambda c: source[c, l - depth])
        return carry

    lax.fori_loop(depth, 2 * depth, body, 0)


def sweep_constants():
    midpoint = (BOUND_HIGH + BOUND_LOW) / 2.0
    halfwidth = (BOUND_HIGH - BOUND_LOW) / 2.0
    ratio = midpoint / halfwidth
    now = 1.0 / ratio
    steps = []
    for _ in range(ITERS - 1):
        following = 1.0 / (2.0 * ratio - now)
        steps.append((following * now, 2.0 * following / halfwidth))
        now = following
    return midpoint, steps


def sweep_kernel(coef_dev, depth, layer_counts, space_ref, known, face, *refs):
    n = len(layer_counts)
    parts = [refs[3 * j : 3 * j + 3] for j in range(n)]
    residual, correction, summed, mode_ext, mode_face, scaled, first, second = refs[3 * n :]
    nx, _ = known.shape[2:]
    targets = coef_dev * M
    even = lax.rem(space_ref[0], 2) == 0
    pair_at = jnp.where(even, 2 * depth, 0)
    other_at = jnp.where(even, 0, 2 * depth)
    last = 3 * depth - 1

    start = 0
    for j, (trio, layers) in enumerate(zip(parts, layer_counts)):
        for part, at in zip(trio, (depth, other_at, pair_at)):
            for t in range(targets):
                for l in range(layers):
                    row = (t * layers + l) * nx
                    summed[t, at + start + l] = part[row : row + nx]
            if j == 0:
                for k in range(M):
                    for l in range(depth):
                        row = (targets * layers + k * depth + l) * nx
                        mode_ext[k, at + l] = part[row : row + nx]
        start += layers

    def mode_faces(l, carry):
        for k in range(M):
            got = faces(mode_ext[k, l - 1], mode_ext[k, l], mode_ext[k, l + 1])
            for i, value in enumerate(got):
                mode_face[k, i, l] = value
        return carry

    lax.fori_loop(1, last, mode_faces, 0)
    midpoint, steps = sweep_constants()

    def coupled(l, own):
        for c in range(coef_dev):
            to = [None] * 4
            rest = known[c, l]
            for k in range(M):
                v = summed[c * M + k, l]
                for i in range(4):
                    term = mode_face[k, i, l] * v
                    to[i] = term if to[i] is None else to[i] + term
                rest = rest - mode_face[k, 6, l] * v
                rest = rest + mode_face[k, 4, l] * summed[c * M + k, l - 1]
                rest = rest + mode_face[k, 5, l] * summed[c * M + k, l + 1]
            rest = rest + lateral(*to)
            w = rest * face[6, l]
            d = w * (1.0 / midpoint)
            scaled[c, l] = w
            first[c, l] = d
            if own:
                residual[c, l - depth] = rest
                correction[c, l - depth] = d

    over_layers(coupled, depth, depth - 1)

    now, later = first, second
    for number, (keep, gain) in enumerate(steps):

        def swept(l, own, now=now, later=later, keep=keep, gain=gain, number=number):
            for c in range(coef_dev):
                v = now[c, l]
                spread = lateral(face[0, l] * v, face[1, l] * v, face[2, l] * v, face[3, l] * v)
                spread = spread + face[4, l] * now[c, l - 1] + face[5, l] * now[c, l + 1]
                w = scaled[c, l] - v + face[6, l] * spread
                d = keep * v + gain * w
                if number + 1 < len(steps):
                    scaled[c, l] = w
                    later[c, l] = d
                if own:
                    correction[c, l - depth] = correction[c, l - depth] + d

        over_layers(swept, depth, len(steps) - 1 - number)
        now, later = later, now


def over_layers(visit, depth, halo):
    def own(l, carry):
        visit(l, True)
        return carry

    def outside(i, carry):
        visit(jnp.where(i < halo, depth - halo + i, 2 * depth - halo + i), False)
        return carry

    lax.fori_loop(depth, 2 * depth, own, 0)
    if halo:
        lax.fori_loop(0, 2 * halo, outside, 0)


def residual_and_correction(coeffs, source, mean_field, mode_bank, mode_owner, links):
    coef_dev, depth, nx, ny = coeffs.shape
    n_space = lax.axis_size("space")
    entries = links.shape[1]
    slot_rows = depth * nx
    per_chunk = depth // CHUNKS
    layer_counts = [per_chunk] * CHUNKS
    index = lax.axis_index("space").astype(jnp.int32).reshape(1)

    s, p, k, level = (links[0, :, i] for i in range(4))
    table = jnp.stack(
        [
            jnp.where(level > 0, p // coef_dev + 1, 0).astype(jnp.float32),
            ((s * coef_dev + p % coef_dev) * M + k).astype(jnp.float32),
            jnp.sqrt(level.astype(jnp.float32)),
        ]
    )
    table = jnp.pad(table, ((0, TABLE_ROWS - 3), (0, ny - entries)))
    chunks, start = [], 0
    for j, layers in enumerate(layer_counts):
        piece = coeffs[:, start : start + layers].reshape(-1, ny)
        if j == 0:
            piece = jnp.concatenate([piece, mode_bank[0].reshape(-1, ny), table], axis=0)
        chunks.append(piece)
        start += layers

    sums = chaos_sums(
        chunks, coef_dev, entries, [layers * nx for layers in layer_counts], slot_rows, mode_owner
    )

    early = jnp.concatenate(
        [coeffs.reshape(-1, nx, ny), source.reshape(-1, nx, ny), mean_field], axis=0
    )
    other, pair = depth_pair(early)
    wide = (coef_dev, 3 * depth, nx, ny)
    known, face = pl.pallas_call(
        functools.partial(base_kernel, coef_dev, depth, n_space),
        out_shape=(
            jax.ShapeDtypeStruct(wide, jnp.float32),
            jax.ShapeDtypeStruct((7, 3 * depth, nx, ny), jnp.float32),
        ),
        in_specs=[SMEM] + [VMEM] * 5,
        out_specs=(VMEM, VMEM),
        scratch_shapes=[
            pltpu.VMEM(wide, jnp.float32),
            pltpu.VMEM((3 * depth, nx, ny), jnp.float32),
        ],
        cost_estimate=cost(3 * depth * coef_dev, nx, ny, 20),
        compiler_params=pltpu.CompilerParams(vmem_limit_bytes=16 << 20),
        name="base",
    )(index, coeffs, source, mean_field, other, pair)

    parts = []
    for own in sums:
        parts += [own, *depth_pair(own)]
    out = jax.ShapeDtypeStruct(coeffs.shape, jnp.float32)
    return pl.pallas_call(
        functools.partial(sweep_kernel, coef_dev, depth, layer_counts),
        out_shape=(out, out),
        in_specs=[SMEM] + [VMEM] * (2 + len(parts)),
        out_specs=(VMEM, VMEM),
        scratch_shapes=[
            pltpu.VMEM((coef_dev * M, 3 * depth, nx, ny), jnp.float32),
            pltpu.VMEM((M, 3 * depth, nx, ny), jnp.float32),
            pltpu.VMEM((M, 7, 3 * depth, nx, ny), jnp.float32),
            pltpu.VMEM(wide, jnp.float32),
            pltpu.VMEM(wide, jnp.float32),
            pltpu.VMEM(wide, jnp.float32),
        ],
        cost_estimate=cost(6 * depth * coef_dev, nx, ny, 40),
        compiler_params=pltpu.CompilerParams(vmem_limit_bytes=24 << 20),
        name="sweeps",
    )(index, known, face, *parts)


def solution(mesh):
    in_specs = (
        P("chaos", "space", None, None),
        P("chaos", "space", None, None),
        P("space", None, None),
        P("chaos", "space", None, None),
        P(),
        P("chaos", None, None),
    )
    out_specs = (P("chaos", "space", None, None), P("chaos", "space", None, None))
    return jax.shard_map(
        residual_and_correction, mesh=mesh, in_specs=in_specs, out_specs=out_specs, check_vma=False
    )
```

profile of v0, /device:TPU:9, one launch (start us, length us, event | category | flops | bytes accessed | tf_op | source)
XLA Modules:
  0.0 102.2 jit_solution(7925035500414241992)
XLA Ops:
  2.3 1.1 %fusion.3 = (f32[8,2,32,128]{3,2,1,0:T(8,128)S(1)}, f32[8,2,32,128]{3,2,1,0:T(8,128)S(1)}) fusion(f32[8,4,32,128]{3,2,1,0:T(8,128)} %coeffs.1), kind=kLoop, calls=%fused_computation.19 | loop fusion | bytes 1048576 | tf_op jit(solution)/shard_map/slice | solution.py:482
  3.4 0.9 pad_maximum_fusion.1.refs_1_
  4.3 2.4 %collective-permute-start.2 = (f32[648,128]{1,0:T(8,128)S(1)}, f32[648,128]{1,0:T(8,128)S(1)}, u32[]{:S(2)}, u32[]{:S(2)}) collective-permute-start(f32[648,128]{1,0:T(8,128)S(1)} %pad_maximum_fusion.1.refs_1_), channel_id=1, source_target_pairs={{0,16},{4,20},{8,24},{12,28},{16,0},{20,4},{24,8},{28,12},{1,17},{... | collective-permute-start | bytes 995336 | tf_op jit(solution)/shard_map/ppermute | solution.py:182
  6.8 2.1 %collective-permute-start.5 = (f32[648,128]{1,0:T(8,128)S(1)}, f32[648,128]{1,0:T(8,128)}, u32[]{:S(2)}, u32[]{:S(2)}) collective-permute-start(f32[648,128]{1,0:T(8,128)S(1)} %pad_maximum_fusion.1.refs_1_), channel_id=1, source_target_pairs={{8,16},{12,20},{16,8},{20,12},{9,17},{13,21},{17,9},{21,13},{10,18... | collective-permute-start | bytes 995336 | tf_op jit(solution)/shard_map/ppermute | solution.py:184
  9.0 12.7 %collective-permute-done.2.refs_3_ = f32[648,128]{1,0:T(8,128)S(1)} collective-permute-done((f32[648,128]{1,0:T(8,128)S(1)}, f32[648,128]{1,0:T(8,128)S(1)}, u32[]{:S(2)}, u32[]{:S(2)}) %collective-permute-start.2) | collective-permute-done | bytes 331808 | tf_op jit(solution)/shard_map/ppermute | solution.py:182
  21.6 2.4 %collective-permute-start.3 = (f32[648,128]{1,0:T(8,128)S(1)}, f32[648,128]{1,0:T(8,128)}, u32[]{:S(2)}, u32[]{:S(2)}) collective-permute-start(f32[648,128]{1,0:T(8,128)S(1)} %collective-permute-done.2.refs_3_), channel_id=1, source_target_pairs={{8,0},{12,4},{16,24},{20,28},{9,1},{13,5},{17,25},{21,29},{10,2},{... | collective-permute-start | bytes 995336 | tf_op jit(solution)/shard_map/ppermute | solution.py:185
  24.1 1.1 %pad_maximum_fusion = f32[68,32,128]{2,1,0:T(8,128)} fusion(f32[4,32,128]{2,1,0:T(8,128)S(1)} %copy-done.2, f32[32,32,128]{2,1,0:T(8,128)S(1)} %bitcast.44, f32[32,32,128]{2,1,0:T(8,128)S(1)} %bitcast.43), kind=kLoop, calls=%fused_computation | loop fusion | flops 557056 | bytes 2228224 | tf_op jit(solution)/shard_map/concatenate | solution.py:492
  25.2 6.8 %collective-permute-start = (f32[68,32,128]{2,1,0:T(8,128)}, f32[68,32,128]{2,1,0:T(8,128)S(1)}, u32[]{:S(2)}, u32[]{:S(2)}) collective-permute-start(f32[68,32,128]{2,1,0:T(8,128)} %pad_maximum_fusion), channel_id=1, source_target_pairs={{1,2},{2,1},{5,6},{6,5},{9,10},{10,9},{13,14},{14,13},{17,18},{18,... | collective-permute-start | bytes 3342344 | tf_op jit(solution)/shard_map/ppermute | solution.py:299
  32.0 7.5 %collective-permute-done.9.refs_5_ = f32[512,128]{1,0:T(8,128)} collective-permute-done((f32[512,128]{1,0:T(8,128)S(1)}, f32[512,128]{1,0:T(8,128)}, u32[]{:S(2)}, u32[]{:S(2)}) %collective-permute-start.9) | collective-permute-done | bytes 262176 | tf_op jit(solution)/shard_map/ppermute | solution.py:182
  40.0 5.0 %collective-permute-start.12 = (f32[512,128]{1,0:T(8,128)S(1)}, f32[512,128]{1,0:T(8,128)}, u32[]{:S(2)}, u32[]{:S(2)}) collective-permute-start(f32[512,128]{1,0:T(8,128)S(1)} %bitcast.47), channel_id=1, source_target_pairs={{8,16},{12,20},{16,8},{20,12},{9,17},{13,21},{17,9},{21,13},{10,18... | collective-permute-start | bytes 786440 | tf_op jit(solution)/shard_map/ppermute | solution.py:184
  45.0 2.0 %collective-permute-start.10 = (f32[512,128]{1,0:T(8,128)}, f32[512,128]{1,0:T(8,128)}, u32[]{:S(2)}, u32[]{:S(2)}) collective-permute-start(f32[512,128]{1,0:T(8,128)} %collective-permute-done.9.refs_5_), channel_id=1, source_target_pairs={{8,0},{12,4},{16,24},{20,28},{9,1},{13,5},{17,25},{21,29},{10,2},{... | collective-permute-start | bytes 786440 | tf_op jit(solution)/shard_map/ppermute | solution.py:185
  47.1 5.7 %shard_map.77 = (f32[1280,128]{1,0:T(8,128)S(1)}, f32[1280,128]{1,0:T(8,128)S(1)}, s32[256]{0:T(256)S(1)}, f32[256]{0:T(256)S(1)}, s32[8]{0:T(128)S(1)}) custom-call(s32[9]{0:T(128)S(1)} %stack.35.refs_0_, f32[648,128]{1,0:T(8,128)S(1)} %pad_maximum_fusion.1.refs_1_, f32[648,128]{1,0:T(8,128)} %collective-permute-done.4.refs_2_, ...), custom_call_target="tpu_custom_call" | custom-call | flops 524288 | bytes 1048576 | tf_op jit(solution)/shard_map/pallas_call | solution.py:157
  52.8 2.9 %shard_map.78 = (f32[1280,128]{1,0:T(8,128)S(1)}, f32[1280,128]{1,0:T(8,128)S(1)}, s32[64]{0:T(128)S(1)}, f32[64]{0:T(128)S(1)}, s32[2]{0:T(128)S(1)}) custom-call(s32[5]{0:T(128)S(1)} %pad_add_fusion.refs_0_, f32[648,128]{1,0:T(8,128)} %collective-permute-done.3.refs_1_, f32[1280,128]{1,0:T(8,128)S(1)} %get-tuple-element.20.refs_2_, ...), custom_call_target="tpu_custom_call" | custom-call | flops 524288 | bytes 1048576 | tf_op jit(solution)/shard_map/pallas_call | solution.py:157
  55.6 1.3 %collective-permute-start.6 = (f32[1280,128]{1,0:T(8,128)S(1)}, f32[1280,128]{1,0:T(8,128)S(1)}, u32[]{:S(2)}, u32[]{:S(2)}) collective-permute-start(f32[1280,128]{1,0:T(8,128)S(1)} %get-tuple-element.23), channel_id=1, source_target_pairs={{0,4},{4,0},{8,12},{12,8},{16,20},{20,16},{24,28},{28,24},{1,5},{5... | collective-permute-start | bytes 1966088 | tf_op jit(solution)/shard_map/ppermute | solution.py:285
  56.9 1.3 %collective-permute-start.1 = (f32[68,32,128]{2,1,0:T(8,128)}, f32[68,32,128]{2,1,0:T(8,128)}, u32[]{:S(2)}, u32[]{:S(2)}) collective-permute-start(f32[68,32,128]{2,1,0:T(8,128)} %pad_maximum_fusion), channel_id=1, source_target_pairs={{0,1},{1,0},{2,3},{3,2},{4,5},{5,4},{6,7},{7,6},{8,9},{9,8},{10,11... | collective-permute-start | bytes 3342344 | tf_op jit(solution)/shard_map/ppermute | solution.py:300
  58.2 1.6 %shard_map.79 = (f32[1024,128]{1,0:T(8,128)S(1)}, f32[1024,128]{1,0:T(8,128)S(1)}) custom-call(s32[256]{0:T(256)S(1)} %get-tuple-element.27.refs_0_, f32[256]{0:T(256)S(1)} %get-tuple-element.28.refs_1_, s32[8]{0:T(128)S(1)} %get-tuple-element.29.refs_2_, f32[512,128]{1,0:T(8,128)S(1)} %bitcast.48, f32[512,128]{1,0:T(8,128)} %collective-permute-done.11.refs_4_, ...), custom_call_target="tpu_custom_call" | custom-call | flops 524288 | bytes 1048576 | tf_op jit(solution)/shard_map/pallas_call | solution.py:157
  59.8 1.0 %shard_map.80 = (f32[1024,128]{1,0:T(8,128)S(1)}, f32[1024,128]{1,0:T(8,128)S(1)}) custom-call(s32[64]{0:T(128)S(1)} %get-tuple-element.24.refs_0_, f32[64]{0:T(128)S(1)} %get-tuple-element.25.refs_1_, s32[2]{0:T(128)S(1)} %get-tuple-element.26.refs_2_, f32[512,128]{1,0:T(8,128)} %collective-permute-done.10.refs_3_, ...), custom_call_target="tpu_custom_call" | custom-call | flops 524288 | bytes 1048576 | tf_op jit(solution)/shard_map/pallas_call | solution.py:157
  61.2 9.7 %collective-permute-done.6 = f32[1280,128]{1,0:T(8,128)S(1)} collective-permute-done((f32[1280,128]{1,0:T(8,128)S(1)}, f32[1280,128]{1,0:T(8,128)S(1)}, u32[]{:S(2)}, u32[]{:S(2)}) %collective-permute-start.6) | collective-permute-done | bytes 655392 | tf_op jit(solution)/shard_map/ppermute | solution.py:285
  71.0 6.5 %collective-permute-start.7 = (f32[1280,128]{1,0:T(8,128)S(1)}, f32[1280,128]{1,0:T(8,128)}, u32[]{:S(2)}, u32[]{:S(2)}) collective-permute-start(f32[1280,128]{1,0:T(8,128)S(1)} %add.99.refs_0_), channel_id=1, source_target_pairs={{1,2},{2,1},{5,6},{6,5},{9,10},{10,9},{13,14},{14,13},{17,18},{18,... | collective-permute-start | bytes 1966088 | tf_op jit(solution)/shard_map/ppermute | solution.py:299
  77.6 4.6 %collective-permute-done.13 = f32[1024,128]{1,0:T(8,128)S(1)} collective-permute-done((f32[1024,128]{1,0:T(8,128)S(1)}, f32[1024,128]{1,0:T(8,128)S(1)}, u32[]{:S(2)}, u32[]{:S(2)}) %collective-permute-start.13) | collective-permute-done | bytes 524320 | tf_op jit(solution)/shard_map/ppermute | solution.py:285
  82.3 4.9 %collective-permute-start.14 = (f32[1024,128]{1,0:T(8,128)S(1)}, f32[1024,128]{1,0:T(8,128)}, u32[]{:S(2)}, u32[]{:S(2)}) collective-permute-start(f32[1024,128]{1,0:T(8,128)S(1)} %add.100.refs_3_), channel_id=1, source_target_pairs={{1,2},{2,1},{5,6},{6,5},{9,10},{10,9},{13,14},{14,13},{17,18},{18,... | collective-permute-start | bytes 1572872 | tf_op jit(solution)/shard_map/ppermute | solution.py:299
  87.3 3.5 %base.1 = (f32[8,12,32,128]{3,2,1,0:T(8,128)S(1)}, f32[7,12,32,128]{3,2,1,0:T(8,128)S(1)}) custom-call(s32[1]{0:T(128)} %bitcast.space_ref, f32[8,4,32,128]{3,2,1,0:T(8,128)S(1)} %copy-done, f32[8,4,32,128]{3,2,1,0:T(8,128)S(1)} %copy-done.1, f32[4,32,128]{2,1,0:T(8,128)S(1)} %copy-done.2, f32[68,32,128]{2,1,0:T(8,128)S(1)} %collective-permute-done.refs_0_, ...), custom_call_target="tpu_custom_call" | custom-call | flops 7864320 | bytes 3145728 | tf_op jit(solution)/shard_map/base/pallas_call | solution.py:497
  90.8 3.3 %collective-permute-done.14.refs_4_ = f32[1024,128]{1,0:T(8,128)} collective-permute-done((f32[1024,128]{1,0:T(8,128)S(1)}, f32[1024,128]{1,0:T(8,128)}, u32[]{:S(2)}, u32[]{:S(2)}) %collective-permute-start.14) | collective-permute-done | bytes 524320 | tf_op jit(solution)/shard_map/ppermute | solution.py:299
  94.2 8.0 %sweeps.1 = (f32[8,4,32,128]{3,2,1,0:T(8,128)}, f32[8,4,32,128]{3,2,1,0:T(8,128)}) custom-call(s32[1]{0:T(128)} %bitcast.space_ref, f32[8,12,32,128]{3,2,1,0:T(8,128)S(1)} %get-tuple-element.18.known, f32[7,12,32,128]{3,2,1,0:T(8,128)S(1)} %get-tuple-element.19.face, f32[1280,128]{1,0:T(8,128)S(1)} %add.99.refs_0_, ...), custom_call_target="tpu_custom_call" | custom-call | flops 31457280 | bytes 6291456 | tf_op jit(solution)/shard_map/sweeps/pallas_call | solution.py:518
  (32 shorter events, 3.1 us)
Async XLA Ops:
  0.6 23.5 %copy-start = (f32[8,4,32,128]{3,2,1,0:T(8,128)S(1)}, f32[8,4,32,128]{3,2,1,0:T(8,128)}, u32[]{:S(2)}) copy-start(f32[8,4,32,128]{3,2,1,0:T(8,128)} %coeffs.1) | copy-start | bytes 1572868
  0.6 23.4 %copy-start.2 = (f32[4,32,128]{2,1,0:T(8,128)S(1)}, f32[4,32,128]{2,1,0:T(8,128)}, u32[]{:S(2)}) copy-start(f32[4,32,128]{2,1,0:T(8,128)} %mean.1) | copy-start | bytes 196612
  0.7 23.4 %copy-start.1 = (f32[8,4,32,128]{3,2,1,0:T(8,128)S(1)}, f32[8,4,32,128]{3,2,1,0:T(8,128)}, u32[]{:S(2)}) copy-start(f32[8,4,32,128]{3,2,1,0:T(8,128)} %source.1) | copy-start | bytes 1572868
  4.3 17.4 %collective-permute-start.2 = (f32[648,128]{1,0:T(8,128)S(1)}, f32[648,128]{1,0:T(8,128)S(1)}, u32[]{:S(2)}, u32[]{:S(2)}) collective-permute-start(f32[648,128]{1,0:T(8,128)S(1)} %pad_maximum_fusion.1.refs_1_), channel_id=1, source_target_pairs={{0,16},{4,20},{8,24},{12,28},{16,0},{20,4},{24,8},{28,12},{1,17},{... | collective-permute-start | bytes 995336 | tf_op jit(solution)/shard_map/ppermute | solution.py:182
  6.6 33.4 %collective-permute-start.4 = (f32[648,128]{1,0:T(8,128)S(1)}, f32[648,128]{1,0:T(8,128)}, u32[]{:S(2)}, u32[]{:S(2)}) collective-permute-start(f32[648,128]{1,0:T(8,128)S(1)} %pad_maximum_fusion.1.refs_1_), channel_id=1, source_target_pairs={{0,8},{4,12},{8,0},{12,4},{16,24},{20,28},{24,16},{28,20},{1,9},{5... | collective-permute-start | bytes 995336 | tf_op jit(solution)/shard_map/ppermute | solution.py:183
  6.8 38.2 %collective-permute-start.5 = (f32[648,128]{1,0:T(8,128)S(1)}, f32[648,128]{1,0:T(8,128)}, u32[]{:S(2)}, u32[]{:S(2)}) collective-permute-start(f32[648,128]{1,0:T(8,128)S(1)} %pad_maximum_fusion.1.refs_1_), channel_id=1, source_target_pairs={{8,16},{12,20},{16,8},{20,12},{9,17},{13,21},{17,9},{21,13},{10,18... | collective-permute-start | bytes 995336 | tf_op jit(solution)/shard_map/ppermute | solution.py:184
  8.9 30.6 %collective-permute-start.9 = (f32[512,128]{1,0:T(8,128)S(1)}, f32[512,128]{1,0:T(8,128)}, u32[]{:S(2)}, u32[]{:S(2)}) collective-permute-start(f32[512,128]{1,0:T(8,128)S(1)} %bitcast.45), channel_id=1, source_target_pairs={{0,16},{4,20},{8,24},{12,28},{16,0},{20,4},{24,8},{28,12},{1,17},{... | collective-permute-start | bytes 786440 | tf_op jit(solution)/shard_map/ppermute | solution.py:182
  21.6 31.1 %collective-permute-start.3 = (f32[648,128]{1,0:T(8,128)S(1)}, f32[648,128]{1,0:T(8,128)}, u32[]{:S(2)}, u32[]{:S(2)}) collective-permute-start(f32[648,128]{1,0:T(8,128)S(1)} %collective-permute-done.2.refs_3_), channel_id=1, source_target_pairs={{8,0},{12,4},{16,24},{20,28},{9,1},{13,5},{17,25},{21,29},{10,2},{... | collective-permute-start | bytes 995336 | tf_op jit(solution)/shard_map/ppermute | solution.py:185
  24.1 15.8 %copy-start.3 = (s32[2]{0:T(128)S(1)}, s32[2]{0:T(128)}, u32[]{:S(2)}) copy-start(s32[2]{0:T(128)} %param.10) | copy-start | bytes 28
  25.2 62.0 %collective-permute-start = (f32[68,32,128]{2,1,0:T(8,128)}, f32[68,32,128]{2,1,0:T(8,128)S(1)}, u32[]{:S(2)}, u32[]{:S(2)}) collective-permute-start(f32[68,32,128]{2,1,0:T(8,128)} %pad_maximum_fusion), channel_id=1, source_target_pairs={{1,2},{2,1},{5,6},{6,5},{9,10},{10,9},{13,14},{14,13},{17,18},{18,... | collective-permute-start | bytes 3342344 | tf_op jit(solution)/shard_map/ppermute | solution.py:299
  39.5 17.4 %collective-permute-start.11 = (f32[512,128]{1,0:T(8,128)S(1)}, f32[512,128]{1,0:T(8,128)}, u32[]{:S(2)}, u32[]{:S(2)}) collective-permute-start(f32[512,128]{1,0:T(8,128)S(1)} %bitcast.46), channel_id=1, source_target_pairs={{0,8},{4,12},{8,0},{12,4},{16,24},{20,28},{24,16},{28,20},{1,9},{5... | collective-permute-start | bytes 786440 | tf_op jit(solution)/shard_map/ppermute | solution.py:183
  40.0 18.2 %collective-permute-start.12 = (f32[512,128]{1,0:T(8,128)S(1)}, f32[512,128]{1,0:T(8,128)}, u32[]{:S(2)}, u32[]{:S(2)}) collective-permute-start(f32[512,128]{1,0:T(8,128)S(1)} %bitcast.47), channel_id=1, source_target_pairs={{8,16},{12,20},{16,8},{20,12},{9,17},{13,21},{17,9},{21,13},{10,18... | collective-permute-start | bytes 786440 | tf_op jit(solution)/shard_map/ppermute | solution.py:184
  45.0 14.8 %collective-permute-start.10 = (f32[512,128]{1,0:T(8,128)}, f32[512,128]{1,0:T(8,128)}, u32[]{:S(2)}, u32[]{:S(2)}) collective-permute-start(f32[512,128]{1,0:T(8,128)} %collective-permute-done.9.refs_5_), channel_id=1, source_target_pairs={{8,0},{12,4},{16,24},{20,28},{9,1},{13,5},{17,25},{21,29},{10,2},{... | collective-permute-start | bytes 786440 | tf_op jit(solution)/shard_map/ppermute | solution.py:185
  55.6 15.3 %collective-permute-start.6 = (f32[1280,128]{1,0:T(8,128)S(1)}, f32[1280,128]{1,0:T(8,128)S(1)}, u32[]{:S(2)}, u32[]{:S(2)}) collective-permute-start(f32[1280,128]{1,0:T(8,128)S(1)} %get-tuple-element.23), channel_id=1, source_target_pairs={{0,4},{4,0},{8,12},{12,8},{16,20},{20,16},{24,28},{28,24},{1,5},{5... | collective-permute-start | bytes 1966088 | tf_op jit(solution)/shard_map/ppermute | solution.py:285
  56.9 30.4 %collective-permute-start.1 = (f32[68,32,128]{2,1,0:T(8,128)}, f32[68,32,128]{2,1,0:T(8,128)}, u32[]{:S(2)}, u32[]{:S(2)}) collective-permute-start(f32[68,32,128]{2,1,0:T(8,128)} %pad_maximum_fusion), channel_id=1, source_target_pairs={{0,1},{1,0},{2,3},{3,2},{4,5},{5,4},{6,7},{7,6},{8,9},{9,8},{10,11... | collective-permute-start | bytes 3342344 | tf_op jit(solution)/shard_map/ppermute | solution.py:300
  60.9 21.3 %collective-permute-start.13 = (f32[1024,128]{1,0:T(8,128)S(1)}, f32[1024,128]{1,0:T(8,128)S(1)}, u32[]{:S(2)}, u32[]{:S(2)}) collective-permute-start(f32[1024,128]{1,0:T(8,128)S(1)} %get-tuple-element.33), channel_id=1, source_target_pairs={{0,4},{4,0},{8,12},{12,8},{16,20},{20,16},{24,28},{28,24},{1,5},{5... | collective-permute-start | bytes 1572872 | tf_op jit(solution)/shard_map/ppermute | solution.py:285
  71.0 23.1 %collective-permute-start.7 = (f32[1280,128]{1,0:T(8,128)S(1)}, f32[1280,128]{1,0:T(8,128)}, u32[]{:S(2)}, u32[]{:S(2)}) collective-permute-start(f32[1280,128]{1,0:T(8,128)S(1)} %add.99.refs_0_), channel_id=1, source_target_pairs={{1,2},{2,1},{5,6},{6,5},{9,10},{10,9},{13,14},{14,13},{17,18},{18,... | collective-permute-start | bytes 1966088 | tf_op jit(solution)/shard_map/ppermute | solution.py:299
  77.5 16.7 %collective-permute-start.8 = (f32[1280,128]{1,0:T(8,128)S(1)}, f32[1280,128]{1,0:T(8,128)}, u32[]{:S(2)}, u32[]{:S(2)}) collective-permute-start(f32[1280,128]{1,0:T(8,128)S(1)} %add.99.refs_0_), channel_id=1, source_target_pairs={{0,1},{1,0},{2,3},{3,2},{4,5},{5,4},{6,7},{7,6},{8,9},{9,8},{10,11... | collective-permute-start | bytes 1966088 | tf_op jit(solution)/shard_map/ppermute | solution.py:300
  82.3 11.9 %collective-permute-start.14 = (f32[1024,128]{1,0:T(8,128)S(1)}, f32[1024,128]{1,0:T(8,128)}, u32[]{:S(2)}, u32[]{:S(2)}) collective-permute-start(f32[1024,128]{1,0:T(8,128)S(1)} %add.100.refs_3_), channel_id=1, source_target_pairs={{1,2},{2,1},{5,6},{6,5},{9,10},{10,9},{13,14},{14,13},{17,18},{18,... | collective-permute-start | bytes 1572872 | tf_op jit(solution)/shard_map/ppermute | solution.py:299
  87.2 6.9 %collective-permute-start.15 = (f32[1024,128]{1,0:T(8,128)S(1)}, f32[1024,128]{1,0:T(8,128)}, u32[]{:S(2)}, u32[]{:S(2)}) collective-permute-start(f32[1024,128]{1,0:T(8,128)S(1)} %add.100.refs_3_), channel_id=1, source_target_pairs={{0,1},{1,0},{2,3},{3,2},{4,5},{5,4},{6,7},{7,6},{8,9},{9,8},{10,11... | collective-permute-start | bytes 1572872 | tf_op jit(solution)/shard_map/ppermute | solution.py:300
where the time goes:
time: 103 us; the launch traced here: 102 us
  waiting for transfers between devices  37.8 us (37%)
  starting transfers between devices  35.8 us (35%)
  Pallas kernels  22.7 us (22%)
  other arithmetic  3.81 us (4%)
  local copies, waits for them, and re-layouts  1.17 us (1%)
    ppermute x2, waiting for transfers between devices, line_of_four(): far = lax.ppermute(block, 'chaos', exchange_pairs(4, inner, 2))  20.1 us
    ppermute x3, starting transfers between devices, depth_pair(): other = lax.ppermute(values, 'space', second)  18.2 us
    ppermute x2, waiting for transfers between devices, chaos_sums(): got = lax.ppermute(other, 'chaos', across)  14.3 us
    pallas_call x4, Pallas kernels, sum_blocks(): pl.pallas_call(functools.partial(sum_kernel, n, coef_dev, entries, rows,...  11.2 us
    pallas_call x1, Pallas kernels, residual_and_correction(): pl.pallas_call(functools.partial(sweep_kernel, coef_dev, depth, layer_cou...  8.02 us
    ppermute x2, starting transfers between devices, line_of_four(): lax.ppermute(block, 'chaos', exchange_pairs(4, inner, 3, lambda o: o in m...  7.06 us
    ppermute x2, starting transfers between devices, line_of_four(): lax.ppermute(far, 'chaos', exchange_pairs(4, inner, 1, lambda o: o in mid...  4.46 us
    pallas_call x1, Pallas kernels, residual_and_correction(): pl.pallas_call(functools.partial(base_kernel, coef_dev, depth, n_space),...  3.54 us
  transfers between devices with their start and end apart: 16, of which 5 were waited for; matrix products, arithmetic and copies ran while one was open for 1% of the time, Pallas kernels for 14%

commit v1 on v0

--- a/solution.py
+++ b/solution.py
@@ -60,6 +60,63 @@
     )
 
 
+def pack_kernel(coef_dev, rows, slot_rows, inner, links, coeffs, bank, block, sems):
+    copies = [
+        pltpu.make_async_copy(
+            coeffs.at[c, pl.ds(0, rows)], block.at[pl.ds(c * rows, rows)], sems.at[c]
+        )
+        for c in range(coef_dev)
+    ]
+    copies.append(
+        pltpu.make_async_copy(
+            bank.at[0], block.at[pl.ds(coef_dev * rows, slot_rows)], sems.at[coef_dev]
+        )
+    )
+    for copy in copies:
+        copy.start()
+    entries, lanes = links.shape[0], block.shape[1]
+    listed = links[...].astype(jnp.float32)
+    s, p, k, level = (listed[:, i : i + 1] for i in range(4))
+    device = jnp.floor((p + 0.5) * (1.0 / coef_dev))
+    outer = jnp.floor((device + 0.5) * (1.0 / inner))
+    target = (p - device * coef_dev) * M + k
+    columns = (
+        jnp.where(level > 0.0, outer + 1.0, 0.0),
+        ((device - outer * inner) * coef_dev + s) * (coef_dev * M) + target,
+        jnp.sqrt(level),
+    )
+    place = lax.broadcasted_iota(jnp.int32, (entries, lanes), 0)
+    at = lax.broadcasted_iota(jnp.int32, (entries, lanes), 1)
+    table = [
+        jnp.sum(jnp.where(place == at, column, 0.0), axis=0, keepdims=True)
+        for column in columns
+    ]
+    table.append(jnp.zeros((TABLE_ROWS - len(columns), lanes), jnp.float32))
+    block[pl.ds(coef_dev * rows + slot_rows, TABLE_ROWS), :] = jnp.concatenate(table, axis=0)
+    for copy in copies:
+        copy.wait()
+
+
+def pack(coeffs, bank, links, rows, inner):
+    coef_dev, lanes = coeffs.shape[0], coeffs.shape[3]
+    whole_rows = coeffs.reshape(coef_dev, -1, lanes)
+    slot = bank.reshape(1, -1, lanes)
+    slot_rows = slot.shape[1]
+    anywhere = pl.BlockSpec(memory_space=pl.ANY)
+    return pl.pallas_call(
+        functools.partial(pack_kernel, coef_dev, rows, slot_rows, inner),
+        out_shape=jax.ShapeDtypeStruct(
+            (coef_dev * rows + slot_rows + TABLE_ROWS, lanes), jnp.float32
+        ),
+        in_specs=[VMEM, anywhere, anywhere],
+        out_specs=VMEM,
+        scratch_shapes=[pltpu.SemaphoreType.DMA((coef_dev + 1,))],
+        compiler_params=pltpu.CompilerParams(vmem_limit_bytes=4 << 20),
+        cost_estimate=cost(coef_dev, rows, lanes, 1),
+        name="pack",
+    )(links, whole_rows, slot)
+
+
 def sum_kernel(n_blocks, coef_dev, entries, rows, slot_rows, scan, more, *refs):
     refs = list(refs)
     where = refs.pop(0) if scan else None
@@ -70,13 +127,7 @@
     lists, weights, counts = [refs.pop(0) for _ in range(3)] if scan else given
     outs = (own, other)
     targets = coef_dev * M
-
-    def add(block, code, w, out):
-        row, target = lax.div(code, targets), lax.rem(code, targets)
-        at = pl.ds(pl.multiple_of(target * rows, rows), rows)
-        src = block[pl.ds(pl.multiple_of(row * rows, rows), rows), :]
-        out[at, :] = out[at, :] + w * src
-
+    spaced = entries + 1
     if scan:
         tables, sems = refs
         table_at = coef_dev * rows + slot_rows
@@ -89,32 +140,29 @@
     for out, start in zip(outs, so_far):
         out[...] = start[...] if more else jnp.zeros_like(out)
     if scan:
-        for copy in copies:
-            copy.wait()
-        names = [where[kind].astype(jnp.float32) for kind in range(2)]
+        name = where[0].astype(jnp.float32)
+        split = jnp.float32(coef_dev * targets)
+        first_is_own = where[1] == 0
     for i, b in enumerate(blocks):
         if scan:
+            copies[i].wait()
+            ends = [(2 * i + kind) * spaced for kind in range(2)]
+
+            def look(e, ends, i=i):
+                code, w = tables[i, 1, e], tables[i, 2, e]
+                mine = tables[i, 0, e] == name
+                low = code < split
+                is_own = low == first_is_own
+                short = jnp.where(low, code, code - split).astype(jnp.int32)
+                for end in ends:
+                    lists[end] = short
+                    weights[end] = w
+                hits = (mine & is_own, mine & jnp.logical_not(is_own))
+                return tuple(end + hit.astype(jnp.int32) for end, hit in zip(ends, hits))
+
+            ends = lax.fori_loop(0, entries, look, tuple(jnp.int32(e) for e in ends), unroll=8)
             for kind in range(2):
-                counts[2 * i + kind] = 0
-
-            def look(e, carry, b=b, i=i):
-                name = tables[i, 0, e]
-                for kind, out in enumerate(outs):
-
-                    @pl.when(name == names[kind])
-                    def _(kind=kind, out=out):
-                        slot = 2 * i + kind
-                        code = tables[i, 1, e].astype(jnp.int32)
-                        w = tables[i, 2, e]
-                        at = counts[slot]
-                        lists[slot * entries + at] = code
-                        weights[slot * entries + at] = w
-                        counts[slot] = at + 1
-                        add(b, code, w, out)
-
-                return carry
-
-            lax.fori_loop(0, entries, look, 0)
+                counts[2 * i + kind] = ends[kind]
             for k in range(M):
 
                 @pl.when(where[2 + k] == where[2 + M + i])
@@ -124,15 +172,17 @@
                     own[at, :] = own[at, :] + slot
                     other[at, :] = other[at, :] + slot
 
-        else:
-            for kind, out in enumerate(outs):
-                slot = 2 * i + kind
-
-                def listed(e, carry, b=b, out=out, slot=slot):
-                    add(b, lists[slot * entries + e], weights[slot * entries + e], out)
-                    return carry
-
-                lax.fori_loop(0, counts[slot], listed, 0)
+        for kind, out in enumerate(outs):
+
+            def listed(e, carry, b=b, out=out):
+                code, w = lists[e], weights[e]
+                row, target = lax.div(code, targets), lax.rem(code, targets)
+                at = pl.ds(pl.multiple_of(target * rows, rows), rows)
+                src = b[pl.ds(pl.multiple_of(row * rows, rows), rows), :]
+                out[at, :] = out[at, :] + w * src
+                return carry
+
+            lax.fori_loop((2 * i + kind) * spaced, counts[2 * i + kind], listed, 0)
 
 
 def sum_blocks(blocks, coef_dev, entries, rows, slot_rows, where, lists, so_far):
@@ -143,8 +193,8 @@
     out_shape, out_specs, scratch = [total, total], [VMEM, VMEM], []
     if scan:
         out_shape += [
-            jax.ShapeDtypeStruct((2 * n * entries,), jnp.int32),
-            jax.ShapeDtypeStruct((2 * n * entries,), jnp.float32),
+            jax.ShapeDtypeStruct((2 * n * (entries + 1),), jnp.int32),
+            jax.ShapeDtypeStruct((2 * n * (entries + 1),), jnp.float32),
             jax.ShapeDtypeStruct((2 * n,), jnp.int32),
         ]
         out_specs += [SMEM] * 3
@@ -192,11 +242,12 @@
     def sums(block, table, device):
         ids = table[:2, :entries].astype(jnp.int32)
         w = table[2, :entries]
-        source_row, target = ids[1] // targets, ids[1] % targets
+        device_inner, source_row = ids[1] // (targets * coef_dev), ids[1] // targets % coef_dev
+        target = ids[1] % targets
         picked = (source_row[:, None] == jnp.arange(coef_dev)[None, :]).astype(jnp.float32)
         found = []
         for who in wanted:
-            mine = jnp.where(ids[0] == who + 1, w, 0.0)
+            mine = jnp.where((ids[0] == who[0] + 1) & (device_inner == who[1]), w, 0.0)
             onehot = (jnp.arange(targets)[:, None] == target[None, :]).astype(jnp.float32)
             matrix = jnp.sum(
                 (onehot * mine[None, :])[:, :, None] * picked[None, :, :], axis=1
@@ -227,11 +278,10 @@
     outer, inner = grid_of(lax.axis_size("chaos"))
     me = lax.axis_index("chaos")
     my_outer, my_inner = me // inner, me % inner
-    neighbour = my_outer * inner + (inner - 1 - my_inner)
     found = []
     if outer == 4:
         where = jnp.stack(
-            [me + 1, neighbour + 1]
+            [my_outer + 1, my_inner]
             + [mode_owner[k] for k in range(M)]
             + [(my_outer ^ mask) * inner + my_inner for mask in (0, 1, 2, 3, 3)]
         ).astype(jnp.int32)
@@ -262,7 +312,7 @@
                         entries,
                         rows_of[j],
                         slot_rows if j == 0 else 0,
-                        (me, neighbour),
+                        ((my_outer, my_inner), (my_outer, inner - 1 - my_inner)),
                         mode_owner,
                     )(block, table, device)
                 )
@@ -468,25 +518,16 @@
     layer_counts = [per_chunk] * CHUNKS
     index = lax.axis_index("space").astype(jnp.int32).reshape(1)
 
-    s, p, k, level = (links[0, :, i] for i in range(4))
-    table = jnp.stack(
-        [
-            jnp.where(level > 0, p // coef_dev + 1, 0).astype(jnp.float32),
-            ((s * coef_dev + p % coef_dev) * M + k).astype(jnp.float32),
-            jnp.sqrt(level.astype(jnp.float32)),
-        ]
-    )
-    table = jnp.pad(table, ((0, TABLE_ROWS - 3), (0, ny - entries)))
-    chunks, start = [], 0
-    for j, layers in enumerate(layer_counts):
-        piece = coeffs[:, start : start + layers].reshape(-1, ny)
-        if j == 0:
-            piece = jnp.concatenate([piece, mode_bank[0].reshape(-1, ny), table], axis=0)
-        chunks.append(piece)
+    rows_of = [layers * nx for layers in layer_counts]
+    inner = grid_of(lax.axis_size("chaos"))[1]
+    chunks = [pack(coeffs, mode_bank, links[0], rows_of[0], inner)]
+    start = layer_counts[0]
+    for layers in layer_counts[1:]:
+        chunks.append(coeffs[:, start : start + layers].reshape(-1, ny))
         start += layers
 
     sums = chaos_sums(
-        chunks, coef_dev, entries, [layers * nx for layers in layer_counts], slot_rows, mode_owner
+        chunks, coef_dev, entries, rows_of, slot_rows, mode_owner
     )
 
     early = jnp.concatenate(

time: 103 us -> 101 us (0.981)
  other arithmetic: 3.81 us -> 1.31 us
  local copies, waits for them, and re-layouts: 1.17 us -> 2.75 us
    unnamed x8 -> x12, local copies, waits for them, and re-layouts: 0.02 us -> 1.89 us
    pallas_call x4, Pallas kernels: 11.2 us -> 9.69 us  [sum_blocks(): pl.pallas_call(functools.partial(sum_kernel, n, coef_dev, entries, rows,...]
    slice x1, local copies, waits for them, and re-layouts: 1.07 us -> 0.02 us  [residual_and_correction(): chunks.append(coeffs[:, start:start + layers].reshape(-1, ny))]
  transfers between devices with their start and end apart: 16 -> 16, of which waited for: 5 -> 5; matrix products, arithmetic and copies ran while one was open for 1% -> 1% of each run, Pallas kernels for 14% -> 13%
where the time goes in v1:
time: 101 us; the launch traced here: 100 us
  waiting for transfers between devices  37.8 us (37%)
  starting transfers between devices  35.8 us (35%)
  Pallas kernels  21.9 us (22%)
  local copies, waits for them, and re-layouts  2.75 us (3%)
  other arithmetic  1.31 us (1%)
    ppermute x2, waiting for transfers between devices, line_of_four(): far = lax.ppermute(block, 'chaos', exchange_pairs(4, inner, 2))  20.1 us
    ppermute x3, starting transfers between devices, depth_pair(): other = lax.ppermute(values, 'space', second)  18.2 us
    ppermute x2, waiting for transfers between devices, chaos_sums(): got = lax.ppermute(other, 'chaos', across)  14.4 us
    pallas_call x4, Pallas kernels, sum_blocks(): pl.pallas_call(functools.partial(sum_kernel, n, coef_dev, entries, rows,...  9.69 us
    pallas_call x1, Pallas kernels, residual_and_correction(): pl.pallas_call(functools.partial(sweep_kernel, coef_dev, depth, layer_cou...  8.02 us
    ppermute x2, starting transfers between devices, line_of_four(): lax.ppermute(block, 'chaos', exchange_pairs(4, inner, 3, lambda o: o in m...  7.06 us
    ppermute x2, starting transfers between devices, line_of_four(): lax.ppermute(far, 'chaos', exchange_pairs(4, inner, 1, lambda o: o in mid...  4.46 us
    pallas_call x1, Pallas kernels, residual_and_correction(): pl.pallas_call(functools.partial(base_kernel, coef_dev, depth, n_space),...  3.54 us
  transfers between devices with their start and end apart: 16, of which 5 were waited for; matrix products, arithmetic and copies ran while one was open for 1% of the time, Pallas kernels for 13%

profile of v1, /device:TPU:9, one launch (start us, length us, event | category | flops | bytes accessed | tf_op | source)
XLA Modules:
  0.0 100.4 jit_solution(12204602514596213149)
XLA Ops:
  1.4 1.0 %copy-done = f32[8,4,32,128]{3,2,1,0:T(8,128)S(1)} copy-done((f32[8,4,32,128]{3,2,1,0:T(8,128)S(1)}, f32[8,4,32,128]{3,2,1,0:T(8,128)}, u32[]{:S(2)}) %copy-start) | copy-done | bytes 524312
  2.4 0.8 copy-done.4
  4.0 2.4 %collective-permute-start.2 = (f32[648,128]{1,0:T(8,128)S(1)}, f32[648,128]{1,0:T(8,128)S(1)}, u32[]{:S(2)}, u32[]{:S(2)}) collective-permute-start(f32[648,128]{1,0:T(8,128)S(1)} %pack.1.refs_1_), channel_id=1, source_target_pairs={{0,16},{4,20},{8,24},{12,28},{16,0},{20,4},{24,8},{28,12},{1,17},{... | collective-permute-start | bytes 995336 | tf_op jit(solution)/shard_map/ppermute | solution.py:232
  6.5 2.1 %collective-permute-start.5 = (f32[648,128]{1,0:T(8,128)S(1)}, f32[648,128]{1,0:T(8,128)}, u32[]{:S(2)}, u32[]{:S(2)}) collective-permute-start(f32[648,128]{1,0:T(8,128)S(1)} %pack.1.refs_1_), channel_id=1, source_target_pairs={{8,16},{12,20},{16,8},{20,12},{9,17},{13,21},{17,9},{21,13},{10,18... | collective-permute-start | bytes 995336 | tf_op jit(solution)/shard_map/ppermute | solution.py:234
  8.7 12.6 %collective-permute-done.2.refs_3_ = f32[648,128]{1,0:T(8,128)S(1)} collective-permute-done((f32[648,128]{1,0:T(8,128)S(1)}, f32[648,128]{1,0:T(8,128)S(1)}, u32[]{:S(2)}, u32[]{:S(2)}) %collective-permute-start.2) | collective-permute-done | bytes 331808 | tf_op jit(solution)/shard_map/ppermute | solution.py:232
  21.3 2.4 %collective-permute-start.3 = (f32[648,128]{1,0:T(8,128)S(1)}, f32[648,128]{1,0:T(8,128)}, u32[]{:S(2)}, u32[]{:S(2)}) collective-permute-start(f32[648,128]{1,0:T(8,128)S(1)} %collective-permute-done.2.refs_3_), channel_id=1, source_target_pairs={{8,0},{12,4},{16,24},{20,28},{9,1},{13,5},{17,25},{21,29},{10,2},{... | collective-permute-start | bytes 995336 | tf_op jit(solution)/shard_map/ppermute | solution.py:235
  23.8 1.1 %pad_maximum_fusion = f32[68,32,128]{2,1,0:T(8,128)} fusion(f32[4,32,128]{2,1,0:T(8,128)S(1)} %copy-done.3, f32[32,32,128]{2,1,0:T(8,128)S(1)} %bitcast.15, f32[32,32,128]{2,1,0:T(8,128)S(1)} %bitcast.14), kind=kLoop, calls=%fused_computation | loop fusion | flops 557056 | bytes 2228224 | tf_op jit(solution)/shard_map/concatenate | solution.py:533
  24.9 6.8 %collective-permute-start = (f32[68,32,128]{2,1,0:T(8,128)}, f32[68,32,128]{2,1,0:T(8,128)S(1)}, u32[]{:S(2)}, u32[]{:S(2)}) collective-permute-start(f32[68,32,128]{2,1,0:T(8,128)} %pad_maximum_fusion), channel_id=1, source_target_pairs={{1,2},{2,1},{5,6},{6,5},{9,10},{10,9},{13,14},{14,13},{17,18},{18,... | collective-permute-start | bytes 3342344 | tf_op jit(solution)/shard_map/ppermute | solution.py:349
  31.7 7.5 %collective-permute-done.9.refs_5_ = f32[512,128]{1,0:T(8,128)} collective-permute-done((f32[512,128]{1,0:T(8,128)S(1)}, f32[512,128]{1,0:T(8,128)}, u32[]{:S(2)}, u32[]{:S(2)}) %collective-permute-start.9) | collective-permute-done | bytes 262176 | tf_op jit(solution)/shard_map/ppermute | solution.py:232
  39.7 5.0 %collective-permute-start.12 = (f32[512,128]{1,0:T(8,128)S(1)}, f32[512,128]{1,0:T(8,128)}, u32[]{:S(2)}, u32[]{:S(2)}) collective-permute-start(f32[512,128]{1,0:T(8,128)S(1)} %bitcast.18), channel_id=1, source_target_pairs={{8,16},{12,20},{16,8},{20,12},{9,17},{13,21},{17,9},{21,13},{10,18... | collective-permute-start | bytes 786440 | tf_op jit(solution)/shard_map/ppermute | solution.py:234
  44.7 2.0 %collective-permute-start.10 = (f32[512,128]{1,0:T(8,128)}, f32[512,128]{1,0:T(8,128)}, u32[]{:S(2)}, u32[]{:S(2)}) collective-permute-start(f32[512,128]{1,0:T(8,128)} %collective-permute-done.9.refs_5_), channel_id=1, source_target_pairs={{8,0},{12,4},{16,24},{20,28},{9,1},{13,5},{17,25},{21,29},{10,2},{... | collective-permute-start | bytes 786440 | tf_op jit(solution)/shard_map/ppermute | solution.py:235
  46.8 4.4 %shard_map.77 = (f32[1280,128]{1,0:T(8,128)S(1)}, f32[1280,128]{1,0:T(8,128)S(1)}, s32[264]{0:T(512)S(1)}, f32[264]{0:T(512)S(1)}, s32[8]{0:T(128)S(1)}) custom-call(s32[9]{0:T(128)S(1)} %stack.28.refs_0_, f32[648,128]{1,0:T(8,128)S(1)} %pack.1.refs_1_, f32[648,128]{1,0:T(8,128)} %collective-permute-done.4.refs_2_, ...), custom_call_target="tpu_custom_call" | custom-call | flops 524288 | bytes 1048576 | tf_op jit(solution)/shard_map/pallas_call | solution.py:207
  51.3 2.6 %shard_map.78 = (f32[1280,128]{1,0:T(8,128)S(1)}, f32[1280,128]{1,0:T(8,128)S(1)}, s32[66]{0:T(128)S(1)}, f32[66]{0:T(128)S(1)}, s32[2]{0:T(128)S(1)}) custom-call(s32[5]{0:T(128)S(1)} %pad_add_fusion.refs_0_, f32[648,128]{1,0:T(8,128)} %collective-permute-done.3.refs_1_, f32[1280,128]{1,0:T(8,128)S(1)} %get-tuple-element.20.refs_2_, ...), custom_call_target="tpu_custom_call" | custom-call | flops 524288 | bytes 1048576 | tf_op jit(solution)/shard_map/pallas_call | solution.py:207
  53.9 1.3 %collective-permute-start.6 = (f32[1280,128]{1,0:T(8,128)S(1)}, f32[1280,128]{1,0:T(8,128)S(1)}, u32[]{:S(2)}, u32[]{:S(2)}) collective-permute-start(f32[1280,128]{1,0:T(8,128)S(1)} %get-tuple-element.23), channel_id=1, source_target_pairs={{0,4},{4,0},{8,12},{12,8},{16,20},{20,16},{24,28},{28,24},{1,5},{5... | collective-permute-start | bytes 1966088 | tf_op jit(solution)/shard_map/ppermute | solution.py:335
  55.2 1.3 %collective-permute-start.1 = (f32[68,32,128]{2,1,0:T(8,128)}, f32[68,32,128]{2,1,0:T(8,128)}, u32[]{:S(2)}, u32[]{:S(2)}) collective-permute-start(f32[68,32,128]{2,1,0:T(8,128)} %pad_maximum_fusion), channel_id=1, source_target_pairs={{0,1},{1,0},{2,3},{3,2},{4,5},{5,4},{6,7},{7,6},{8,9},{9,8},{10,11... | collective-permute-start | bytes 3342344 | tf_op jit(solution)/shard_map/ppermute | solution.py:350
  56.5 1.6 %shard_map.79 = (f32[1024,128]{1,0:T(8,128)S(1)}, f32[1024,128]{1,0:T(8,128)S(1)}) custom-call(s32[264]{0:T(512)S(1)} %get-tuple-element.27.refs_0_, f32[264]{0:T(512)S(1)} %get-tuple-element.28.refs_1_, s32[8]{0:T(128)S(1)} %get-tuple-element.29.refs_2_, f32[512,128]{1,0:T(8,128)S(1)} %bitcast.19, f32[512,128]{1,0:T(8,128)} %collective-permute-done.11.refs_4_, ...), custom_call_target="tpu_custom_call" | custom-call | flops 524288 | bytes 1048576 | tf_op jit(solution)/shard_map/pallas_call | solution.py:207
  58.1 1.0 %shard_map.80 = (f32[1024,128]{1,0:T(8,128)S(1)}, f32[1024,128]{1,0:T(8,128)S(1)}) custom-call(s32[66]{0:T(128)S(1)} %get-tuple-element.24.refs_0_, f32[66]{0:T(128)S(1)} %get-tuple-element.25.refs_1_, s32[2]{0:T(128)S(1)} %get-tuple-element.26.refs_2_, f32[512,128]{1,0:T(8,128)} %collective-permute-done.10.refs_3_, ...), custom_call_target="tpu_custom_call" | custom-call | flops 524288 | bytes 1048576 | tf_op jit(solution)/shard_map/pallas_call | solution.py:207
  59.5 9.7 %collective-permute-done.6 = f32[1280,128]{1,0:T(8,128)S(1)} collective-permute-done((f32[1280,128]{1,0:T(8,128)S(1)}, f32[1280,128]{1,0:T(8,128)S(1)}, u32[]{:S(2)}, u32[]{:S(2)}) %collective-permute-start.6) | collective-permute-done | bytes 655392 | tf_op jit(solution)/shard_map/ppermute | solution.py:335
  69.3 6.5 %collective-permute-start.7 = (f32[1280,128]{1,0:T(8,128)S(1)}, f32[1280,128]{1,0:T(8,128)}, u32[]{:S(2)}, u32[]{:S(2)}) collective-permute-start(f32[1280,128]{1,0:T(8,128)S(1)} %add.33.refs_0_), channel_id=1, source_target_pairs={{1,2},{2,1},{5,6},{6,5},{9,10},{10,9},{13,14},{14,13},{17,18},{18,... | collective-permute-start | bytes 1966088 | tf_op jit(solution)/shard_map/ppermute | solution.py:349
  75.8 4.6 %collective-permute-done.13 = f32[1024,128]{1,0:T(8,128)S(1)} collective-permute-done((f32[1024,128]{1,0:T(8,128)S(1)}, f32[1024,128]{1,0:T(8,128)S(1)}, u32[]{:S(2)}, u32[]{:S(2)}) %collective-permute-start.13) | collective-permute-done | bytes 524320 | tf_op jit(solution)/shard_map/ppermute | solution.py:335
  80.5 4.9 %collective-permute-start.14 = (f32[1024,128]{1,0:T(8,128)S(1)}, f32[1024,128]{1,0:T(8,128)}, u32[]{:S(2)}, u32[]{:S(2)}) collective-permute-start(f32[1024,128]{1,0:T(8,128)S(1)} %add.34.refs_3_), channel_id=1, source_target_pairs={{1,2},{2,1},{5,6},{6,5},{9,10},{10,9},{13,14},{14,13},{17,18},{18,... | collective-permute-start | bytes 1572872 | tf_op jit(solution)/shard_map/ppermute | solution.py:349
  85.6 3.5 %base.1 = (f32[8,12,32,128]{3,2,1,0:T(8,128)S(1)}, f32[7,12,32,128]{3,2,1,0:T(8,128)S(1)}) custom-call(s32[1]{0:T(128)} %bitcast.space_ref, f32[8,4,32,128]{3,2,1,0:T(8,128)S(1)} %copy-done.1, f32[8,4,32,128]{3,2,1,0:T(8,128)S(1)} %copy-done.2, f32[4,32,128]{2,1,0:T(8,128)S(1)} %copy-done.3, f32[68,32,128]{2,1,0:T(8,128)S(1)} %collective-permute-done.refs_0_, ...), custom_call_target="tpu_custom_call" | custom-call | flops 7864320 | bytes 3145728 | tf_op jit(solution)/shard_map/base/pallas_call | solution.py:538
  89.1 3.3 %collective-permute-done.14.refs_4_ = f32[1024,128]{1,0:T(8,128)} collective-permute-done((f32[1024,128]{1,0:T(8,128)S(1)}, f32[1024,128]{1,0:T(8,128)}, u32[]{:S(2)}, u32[]{:S(2)}) %collective-permute-start.14) | collective-permute-done | bytes 524320 | tf_op jit(solution)/shard_map/ppermute | solution.py:349
  92.4 8.0 %sweeps.1 = (f32[8,4,32,128]{3,2,1,0:T(8,128)}, f32[8,4,32,128]{3,2,1,0:T(8,128)}) custom-call(s32[1]{0:T(128)} %bitcast.space_ref, f32[8,12,32,128]{3,2,1,0:T(8,128)S(1)} %get-tuple-element.18.known, f32[7,12,32,128]{3,2,1,0:T(8,128)S(1)} %get-tuple-element.19.face, f32[1280,128]{1,0:T(8,128)S(1)} %add.33.refs_0_, ...), custom_call_target="tpu_custom_call" | custom-call | flops 31457280 | bytes 6291456 | tf_op jit(solution)/shard_map/sweeps/pallas_call | solution.py:559
  (34 shorter events, 2.9 us)
Async XLA Ops:
  1.4 1.0 %copy-start = (f32[8,4,32,128]{3,2,1,0:T(8,128)S(1)}, f32[8,4,32,128]{3,2,1,0:T(8,128)}, u32[]{:S(2)}) copy-start(f32[8,4,32,128]{3,2,1,0:T(8,128)} %coeffs.1) | copy-start | bytes 1572868
  2.4 0.8 copy-start.4
  3.3 5.3 %copy-start.1 = (f32[8,4,32,128]{3,2,1,0:T(8,128)S(1)}, f32[8,4,32,128]{3,2,1,0:T(8,128)}, u32[]{:S(2)}) copy-start(f32[8,4,32,128]{3,2,1,0:T(8,128)} %coeffs.1) | copy-start | bytes 1572868
  3.3 20.5 %copy-start.2 = (f32[8,4,32,128]{3,2,1,0:T(8,128)S(1)}, f32[8,4,32,128]{3,2,1,0:T(8,128)}, u32[]{:S(2)}) copy-start(f32[8,4,32,128]{3,2,1,0:T(8,128)} %source.1) | copy-start | bytes 1572868
  3.3 20.5 %copy-start.3 = (f32[4,32,128]{2,1,0:T(8,128)S(1)}, f32[4,32,128]{2,1,0:T(8,128)}, u32[]{:S(2)}) copy-start(f32[4,32,128]{2,1,0:T(8,128)} %mean.1) | copy-start | bytes 196612
  4.0 17.4 %collective-permute-start.2 = (f32[648,128]{1,0:T(8,128)S(1)}, f32[648,128]{1,0:T(8,128)S(1)}, u32[]{:S(2)}, u32[]{:S(2)}) collective-permute-start(f32[648,128]{1,0:T(8,128)S(1)} %pack.1.refs_1_), channel_id=1, source_target_pairs={{0,16},{4,20},{8,24},{12,28},{16,0},{20,4},{24,8},{28,12},{1,17},{... | collective-permute-start | bytes 995336 | tf_op jit(solution)/shard_map/ppermute | solution.py:232
  6.3 33.4 %collective-permute-start.4 = (f32[648,128]{1,0:T(8,128)S(1)}, f32[648,128]{1,0:T(8,128)}, u32[]{:S(2)}, u32[]{:S(2)}) collective-permute-start(f32[648,128]{1,0:T(8,128)S(1)} %pack.1.refs_1_), channel_id=1, source_target_pairs={{0,8},{4,12},{8,0},{12,4},{16,24},{20,28},{24,16},{28,20},{1,9},{5... | collective-permute-start | bytes 995336 | tf_op jit(solution)/shard_map/ppermute | solution.py:233
  6.5 38.2 %collective-permute-start.5 = (f32[648,128]{1,0:T(8,128)S(1)}, f32[648,128]{1,0:T(8,128)}, u32[]{:S(2)}, u32[]{:S(2)}) collective-permute-start(f32[648,128]{1,0:T(8,128)S(1)} %pack.1.refs_1_), channel_id=1, source_target_pairs={{8,16},{12,20},{16,8},{20,12},{9,17},{13,21},{17,9},{21,13},{10,18... | collective-permute-start | bytes 995336 | tf_op jit(solution)/shard_map/ppermute | solution.py:234
  8.6 30.6 %collective-permute-start.9 = (f32[512,128]{1,0:T(8,128)S(1)}, f32[512,128]{1,0:T(8,128)}, u32[]{:S(2)}, u32[]{:S(2)}) collective-permute-start(f32[512,128]{1,0:T(8,128)S(1)} %bitcast.16), channel_id=1, source_target_pairs={{0,16},{4,20},{8,24},{12,28},{16,0},{20,4},{24,8},{28,12},{1,17},{... | collective-permute-start | bytes 786440 | tf_op jit(solution)/shard_map/ppermute | solution.py:232
  21.3 29.9 %collective-permute-start.3 = (f32[648,128]{1,0:T(8,128)S(1)}, f32[648,128]{1,0:T(8,128)}, u32[]{:S(2)}, u32[]{:S(2)}) collective-permute-start(f32[648,128]{1,0:T(8,128)S(1)} %collective-permute-done.2.refs_3_), channel_id=1, source_target_pairs={{8,0},{12,4},{16,24},{20,28},{9,1},{13,5},{17,25},{21,29},{10,2},{... | collective-permute-start | bytes 995336 | tf_op jit(solution)/shard_map/ppermute | solution.py:235
  23.8 15.8 %copy-start.5 = (s32[2]{0:T(128)S(1)}, s32[2]{0:T(128)}, u32[]{:S(2)}) copy-start(s32[2]{0:T(128)} %param.10) | copy-start | bytes 28
  24.9 60.6 %collective-permute-start = (f32[68,32,128]{2,1,0:T(8,128)}, f32[68,32,128]{2,1,0:T(8,128)S(1)}, u32[]{:S(2)}, u32[]{:S(2)}) collective-permute-start(f32[68,32,128]{2,1,0:T(8,128)} %pad_maximum_fusion), channel_id=1, source_target_pairs={{1,2},{2,1},{5,6},{6,5},{9,10},{10,9},{13,14},{14,13},{17,18},{18,... | collective-permute-start | bytes 3342344 | tf_op jit(solution)/shard_map/ppermute | solution.py:349
  39.2 16.0 %collective-permute-start.11 = (f32[512,128]{1,0:T(8,128)S(1)}, f32[512,128]{1,0:T(8,128)}, u32[]{:S(2)}, u32[]{:S(2)}) collective-permute-start(f32[512,128]{1,0:T(8,128)S(1)} %bitcast.17), channel_id=1, source_target_pairs={{0,8},{4,12},{8,0},{12,4},{16,24},{20,28},{24,16},{28,20},{1,9},{5... | collective-permute-start | bytes 786440 | tf_op jit(solution)/shard_map/ppermute | solution.py:233
  39.7 16.8 %collective-permute-start.12 = (f32[512,128]{1,0:T(8,128)S(1)}, f32[512,128]{1,0:T(8,128)}, u32[]{:S(2)}, u32[]{:S(2)}) collective-permute-start(f32[512,128]{1,0:T(8,128)S(1)} %bitcast.18), channel_id=1, source_target_pairs={{8,16},{12,20},{16,8},{20,12},{9,17},{13,21},{17,9},{21,13},{10,18... | collective-permute-start | bytes 786440 | tf_op jit(solution)/shard_map/ppermute | solution.py:234
  44.7 13.4 %collective-permute-start.10 = (f32[512,128]{1,0:T(8,128)}, f32[512,128]{1,0:T(8,128)}, u32[]{:S(2)}, u32[]{:S(2)}) collective-permute-start(f32[512,128]{1,0:T(8,128)} %collective-permute-done.9.refs_5_), channel_id=1, source_target_pairs={{8,0},{12,4},{16,24},{20,28},{9,1},{13,5},{17,25},{21,29},{10,2},{... | collective-permute-start | bytes 786440 | tf_op jit(solution)/shard_map/ppermute | solution.py:235
  53.9 15.3 %collective-permute-start.6 = (f32[1280,128]{1,0:T(8,128)S(1)}, f32[1280,128]{1,0:T(8,128)S(1)}, u32[]{:S(2)}, u32[]{:S(2)}) collective-permute-start(f32[1280,128]{1,0:T(8,128)S(1)} %get-tuple-element.23), channel_id=1, source_target_pairs={{0,4},{4,0},{8,12},{12,8},{16,20},{20,16},{24,28},{28,24},{1,5},{5... | collective-permute-start | bytes 1966088 | tf_op jit(solution)/shard_map/ppermute | solution.py:335
  55.2 30.4 %collective-permute-start.1 = (f32[68,32,128]{2,1,0:T(8,128)}, f32[68,32,128]{2,1,0:T(8,128)}, u32[]{:S(2)}, u32[]{:S(2)}) collective-permute-start(f32[68,32,128]{2,1,0:T(8,128)} %pad_maximum_fusion), channel_id=1, source_target_pairs={{0,1},{1,0},{2,3},{3,2},{4,5},{5,4},{6,7},{7,6},{8,9},{9,8},{10,11... | collective-permute-start | bytes 3342344 | tf_op jit(solution)/shard_map/ppermute | solution.py:350
  59.1 21.3 %collective-permute-start.13 = (f32[1024,128]{1,0:T(8,128)S(1)}, f32[1024,128]{1,0:T(8,128)S(1)}, u32[]{:S(2)}, u32[]{:S(2)}) collective-permute-start(f32[1024,128]{1,0:T(8,128)S(1)} %get-tuple-element.33), channel_id=1, source_target_pairs={{0,4},{4,0},{8,12},{12,8},{16,20},{20,16},{24,28},{28,24},{1,5},{5... | collective-permute-start | bytes 1572872 | tf_op jit(solution)/shard_map/ppermute | solution.py:335
  69.3 23.1 %collective-permute-start.7 = (f32[1280,128]{1,0:T(8,128)S(1)}, f32[1280,128]{1,0:T(8,128)}, u32[]{:S(2)}, u32[]{:S(2)}) collective-permute-start(f32[1280,128]{1,0:T(8,128)S(1)} %add.33.refs_0_), channel_id=1, source_target_pairs={{1,2},{2,1},{5,6},{6,5},{9,10},{10,9},{13,14},{14,13},{17,18},{18,... | collective-permute-start | bytes 1966088 | tf_op jit(solution)/shard_map/ppermute | solution.py:349
  75.7 16.7 %collective-permute-start.8 = (f32[1280,128]{1,0:T(8,128)S(1)}, f32[1280,128]{1,0:T(8,128)}, u32[]{:S(2)}, u32[]{:S(2)}) collective-permute-start(f32[1280,128]{1,0:T(8,128)S(1)} %add.33.refs_0_), channel_id=1, source_target_pairs={{0,1},{1,0},{2,3},{3,2},{4,5},{5,4},{6,7},{7,6},{8,9},{9,8},{10,11... | collective-permute-start | bytes 1966088 | tf_op jit(solution)/shard_map/ppermute | solution.py:350
  80.5 11.9 %collective-permute-start.14 = (f32[1024,128]{1,0:T(8,128)S(1)}, f32[1024,128]{1,0:T(8,128)}, u32[]{:S(2)}, u32[]{:S(2)}) collective-permute-start(f32[1024,128]{1,0:T(8,128)S(1)} %add.34.refs_3_), channel_id=1, source_target_pairs={{1,2},{2,1},{5,6},{6,5},{9,10},{10,9},{13,14},{14,13},{17,18},{18,... | collective-permute-start | bytes 1572872 | tf_op jit(solution)/shard_map/ppermute | solution.py:349
  85.5 6.9 %collective-permute-start.15 = (f32[1024,128]{1,0:T(8,128)S(1)}, f32[1024,128]{1,0:T(8,128)}, u32[]{:S(2)}, u32[]{:S(2)}) collective-permute-start(f32[1024,128]{1,0:T(8,128)S(1)} %add.34.refs_3_), channel_id=1, source_target_pairs={{0,1},{1,0},{2,3},{3,2},{4,5},{5,4},{6,7},{7,6},{8,9},{9,8},{10,11... | collective-permute-start | bytes 1572872 | tf_op jit(solution)/shard_map/ppermute | solution.py:350

commit v2 on v0

v2 whole, which is shorter than its diff:
```python
import functools

import jax
import jax.numpy as jnp
from jax import lax
from jax.experimental import pallas as pl
from jax.experimental.pallas import tpu as pltpu
from jax.sharding import PartitionSpec as P


M = 2
ITERS = 4

REACTION = 0.5
BOUND_LOW = 0.04
BOUND_HIGH = 2.0

CHUNKS = 2
TABLE_ROWS = 8


VMEM = pl.BlockSpec(memory_space=pltpu.VMEM)
SMEM = pl.BlockSpec(memory_space=pltpu.SMEM)


def cost(planes, nx, ny, flops):
    return pl.CostEstimate(
        flops=flops * planes * nx * ny, bytes_accessed=8 * planes * nx * ny, transcendentals=0
    )


def shifted(values, axis, step):
    return pltpu.roll(values, step % values.shape[axis], axis)


def faces(below, own, above):
    nx, ny = own.shape
    ix = lax.broadcasted_iota(jnp.int32, (nx, ny), 0)
    iy = lax.broadcasted_iota(jnp.int32, (nx, ny), 1)
    half = 0.5 * own
    zero = jnp.zeros_like(own)
    xm = jnp.where(ix == 0, zero, half + shifted(half, 0, 1))
    xp = jnp.where(ix == nx - 1, zero, half + shifted(half, 0, -1))
    ym = jnp.where(iy == 0, zero, half + shifted(half, 1, 1))
    yp = jnp.where(iy == ny - 1, zero, half + shifted(half, 1, -1))
    up = half + 0.5 * above
    down = half + 0.5 * below
    total = up + down
    total = total + jnp.where(ix == 0, half, xm) + jnp.where(ix == nx - 1, half, xp)
    total = total + jnp.where(iy == 0, half, ym) + jnp.where(iy == ny - 1, half, yp)
    return xm, xp, ym, yp, down, up, total


def lateral(to_xm, to_xp, to_ym, to_yp):
    return (
        shifted(to_xm, 0, -1)
        + shifted(to_xp, 0, 1)
        + shifted(to_ym, 1, -1)
        + shifted(to_yp, 1, 1)
    )


def pack_kernel(coef_dev, capacity, rows_of, slot_rows, links, coeffs, bank, *refs):
    blocks, (sems,) = refs[: len(rows_of)], refs[len(rows_of) :]
    slot = blocks[0].at[pl.ds(coef_dev * rows_of[0], slot_rows)]
    copies = [pltpu.make_async_copy(bank.at[0], slot, sems.at[len(rows_of) * coef_dev])]
    start = 0
    for j, (block, rows) in enumerate(zip(blocks, rows_of)):
        for c in range(coef_dev):
            copies.append(
                pltpu.make_async_copy(
                    coeffs.at[c, pl.ds(start, rows)],
                    block.at[pl.ds(c * rows, rows)],
                    sems.at[j * coef_dev + c],
                )
            )
        start += rows
    for copy in copies:
        copy.start()
    entries, lanes = links.shape[1], blocks[0].shape[1]
    listed = links[...].astype(jnp.float32)
    s, p, k, level = (listed[i : i + 1] for i in range(4))
    device = jnp.floor((p + 0.5) * (1.0 / coef_dev))
    code = (s * coef_dev + p - device * coef_dev) * M + k
    square = (entries, entries)
    row = lax.broadcasted_iota(jnp.int32, square, 0)
    column = lax.broadcasted_iota(jnp.int32, square, 1)

    def upright(values):
        return jnp.sum(jnp.where(row == column, values, 0.0), axis=1, keepdims=True)

    device_up, level_up = upright(device), upright(level)
    earlier = (device == device_up) & (level > 0.0) & (column < row)
    rank = jnp.sum(jnp.where(earlier, 1.0, 0.0), axis=1, keepdims=True)
    place = jnp.where(level_up > 0.0, device_up * capacity + rank, -1.0)
    lane = lax.broadcasted_iota(jnp.int32, (entries, lanes), 1).astype(jnp.float32)
    table = [
        jnp.sum(jnp.where(place == lane, values, 0.0), axis=0, keepdims=True)
        for values in (upright(code), jnp.sqrt(level_up))
    ]
    table.append(jnp.zeros((TABLE_ROWS - len(table), lanes), jnp.float32))
    table = jnp.concatenate(table, axis=0)
    for block in blocks:
        block[pl.ds(block.shape[0] - TABLE_ROWS, TABLE_ROWS), :] = table
    for copy in copies:
        copy.wait()


def pack(coeffs, bank, links, capacity, rows_of):
    coef_dev, lanes = coeffs.shape[0], coeffs.shape[3]
    whole_rows = coeffs.reshape(coef_dev, -1, lanes)
    slot = bank.reshape(1, -1, lanes)
    slot_rows = slot.shape[1]
    hbm = pl.BlockSpec(memory_space=pltpu.HBM)
    sizes = [
        coef_dev * rows + (slot_rows if j == 0 else 0) + TABLE_ROWS
        for j, rows in enumerate(rows_of)
    ]
    return pl.pallas_call(
        functools.partial(pack_kernel, coef_dev, capacity, rows_of, slot_rows),
        out_shape=[jax.ShapeDtypeStruct((size, lanes), jnp.float32) for size in sizes],
        in_specs=[VMEM, hbm, hbm],
        out_specs=[VMEM] * len(sizes),
        scratch_shapes=[pltpu.SemaphoreType.DMA((len(sizes) * coef_dev + 1,))],
        cost_estimate=cost(coef_dev, sum(rows_of), lanes, 1),
        name="pack",
    )(links.T, whole_rows, slot)


def sum_kernel(n, coef_dev, capacity, rows, slot_rows, more, where, *refs):
    refs = list(refs)
    blocks = [refs.pop(0) for _ in range(n)]
    so_far = refs.pop(0) if more else None
    out, tables, sems = refs
    targets = coef_dev * M
    copies = [
        pltpu.make_async_copy(
            block.at[pl.ds(block.shape[0] - TABLE_ROWS, TABLE_ROWS)], tables.at[i], sems.at[i]
        )
        for i, block in enumerate(blocks)
    ]
    for copy in copies:
        copy.start()
    out[...] = so_far[...] if more else jnp.zeros_like(out)
    if slot_rows:
        for i, block in enumerate(blocks):
            for k in range(M):

                @pl.when(where[1 + k] == where[1 + M + i])
                def _(block=block, k=k):
                    at = pl.ds(targets * rows + k * slot_rows, slot_rows)
                    out[at, :] = block[pl.ds(coef_dev * rows, slot_rows), :]

    begin = where[0] * capacity
    for i, block in enumerate(blocks):
        copies[i].wait()

        def listed(e, carry, i=i, block=block):
            code, w = tables[i, 0, e].astype(jnp.int32), tables[i, 1, e]
            row, target = lax.div(code, targets), lax.rem(code, targets)
            at = pl.ds(pl.multiple_of(target * rows, rows), rows)
            src = block[pl.ds(pl.multiple_of(row * rows, rows), rows), :]
            out[at, :] = out[at, :] + w * src
            return carry

        lax.fori_loop(begin, begin + capacity, listed, 0)


def sum_blocks(blocks, devices, me, mode_owner, coef_dev, capacity, rows, slot_rows, so_far):
    n, lanes = len(blocks), blocks[0].shape[1]
    size = coef_dev * M * rows + M * slot_rows
    where = jnp.stack([me] + [mode_owner[k] for k in range(M)] + devices).astype(jnp.int32)
    more = so_far is not None
    return pl.pallas_call(
        functools.partial(
            sum_kernel, n, coef_dev, capacity, rows, slot_rows, more
        ),
        out_shape=jax.ShapeDtypeStruct((size, lanes), jnp.float32),
        in_specs=[SMEM] + [VMEM] * (n + more),
        out_specs=VMEM,
        scratch_shapes=[
            pltpu.SMEM((n, TABLE_ROWS, lanes), jnp.float32),
            pltpu.SemaphoreType.DMA((n,)),
        ],
        compiler_params=pltpu.CompilerParams(vmem_limit_bytes=12 << 20),
        cost_estimate=cost(coef_dev * M, rows, lanes, 4),
    )(where, *blocks, *([so_far] if more else []))


def plain_sums(block, table, mode_slot, device, me, mode_owner, coef_dev, capacity, rows):
    targets = coef_dev * M
    code = lax.dynamic_slice(table[0], (me * capacity,), (capacity,)).astype(jnp.int32)
    w = lax.dynamic_slice(table[1], (me * capacity,), (capacity,))
    row = (code[:, None] // targets == jnp.arange(coef_dev)[None, :]).astype(jnp.float32)
    target = (code[:, None] % targets == jnp.arange(targets)[None, :]).astype(jnp.float32)
    matrix = jnp.sum((target * w[:, None])[:, :, None] * row[:, None, :], axis=0)
    data = block[: coef_dev * rows].reshape(coef_dev, -1)
    found = jnp.dot(matrix, data, precision=lax.Precision.HIGHEST)
    found = found.reshape(targets * rows, -1)
    if mode_slot is None:
        return found
    modes = [jnp.where(mode_owner[k] == device, mode_slot, 0.0) for k in range(M)]
    return jnp.concatenate([found, *modes], axis=0)


def unrolled(count):
    return count % 2 == 0 and count <= 16


def ring_order(count):
    return list(range(0, count, 2)) + list(range(count - 1, 0, -2))


def ring_steps(count):
    half = count // 2
    return [
        (half, half - 1) if j == 0 else (half - 1, half) for j in range(CHUNKS)
    ]


def chaos_sums(chunks, coef_dev, capacity, rows_of, slot_rows, mode_owner):
    count = lax.axis_size("chaos")
    me = lax.axis_index("chaos")
    fixed = (me, mode_owner, coef_dev, capacity)
    if not unrolled(count):
        ring = [(i, (i + 1) % count) for i in range(count)]

        def at_step(step, blocks):
            device = (me - step) % count
            slot_at = coef_dev * rows_of[0]
            table, slot = blocks[0][-TABLE_ROWS:], blocks[0][slot_at : slot_at + slot_rows]
            return [
                plain_sums(b, table, slot if j == 0 else None, device, *fixed, rows_of[j])
                for j, b in enumerate(blocks)
            ]

        def body(step, carry):
            blocks, sums = carry
            blocks = [lax.ppermute(b, "chaos", ring) for b in blocks]
            return blocks, jax.tree.map(jnp.add, sums, at_step(step, blocks))

        return lax.fori_loop(1, count, body, (list(chunks), at_step(0, chunks)))[1]

    order = ring_order(count)
    there = [(order[i], order[(i + 1) % count]) for i in range(count)]
    back = [(b, a) for a, b in there]
    half = count // 2
    place = jnp.where(me % 2 == 0, me // 2, count - 1 - me // 2)

    def device_at(shift):
        q = (place + shift) % count
        return jnp.where(q < half, 2 * q, 2 * (count - 1 - q) + 1)

    gathered = []
    for chunk, steps in zip(chunks, ring_steps(count)):
        blocks = {0: chunk}
        for pairs, sign, n_steps in ((there, -1, steps[0]), (back, 1, steps[1])):
            block = chunk
            for step in range(1, n_steps + 1):
                block = lax.ppermute(block, "chaos", pairs)
                blocks[sign * step] = block
        gathered.append({shift % count: block for shift, block in blocks.items()})
    early = [0] + [s for step in range(1, half - 1) for s in (step, count - step)]
    late = [s for s in range(count) if s not in early]
    found = []
    for j, blocks in enumerate(gathered):
        sums = None
        for shifts in (early, late):
            sums = sum_blocks(
                [blocks[s] for s in shifts],
                [device_at(s) for s in shifts],
                *fixed,
                rows_of[j],
                slot_rows if j == 0 else 0,
                sums,
            )
        found.append(sums)
    return found


def depth_pair(values):
    count = lax.axis_size("space")
    first = [(i, i ^ 1) for i in range(count) if i ^ 1 < count]
    second = [
        (i, j)
        for i in range(count)
        for j in [i - 1 if i % 2 == 0 else i + 1]
        if 0 <= j < count
    ]
    other = lax.ppermute(values, "space", second)
    pair = lax.ppermute(values, "space", first)
    return other, pair


def base_kernel(coef_dev, depth, n_space, space_ref, coeffs, source, mean, *refs):
    other, pair, known, face, coef_ext, mean_ext = refs
    index = space_ref[0]
    even = lax.rem(index, 2) == 0
    pair_at = jnp.where(even, 2 * depth, 0)
    other_at = jnp.where(even, 0, 2 * depth)
    total_layers = 3 * depth
    planes = coef_dev * depth

    for at, part in ((pair_at, pair), (other_at, other)):
        for c in range(coef_dev):
            coef_ext[c, pl.ds(at, depth)] = part[c * depth : (c + 1) * depth]
        mean_ext[pl.ds(at, depth)] = part[2 * planes : 2 * planes + depth]
    for c in range(coef_dev):
        coef_ext[c, depth : 2 * depth] = coeffs[c]
    mean_ext[depth : 2 * depth] = mean[...]

    def layer(l, source_of):
        xm, xp, ym, yp, down, up, total = faces(mean_ext[l - 1], mean_ext[l], mean_ext[l + 1])
        diagonal = REACTION + total
        absolute = index * depth + l - depth
        inside = (absolute >= 0) & (absolute < n_space * depth)
        face[0, l], face[1, l], face[2, l], face[3, l] = xm, xp, ym, yp
        face[4, l], face[5, l] = down, up
        face[6, l] = jnp.where(inside, 1.0 / diagonal, 0.0)

        def coefficient(c, carry):
            v = coef_ext[c, l]
            spread = lateral(xm * v, xp * v, ym * v, yp * v)
            spread = spread + down * coef_ext[c, l - 1] + up * coef_ext[c, l + 1]
            known[c, l] = source_of(c) - (diagonal * v - spread)
            return carry

        for c in range(coef_dev):
            coefficient(c, 0)

    def from_part(part, at):
        def body(l, carry):
            layer(l, lambda c: part[planes + c * depth + l - at])
            return carry

        lax.fori_loop(jnp.maximum(at, 1), jnp.minimum(at + depth, total_layers - 1), body, 0)

    from_part(pair, pair_at)
    from_part(other, other_at)

    def body(l, carry):
        layer(l, lambda c: source[c, l - depth])
        return carry

    lax.fori_loop(depth, 2 * depth, body, 0)


def sweep_constants():
    midpoint = (BOUND_HIGH + BOUND_LOW) / 2.0
    halfwidth = (BOUND_HIGH - BOUND_LOW) / 2.0
    ratio = midpoint / halfwidth
    now = 1.0 / ratio
    steps = []
    for _ in range(ITERS - 1):
        following = 1.0 / (2.0 * ratio - now)
        steps.append((following * now, 2.0 * following / halfwidth))
        now = following
    return midpoint, steps


def order_parts(trio, even, n, layers, summed, nx):
    for part, slab in zip(trio, (1, jnp.where(even, 0, 2), jnp.where(even, 2, 0))):
        for t in range(n):
            at = t * layers * nx
            summed[slab, t] = part[at : at + layers * nx].reshape(layers, nx, -1)


def coupled(l, depth, start, layers, coef_dev, summed, mode_face, visit):
    slab, at = divmod(l, depth)
    near = {}
    for offset in (-1, 0, 1):
        s, i = divmod(l + offset, depth)
        if 0 <= s < 3 and start <= i < start + layers:
            near[offset] = (s, i - start)
    if not near:
        return False
    for c in range(coef_dev):
        to, rest = [None] * 4, None

        def add(total, term):
            return term if total is None else total + term

        for k in range(M):
            if 0 in near:
                s, i = near[0]
                v = summed[s, c * M + k, i]
                for q in range(4):
                    to[q] = add(to[q], mode_face[k, q, l] * v)
                rest = add(rest, -(mode_face[k, 6, l] * v))
            for offset, which in ((-1, 4), (1, 5)):
                if offset in near:
                    s, i = near[offset]
                    rest = add(rest, mode_face[k, which, l] * summed[s, c * M + k, i])
        visit(c, rest + lateral(*to) if 0 in near else rest)
    return True


def begin_kernel(coef_dev, depth, layers, space_ref, known, own, other, pair, *refs):
    rest, mode_face, summed, mode_ext = refs
    nx = known.shape[2]
    targets = coef_dev * M
    even = lax.rem(space_ref[0], 2) == 0
    order_parts((own, other, pair), even, targets, layers, summed, nx)
    for part, slab in zip(
        (own, other, pair), (1, jnp.where(even, 0, 2), jnp.where(even, 2, 0))
    ):
        for k in range(M):
            at = (targets * layers + k * depth) * nx
            mode_ext[k, pl.ds(slab * depth, depth)] = part[at : at + depth * nx].reshape(
                depth, nx, -1
            )
    last = 3 * depth - 1

    def mode_faces(l, carry):
        for k in range(M):
            got = faces(mode_ext[k, l - 1], mode_ext[k, l], mode_ext[k, l + 1])
            for i, value in enumerate(got):
                mode_face[k, i, l] = value
        return carry

    lax.fori_loop(1, last, mode_faces, 0)
    for l in range(1, last):

        def visit(c, value, l=l):
            rest[c, l] = known[c, l] + value

        if not coupled(l, depth, 0, layers, coef_dev, summed, mode_face, visit):
            for c in range(coef_dev):
                rest[c, l] = known[c, l]


def sweep_kernel(coef_dev, depth, start, layers, space_ref, rest, mode_face, face, *refs):
    own, other, pair, residual, correction, summed, scaled, first, second = refs
    nx = rest.shape[2]
    even = lax.rem(space_ref[0], 2) == 0
    order_parts((own, other, pair), even, coef_dev * M, layers, summed, nx)
    last = 3 * depth - 1
    midpoint, steps = sweep_constants()
    for l in range(1, last):

        def visit(c, value, l=l):
            total = rest[c, l] if value is None else rest[c, l] + value
            w = total * face[6, l]
            d = w * (1.0 / midpoint)
            scaled[c, l] = w
            first[c, l] = d
            if depth <= l < 2 * depth:
                residual[c, l - depth] = total
                correction[c, l - depth] = d

        if not coupled(l, depth, start, layers, coef_dev, summed, mode_face, visit):
            for c in range(coef_dev):
                visit(c, None)

    now, later = first, second
    for number, (keep, gain) in enumerate(steps):

        def swept(l, own, now=now, later=later, keep=keep, gain=gain, number=number):
            for c in range(coef_dev):
                v = now[c, l]
                spread = lateral(face[0, l] * v, face[1, l] * v, face[2, l] * v, face[3, l] * v)
                spread = spread + face[4, l] * now[c, l - 1] + face[5, l] * now[c, l + 1]
                w = scaled[c, l] - v + face[6, l] * spread
                d = keep * v + gain * w
                if number + 1 < len(steps):
                    scaled[c, l] = w
                    later[c, l] = d
                if own:
                    correction[c, l - depth] = correction[c, l - depth] + d

        over_layers(swept, depth, len(steps) - 1 - number)
        now, later = later, now


def over_layers(visit, depth, halo):
    def own(l, carry):
        visit(l, True)
        return carry

    def outside(i, carry):
        visit(jnp.where(i < halo, depth - halo + i, 2 * depth - halo + i), False)
        return carry

    lax.fori_loop(depth, 2 * depth, own, 0)
    if halo:
        lax.fori_loop(0, 2 * halo, outside, 0)


def residual_and_correction(coeffs, source, mean_field, mode_bank, mode_owner, links):
    coef_dev, depth, nx, ny = coeffs.shape
    n_space = lax.axis_size("space")
    slot_rows = depth * nx
    per_chunk = depth // CHUNKS
    layer_counts = [per_chunk] * CHUNKS
    index = lax.axis_index("space").astype(jnp.int32).reshape(1)

    rows_of = [layers * nx for layers in layer_counts]
    count = lax.axis_size("chaos")
    shifts = count // 2 - 1
    capacity = max(2, (M * coef_dev - 1 + shifts - 1) // shifts)
    assert count * capacity <= ny
    chunks = pack(coeffs, mode_bank, links[0], capacity, rows_of)

    sums = chaos_sums(
        chunks, coef_dev, capacity, rows_of, slot_rows, mode_owner
    )

    early = jnp.concatenate(
        [coeffs.reshape(-1, nx, ny), source.reshape(-1, nx, ny), mean_field], axis=0
    )
    other, pair = depth_pair(early)
    wide = (coef_dev, 3 * depth, nx, ny)
    known, face = pl.pallas_call(
        functools.partial(base_kernel, coef_dev, depth, n_space),
        out_shape=(
            jax.ShapeDtypeStruct(wide, jnp.float32),
            jax.ShapeDtypeStruct((7, 3 * depth, nx, ny), jnp.float32),
        ),
        in_specs=[SMEM] + [VMEM] * 5,
        out_specs=(VMEM, VMEM),
        scratch_shapes=[
            pltpu.VMEM(wide, jnp.float32),
            pltpu.VMEM((3 * depth, nx, ny), jnp.float32),
        ],
        cost_estimate=cost(3 * depth * coef_dev, nx, ny, 20),
        compiler_params=pltpu.CompilerParams(vmem_limit_bytes=16 << 20),
        name="base",
    )(index, coeffs, source, mean_field, other, pair)

    parts = [[own, *depth_pair(own)] for own in sums]
    layers = layer_counts[0]
    ordered = pltpu.VMEM((3, coef_dev * M, layers, nx, ny), jnp.float32)
    mode_faces = (M, 7, 3 * depth, nx, ny)
    rest, mode_face = pl.pallas_call(
        functools.partial(begin_kernel, coef_dev, depth, layers),
        out_shape=(
            jax.ShapeDtypeStruct(wide, jnp.float32),
            jax.ShapeDtypeStruct(mode_faces, jnp.float32),
        ),
        in_specs=[SMEM] + [VMEM] * 4,
        out_specs=(VMEM, VMEM),
        scratch_shapes=[ordered, pltpu.VMEM((M, 3 * depth, nx, ny), jnp.float32)],
        compiler_params=pltpu.CompilerParams(vmem_limit_bytes=16 << 20),
        cost_estimate=cost(3 * depth * coef_dev, nx, ny, 40),
        name="begin",
    )(index, known, *parts[0])
    out = jax.ShapeDtypeStruct(coeffs.shape, jnp.float32)
    return pl.pallas_call(
        functools.partial(sweep_kernel, coef_dev, depth, depth - layers, layers),
        out_shape=(out, out),
        in_specs=[SMEM] + [VMEM] * 6,
        out_specs=(VMEM, VMEM),
        scratch_shapes=[ordered] + [pltpu.VMEM(wide, jnp.float32)] * 3,
        compiler_params=pltpu.CompilerParams(vmem_limit_bytes=20 << 20),
        cost_estimate=cost(6 * depth * coef_dev, nx, ny, 40),
        name="sweeps",
    )(index, rest, mode_face, face, *parts[1])


def solution(mesh):
    in_specs = (
        P("chaos", "space", None, None),
        P("chaos", "space", None, None),
        P("space", None, None),
        P("chaos", "space", None, None),
        P(),
        P("chaos", None, None),
    )
    out_specs = (P("chaos", "space", None, None), P("chaos", "space", None, None))
    return jax.shard_map(
        residual_and_correction, mesh=mesh, in_specs=in_specs, out_specs=out_specs, check_vma=False
    )
```

time: 103 us -> 79.2 us (0.77)
  the two profiles are of different devices: /device:TPU:9 before, /device:TPU:1 now
where the time goes in v2:
time: 79.2 us; the launch traced here: 78.7 us
  waiting for transfers between devices  28.3 us (36%)
  Pallas kernels  23.1 us (29%)
  starting transfers between devices  21.1 us (27%)
  local copies, waits for them, and re-layouts  3.09 us (4%)
  other arithmetic  2.36 us (3%)
  between operations  0.92 us (1%)
    ppermute x14, waiting for transfers between devices, chaos_sums(): block = lax.ppermute(block, 'chaos', pairs)  27.4 us
    ppermute x3, starting transfers between devices, depth_pair(): other = lax.ppermute(values, 'space', second)  11 us
    ppermute x14, starting transfers between devices, chaos_sums(): block = lax.ppermute(block, 'chaos', pairs)  9.94 us
    pallas_call x4, Pallas kernels, sum_blocks(): pl.pallas_call(functools.partial(sum_kernel, n, coef_dev, capacity, rows,...  7.66 us
    pallas_call x1, Pallas kernels, residual_and_correction(): pl.pallas_call(functools.partial(sweep_kernel, coef_dev, depth, depth - l...  6.01 us
    pallas_call x1, Pallas kernels, residual_and_correction(): pl.pallas_call(functools.partial(base_kernel, coef_dev, depth, n_space),...  3.53 us
    pallas_call x1, Pallas kernels, residual_and_correction(): pl.pallas_call(functools.partial(begin_kernel, coef_dev, depth, layers),...  3.18 us
    unnamed x28, local copies, waits for them, and re-layouts  2.92 us
  transfers between devices with their start and end apart: 20, of which 9 were waited for; matrix products, arithmetic and copies ran while one was open for 3% of the time, Pallas kernels for 18%

profile of v2, /device:TPU:1, one launch (start us, length us, event | category | flops | bytes accessed | tf_op | source)
XLA Modules:
  0.0 78.7 jit_solution(8592246220051154956)
XLA Ops:
  0.6 2.7 %pack.1 = (f32[648,128]{1,0:T(8,128)}, f32[520,128]{1,0:T(8,128)}) custom-call(s32[4,32]{1,0:T(4,128)} %bitcast.21, f32[8,128,128]{2,1,0:T(8,128)} %bitcast.17, f32[1,128,128]{2,1,0:T(8,128)} %bitcast.20), custom_call_target="tpu_custom_call" | custom-call | flops 131072 | bytes 1048576 | tf_op jit(solution)/shard_map/pack/pallas_call | solution.py:119
  3.3 2.2 %collective-permute-start.5 = (f32[648,128]{1,0:T(8,128)}, f32[648,128]{1,0:T(8,128)S(1)}, u32[]{:S(2)}, u32[]{:S(2)}) collective-permute-start(f32[648,128]{1,0:T(8,128)} %get-tuple-element.9.refs_0_), channel_id=1, source_target_pairs={{0,8},{8,16},{16,24},{24,28},{28,20},{20,12},{12,4},{4,0},{1,9},{9... | collective-permute-start | bytes 995336 | tf_op jit(solution)/shard_map/ppermute | solution.py:260
  5.5 1.4 %collective-permute-start.11 = (f32[520,128]{1,0:T(8,128)}, f32[520,128]{1,0:T(8,128)S(1)}, u32[]{:S(2)}, u32[]{:S(2)}) collective-permute-start(f32[520,128]{1,0:T(8,128)} %get-tuple-element.13.refs_0_), channel_id=1, source_target_pairs={{8,0},{16,8},{24,16},{28,24},{20,28},{12,20},{4,12},{0,4},{9,1},{1... | collective-permute-start | bytes 798728 | tf_op jit(solution)/shard_map/ppermute | solution.py:260
  7.0 6.1 %collective-permute-done.5.refs_2_ = f32[648,128]{1,0:T(8,128)S(1)} collective-permute-done((f32[648,128]{1,0:T(8,128)}, f32[648,128]{1,0:T(8,128)S(1)}, u32[]{:S(2)}, u32[]{:S(2)}) %collective-permute-start.5) | collective-permute-done | bytes 331808 | tf_op jit(solution)/shard_map/ppermute | solution.py:260
  13.1 1.3 %collective-permute-start.6 = (f32[648,128]{1,0:T(8,128)S(1)}, f32[648,128]{1,0:T(8,128)S(1)}, u32[]{:S(2)}, u32[]{:S(2)}) collective-permute-start(f32[648,128]{1,0:T(8,128)S(1)} %collective-permute-done.5.refs_2_), channel_id=1, source_target_pairs={{0,8},{8,16},{16,24},{24,28},{28,20},{20,12},{12,4},{4,0},{1,9},{9... | collective-permute-start | bytes 995336 | tf_op jit(solution)/shard_map/ppermute | solution.py:260
  14.4 2.4 %pad_maximum_fusion = f32[68,32,128]{2,1,0:T(8,128)} fusion(f32[4,32,128]{2,1,0:T(8,128)} %mean.1, f32[32,32,128]{2,1,0:T(8,128)} %bitcast.19, f32[32,32,128]{2,1,0:T(8,128)} %bitcast.18), kind=kLoop, calls=%fused_computation | loop fusion | flops 557056 | bytes 2228224 | tf_op jit(solution)/shard_map/concatenate | solution.py:508
  16.7 6.0 %collective-permute-start = (f32[68,32,128]{2,1,0:T(8,128)}, f32[68,32,128]{2,1,0:T(8,128)S(1)}, u32[]{:S(2)}, u32[]{:S(2)}) collective-permute-start(f32[68,32,128]{2,1,0:T(8,128)} %pad_maximum_fusion), channel_id=1, source_target_pairs={{1,2},{2,1},{5,6},{6,5},{9,10},{10,9},{13,14},{14,13},{17,18},{18,... | collective-permute-start | bytes 3342344 | tf_op jit(solution)/shard_map/ppermute | solution.py:290
  23.6 1.2 %collective-permute-start.3 = (f32[648,128]{1,0:T(8,128)S(1)}, f32[648,128]{1,0:T(8,128)S(1)}, u32[]{:S(2)}, u32[]{:S(2)}) collective-permute-start(f32[648,128]{1,0:T(8,128)S(1)} %collective-permute-done.2.refs_1_), channel_id=1, source_target_pairs={{8,0},{16,8},{24,16},{28,24},{20,28},{12,20},{4,12},{0,4},{9,1},{1... | collective-permute-start | bytes 995336 | tf_op jit(solution)/shard_map/ppermute | solution.py:260
  25.9 1.3 %collective-permute-start.7 = (f32[648,128]{1,0:T(8,128)S(1)}, f32[648,128]{1,0:T(8,128)S(1)}, u32[]{:S(2)}, u32[]{:S(2)}) collective-permute-start(f32[648,128]{1,0:T(8,128)S(1)} %collective-permute-done.6.refs_4_), channel_id=1, source_target_pairs={{0,8},{8,16},{16,24},{24,28},{28,20},{20,12},{12,4},{4,0},{1,9},{9... | collective-permute-start | bytes 995336 | tf_op jit(solution)/shard_map/ppermute | solution.py:260
  27.2 4.1 %collective-permute-done.12.refs_3_ = f32[520,128]{1,0:T(8,128)S(1)} collective-permute-done((f32[520,128]{1,0:T(8,128)S(1)}, f32[520,128]{1,0:T(8,128)S(1)}, u32[]{:S(2)}, u32[]{:S(2)}) %collective-permute-start.12) | collective-permute-done | bytes 266272 | tf_op jit(solution)/shard_map/ppermute | solution.py:260
  32.1 6.2 %collective-permute-done.3.refs_3_ = f32[648,128]{1,0:T(8,128)S(1)} collective-permute-done((f32[648,128]{1,0:T(8,128)S(1)}, f32[648,128]{1,0:T(8,128)S(1)}, u32[]{:S(2)}, u32[]{:S(2)}) %collective-permute-start.3) | collective-permute-done | bytes 331808 | tf_op jit(solution)/shard_map/ppermute | solution.py:260
  38.6 1.8 %collective-permute-done.7.refs_2_ = f32[648,128]{1,0:T(8,128)S(1)} collective-permute-done((f32[648,128]{1,0:T(8,128)S(1)}, f32[648,128]{1,0:T(8,128)S(1)}, u32[]{:S(2)}, u32[]{:S(2)}) %collective-permute-start.7) | collective-permute-done | bytes 331808 | tf_op jit(solution)/shard_map/ppermute | solution.py:260
  40.7 3.3 %collective-permute-done.13.refs_0_ = f32[520,128]{1,0:T(8,128)} collective-permute-done((f32[520,128]{1,0:T(8,128)S(1)}, f32[520,128]{1,0:T(8,128)}, u32[]{:S(2)}, u32[]{:S(2)}) %collective-permute-start.13) | collective-permute-done | bytes 266272 | tf_op jit(solution)/shard_map/ppermute | solution.py:260
  44.1 1.3 %collective-permute-start.17 = (f32[520,128]{1,0:T(8,128)}, f32[520,128]{1,0:T(8,128)}, u32[]{:S(2)}, u32[]{:S(2)}) collective-permute-start(f32[520,128]{1,0:T(8,128)} %collective-permute-done.16.refs_4_), channel_id=1, source_target_pairs={{0,8},{8,16},{16,24},{24,28},{28,20},{20,12},{12,4},{4,0},{1,9},{9... | collective-permute-start | bytes 798728 | tf_op jit(solution)/shard_map/ppermute | solution.py:260
  45.4 5.1 %collective-permute-done.4.refs_0_ = f32[648,128]{1,0:T(8,128)S(1)} collective-permute-done((f32[648,128]{1,0:T(8,128)S(1)}, f32[648,128]{1,0:T(8,128)S(1)}, u32[]{:S(2)}, u32[]{:S(2)}) %collective-permute-start.4) | collective-permute-done | bytes 331808 | tf_op jit(solution)/shard_map/ppermute | solution.py:260
  51.4 1.6 %shard_map.77.refs_3_ = f32[1280,128]{1,0:T(8,128)S(1)} custom-call(s32[8]{0:T(128)S(1)} %stack.56.where, f32[648,128]{1,0:T(8,128)S(1)} %copy-done.2, f32[648,128]{1,0:T(8,128)S(1)} %collective-permute-done.2.refs_1_, f32[648,128]{1,0:T(8,128)S(1)} %collective-permute-done.5.refs_2_, f32[648,128]{1,0:T(8,128)S(1)} %collective-permute-done.3.refs_3_, ...), custom_call_target="tpu_custom_call" | custom-call | flops 524288 | bytes 1048576 | tf_op jit(solution)/shard_map/pallas_call | solution.py:174
  53.1 2.0 %shard_map.78.own = f32[1280,128]{1,0:T(8,128)S(1)} custom-call(s32[6]{0:T(128)S(1)} %stack.50.where, f32[648,128]{1,0:T(8,128)S(1)} %copy-done.4, f32[648,128]{1,0:T(8,128)} %collective-permute-done.8.refs_1_, f32[648,128]{1,0:T(8,128)S(1)} %collective-permute-done.7.refs_2_, f32[1280,128]{1,0:T(8,128)S(1)} %shard_map.77.refs_3_), custom_call_target="tpu_custom_call" | custom-call | flops 524288 | bytes 1048576 | tf_op jit(solution)/shard_map/pallas_call | solution.py:174
  55.1 1.9 %collective-permute-start.9 = (f32[1280,128]{1,0:T(8,128)S(1)}, f32[1280,128]{1,0:T(8,128)}, u32[]{:S(2)}, u32[]{:S(2)}) collective-permute-start(f32[1280,128]{1,0:T(8,128)S(1)} %shard_map.78.own), channel_id=1, source_target_pairs={{1,2},{2,1},{5,6},{6,5},{9,10},{10,9},{13,14},{14,13},{17,18},{18,... | collective-permute-start | bytes 1966088 | tf_op jit(solution)/shard_map/ppermute | solution.py:290
  57.2 2.1 %shard_map.79.refs_3_ = f32[1024,128]{1,0:T(8,128)S(1)} custom-call(s32[8]{0:T(128)S(1)} %stack.56.where, f32[520,128]{1,0:T(8,128)S(1)} %copy-done.5, f32[520,128]{1,0:T(8,128)S(1)} %copy-done.7, f32[520,128]{1,0:T(8,128)S(1)} %copy-done.9, f32[520,128]{1,0:T(8,128)S(1)} %copy-done.11, f32[520,128]{1,0:T(8,128)} %collective-permute-done.16.refs_4_), custom_call_target="tpu_custom_call" | custom-call | flops 524288 | bytes 1048576 | tf_op jit(solution)/shard_map/pallas_call | solution.py:174
  59.9 2.0 %shard_map.80.refs_0_ = f32[1024,128]{1,0:T(8,128)S(1)} custom-call(s32[6]{0:T(128)S(1)} %stack.50.where, f32[520,128]{1,0:T(8,128)} %collective-permute-done.13.refs_0_, f32[520,128]{1,0:T(8,128)} %collective-permute-done.14.refs_1_, f32[520,128]{1,0:T(8,128)} %collective-permute-done.17.refs_2_, f32[1024,128]{1,0:T(8,128)S(1)} %shard_map.79.refs_3_), custom_call_target="tpu_custom_call" | custom-call | flops 524288 | bytes 1048576 | tf_op jit(solution)/shard_map/pallas_call | solution.py:174
  61.9 3.1 %collective-permute-start.18 = (f32[1024,128]{1,0:T(8,128)S(1)}, f32[1024,128]{1,0:T(8,128)}, u32[]{:S(2)}, u32[]{:S(2)}) collective-permute-start(f32[1024,128]{1,0:T(8,128)S(1)} %shard_map.80.refs_0_), channel_id=1, source_target_pairs={{1,2},{2,1},{5,6},{6,5},{9,10},{10,9},{13,14},{14,13},{17,18},{18,... | collective-permute-start | bytes 1572872 | tf_op jit(solution)/shard_map/ppermute | solution.py:290
  65.2 3.5 %base.1 = (f32[8,12,32,128]{3,2,1,0:T(8,128)S(1)}, f32[7,12,32,128]{3,2,1,0:T(8,128)S(1)}) custom-call(s32[1]{0:T(128)} %bitcast.space_ref, f32[8,4,32,128]{3,2,1,0:T(8,128)S(1)} %copy-done, f32[8,4,32,128]{3,2,1,0:T(8,128)S(1)} %copy-done.1, f32[4,32,128]{2,1,0:T(8,128)S(1)} %copy-done.12, f32[68,32,128]{2,1,0:T(8,128)S(1)} %collective-permute-done.refs_0_, ...), custom_call_target="tpu_custom_call" | custom-call | flops 7864320 | bytes 3145728 | tf_op jit(solution)/shard_map/base/pallas_call | solution.py:513
  68.7 3.2 %begin.1 = (f32[8,12,32,128]{3,2,1,0:T(8,128)S(1)}, f32[2,7,12,32,128]{4,3,2,1,0:T(8,128)S(1)}) custom-call(s32[1]{0:T(128)} %bitcast.space_ref, f32[8,12,32,128]{3,2,1,0:T(8,128)S(1)} %get-tuple-element.8.known, f32[1280,128]{1,0:T(8,128)S(1)} %shard_map.78.own, f32[1280,128]{1,0:T(8,128)} %collective-permute-done.9.other, ...), custom_call_target="tpu_custom_call" | custom-call | flops 15728640 | bytes 3145728 | tf_op jit(solution)/shard_map/begin/pallas_call | solution.py:534
  72.7 6.0 %sweeps.1 = (f32[8,4,32,128]{3,2,1,0:T(8,128)}, f32[8,4,32,128]{3,2,1,0:T(8,128)}) custom-call(s32[1]{0:T(128)} %bitcast.space_ref, f32[8,12,32,128]{3,2,1,0:T(8,128)S(1)} %get-tuple-element.10.rest, f32[2,7,12,32,128]{4,3,2,1,0:T(8,128)S(1)} %get-tuple-element.11.mode_face, f32[7,12,32,128]{3,2,1,0:T(8,128)S(1)} %get-tuple-element.12.face, ...), custom_call_target="tpu_custom_call" | custom-call | flops 31457280 | bytes 6291456 | tf_op jit(solution)/shard_map/sweeps/pallas_call | solution.py:548
  (55 shorter events, 6.1 us)
Async XLA Ops:
  3.3 9.8 %collective-permute-start.5 = (f32[648,128]{1,0:T(8,128)}, f32[648,128]{1,0:T(8,128)S(1)}, u32[]{:S(2)}, u32[]{:S(2)}) collective-permute-start(f32[648,128]{1,0:T(8,128)} %get-tuple-element.9.refs_0_), channel_id=1, source_target_pairs={{0,8},{8,16},{16,24},{24,28},{28,20},{20,12},{12,4},{4,0},{1,9},{9... | collective-permute-start | bytes 995336 | tf_op jit(solution)/shard_map/ppermute | solution.py:260
  5.5 18.2 %collective-permute-start.2 = (f32[648,128]{1,0:T(8,128)}, f32[648,128]{1,0:T(8,128)S(1)}, u32[]{:S(2)}, u32[]{:S(2)}) collective-permute-start(f32[648,128]{1,0:T(8,128)} %get-tuple-element.9.refs_0_), channel_id=1, source_target_pairs={{8,0},{16,8},{24,16},{28,24},{20,28},{12,20},{4,12},{0,4},{9,1},{1... | collective-permute-start | bytes 995336 | tf_op jit(solution)/shard_map/ppermute | solution.py:260
  5.5 17.2 %collective-permute-start.11 = (f32[520,128]{1,0:T(8,128)}, f32[520,128]{1,0:T(8,128)S(1)}, u32[]{:S(2)}, u32[]{:S(2)}) collective-permute-start(f32[520,128]{1,0:T(8,128)} %get-tuple-element.13.refs_0_), channel_id=1, source_target_pairs={{8,0},{16,8},{24,16},{28,24},{20,28},{12,20},{4,12},{0,4},{9,1},{1... | collective-permute-start | bytes 798728 | tf_op jit(solution)/shard_map/ppermute | solution.py:260
  6.8 18.0 %collective-permute-start.15 = (f32[520,128]{1,0:T(8,128)}, f32[520,128]{1,0:T(8,128)S(1)}, u32[]{:S(2)}, u32[]{:S(2)}) collective-permute-start(f32[520,128]{1,0:T(8,128)} %get-tuple-element.13.refs_0_), channel_id=1, source_target_pairs={{0,8},{8,16},{16,24},{24,28},{28,20},{20,12},{12,4},{4,0},{1,9},{9... | collective-permute-start | bytes 798728 | tf_op jit(solution)/shard_map/ppermute | solution.py:260
  13.1 12.8 %collective-permute-start.6 = (f32[648,128]{1,0:T(8,128)S(1)}, f32[648,128]{1,0:T(8,128)S(1)}, u32[]{:S(2)}, u32[]{:S(2)}) collective-permute-start(f32[648,128]{1,0:T(8,128)S(1)} %collective-permute-done.5.refs_2_), channel_id=1, source_target_pairs={{0,8},{8,16},{16,24},{24,28},{28,20},{20,12},{12,4},{4,0},{1,9},{9... | collective-permute-start | bytes 995336 | tf_op jit(solution)/shard_map/ppermute | solution.py:260
  14.4 36.9 %copy-start.13 = (s32[2]{0:T(128)S(1)}, s32[2]{0:T(128)}, u32[]{:S(2)}) copy-start(s32[2]{0:T(128)} %param.10) | copy-start | bytes 28
  14.4 37.1 %copy-start.2 = (f32[648,128]{1,0:T(8,128)S(1)}, f32[648,128]{1,0:T(8,128)}, u32[]{:S(2)}) copy-start(f32[648,128]{1,0:T(8,128)} %get-tuple-element.9.refs_0_) | copy-start | bytes 995332
  16.7 48.3 %collective-permute-start = (f32[68,32,128]{2,1,0:T(8,128)}, f32[68,32,128]{2,1,0:T(8,128)S(1)}, u32[]{:S(2)}, u32[]{:S(2)}) collective-permute-start(f32[68,32,128]{2,1,0:T(8,128)} %pad_maximum_fusion), channel_id=1, source_target_pairs={{1,2},{2,1},{5,6},{6,5},{9,10},{10,9},{13,14},{14,13},{17,18},{18,... | collective-permute-start | bytes 3342344 | tf_op jit(solution)/shard_map/ppermute | solution.py:290
  22.7 8.6 %collective-permute-start.12 = (f32[520,128]{1,0:T(8,128)S(1)}, f32[520,128]{1,0:T(8,128)S(1)}, u32[]{:S(2)}, u32[]{:S(2)}) collective-permute-start(f32[520,128]{1,0:T(8,128)S(1)} %collective-permute-done.11.refs_1_), channel_id=1, source_target_pairs={{8,0},{16,8},{24,16},{28,24},{20,28},{12,20},{4,12},{0,4},{9,1},{1... | collective-permute-start | bytes 798728 | tf_op jit(solution)/shard_map/ppermute | solution.py:260
  23.6 14.7 %collective-permute-start.3 = (f32[648,128]{1,0:T(8,128)S(1)}, f32[648,128]{1,0:T(8,128)S(1)}, u32[]{:S(2)}, u32[]{:S(2)}) collective-permute-start(f32[648,128]{1,0:T(8,128)S(1)} %collective-permute-done.2.refs_1_), channel_id=1, source_target_pairs={{8,0},{16,8},{24,16},{28,24},{20,28},{12,20},{4,12},{0,4},{9,1},{1... | collective-permute-start | bytes 995336 | tf_op jit(solution)/shard_map/ppermute | solution.py:260
  24.9 13.7 %collective-permute-start.16 = (f32[520,128]{1,0:T(8,128)S(1)}, f32[520,128]{1,0:T(8,128)}, u32[]{:S(2)}, u32[]{:S(2)}) collective-permute-start(f32[520,128]{1,0:T(8,128)S(1)} %collective-permute-done.15.refs_2_), channel_id=1, source_target_pairs={{0,8},{8,16},{16,24},{24,28},{28,20},{20,12},{12,4},{4,0},{1,9},{9... | collective-permute-start | bytes 798728 | tf_op jit(solution)/shard_map/ppermute | solution.py:260
  25.9 14.4 %collective-permute-start.7 = (f32[648,128]{1,0:T(8,128)S(1)}, f32[648,128]{1,0:T(8,128)S(1)}, u32[]{:S(2)}, u32[]{:S(2)}) collective-permute-start(f32[648,128]{1,0:T(8,128)S(1)} %collective-permute-done.6.refs_4_), channel_id=1, source_target_pairs={{0,8},{8,16},{16,24},{24,28},{28,20},{20,12},{12,4},{4,0},{1,9},{9... | collective-permute-start | bytes 995336 | tf_op jit(solution)/shard_map/ppermute | solution.py:260
  31.3 12.8 %collective-permute-start.13 = (f32[520,128]{1,0:T(8,128)S(1)}, f32[520,128]{1,0:T(8,128)}, u32[]{:S(2)}, u32[]{:S(2)}) collective-permute-start(f32[520,128]{1,0:T(8,128)S(1)} %collective-permute-done.12.refs_3_), channel_id=1, source_target_pairs={{8,0},{16,8},{24,16},{28,24},{20,28},{12,20},{4,12},{0,4},{9,1},{1... | collective-permute-start | bytes 798728 | tf_op jit(solution)/shard_map/ppermute | solution.py:260
  38.4 12.1 %collective-permute-start.4 = (f32[648,128]{1,0:T(8,128)S(1)}, f32[648,128]{1,0:T(8,128)S(1)}, u32[]{:S(2)}, u32[]{:S(2)}) collective-permute-start(f32[648,128]{1,0:T(8,128)S(1)} %collective-permute-done.3.refs_3_), channel_id=1, source_target_pairs={{8,0},{16,8},{24,16},{28,24},{20,28},{12,20},{4,12},{0,4},{9,1},{1... | collective-permute-start | bytes 995336 | tf_op jit(solution)/shard_map/ppermute | solution.py:260
  38.5 26.6 %collective-permute-start.1 = (f32[68,32,128]{2,1,0:T(8,128)}, f32[68,32,128]{2,1,0:T(8,128)}, u32[]{:S(2)}, u32[]{:S(2)}) collective-permute-start(f32[68,32,128]{2,1,0:T(8,128)} %pad_maximum_fusion), channel_id=1, source_target_pairs={{0,1},{1,0},{2,3},{3,2},{4,5},{5,4},{6,7},{7,6},{8,9},{9,8},{10,11... | collective-permute-start | bytes 3342344 | tf_op jit(solution)/shard_map/ppermute | solution.py:291
  40.4 12.8 %collective-permute-start.8 = (f32[648,128]{1,0:T(8,128)S(1)}, f32[648,128]{1,0:T(8,128)}, u32[]{:S(2)}, u32[]{:S(2)}) collective-permute-start(f32[648,128]{1,0:T(8,128)S(1)} %collective-permute-done.7.refs_2_), channel_id=1, source_target_pairs={{0,8},{8,16},{16,24},{24,28},{28,20},{20,12},{12,4},{4,0},{1,9},{9... | collective-permute-start | bytes 995336 | tf_op jit(solution)/shard_map/ppermute | solution.py:260
  44.1 13.0 %collective-permute-start.17 = (f32[520,128]{1,0:T(8,128)}, f32[520,128]{1,0:T(8,128)}, u32[]{:S(2)}, u32[]{:S(2)}) collective-permute-start(f32[520,128]{1,0:T(8,128)} %collective-permute-done.16.refs_4_), channel_id=1, source_target_pairs={{0,8},{8,16},{16,24},{24,28},{28,20},{20,12},{12,4},{4,0},{1,9},{9... | collective-permute-start | bytes 798728 | tf_op jit(solution)/shard_map/ppermute | solution.py:260
  51.2 8.7 %collective-permute-start.14 = (f32[520,128]{1,0:T(8,128)}, f32[520,128]{1,0:T(8,128)}, u32[]{:S(2)}, u32[]{:S(2)}) collective-permute-start(f32[520,128]{1,0:T(8,128)} %collective-permute-done.13.refs_0_), channel_id=1, source_target_pairs={{8,0},{16,8},{24,16},{28,24},{20,28},{12,20},{4,12},{0,4},{9,1},{1... | collective-permute-start | bytes 798728 | tf_op jit(solution)/shard_map/ppermute | solution.py:260
  55.1 13.6 %collective-permute-start.9 = (f32[1280,128]{1,0:T(8,128)S(1)}, f32[1280,128]{1,0:T(8,128)}, u32[]{:S(2)}, u32[]{:S(2)}) collective-permute-start(f32[1280,128]{1,0:T(8,128)S(1)} %shard_map.78.own), channel_id=1, source_target_pairs={{1,2},{2,1},{5,6},{6,5},{9,10},{10,9},{13,14},{14,13},{17,18},{18,... | collective-permute-start | bytes 1966088 | tf_op jit(solution)/shard_map/ppermute | solution.py:290
  57.0 11.7 %collective-permute-start.10 = (f32[1280,128]{1,0:T(8,128)S(1)}, f32[1280,128]{1,0:T(8,128)}, u32[]{:S(2)}, u32[]{:S(2)}) collective-permute-start(f32[1280,128]{1,0:T(8,128)S(1)} %shard_map.78.own), channel_id=1, source_target_pairs={{0,1},{1,0},{2,3},{3,2},{4,5},{5,4},{6,7},{7,6},{8,9},{9,8},{10,11... | collective-permute-start | bytes 1966088 | tf_op jit(solution)/shard_map/ppermute | solution.py:291
  59.2 5.9 %copy-start = (f32[8,4,32,128]{3,2,1,0:T(8,128)S(1)}, f32[8,4,32,128]{3,2,1,0:T(8,128)}, u32[]{:S(2)}) copy-start(f32[8,4,32,128]{3,2,1,0:T(8,128)} %coeffs.1) | copy-start | bytes 1572868
  59.2 5.9 %copy-start.1 = (f32[8,4,32,128]{3,2,1,0:T(8,128)S(1)}, f32[8,4,32,128]{3,2,1,0:T(8,128)}, u32[]{:S(2)}) copy-start(f32[8,4,32,128]{3,2,1,0:T(8,128)} %source.1) | copy-start | bytes 1572868
  61.9 10.8 %collective-permute-start.18 = (f32[1024,128]{1,0:T(8,128)S(1)}, f32[1024,128]{1,0:T(8,128)}, u32[]{:S(2)}, u32[]{:S(2)}) collective-permute-start(f32[1024,128]{1,0:T(8,128)S(1)} %shard_map.80.refs_0_), channel_id=1, source_target_pairs={{1,2},{2,1},{5,6},{6,5},{9,10},{10,9},{13,14},{14,13},{17,18},{18,... | collective-permute-start | bytes 1572872 | tf_op jit(solution)/shard_map/ppermute | solution.py:290
  65.0 7.7 %collective-permute-start.19 = (f32[1024,128]{1,0:T(8,128)S(1)}, f32[1024,128]{1,0:T(8,128)}, u32[]{:S(2)}, u32[]{:S(2)}) collective-permute-start(f32[1024,128]{1,0:T(8,128)S(1)} %shard_map.80.refs_0_), channel_id=1, source_target_pairs={{0,1},{1,0},{2,3},{3,2},{4,5},{5,4},{6,7},{7,6},{8,9},{9,8},{10,11... | collective-permute-start | bytes 1572872 | tf_op jit(solution)/shard_map/ppermute | solution.py:291
  (10 other events, 26.7 us)

commit v3 on v2

--- a/solution.py
+++ b/solution.py
@@ -127,61 +127,85 @@
     )(links.T, whole_rows, slot)
 
 
-def sum_kernel(n, coef_dev, capacity, rows, slot_rows, more, where, *refs):
+def start_tables(blocks, tables, sems):
+    copies = []
+    for i, block in enumerate(blocks):
+        at = pl.ds(block.shape[0] - TABLE_ROWS, TABLE_ROWS)
+        copies.append(pltpu.make_async_copy(block.at[at], tables.at[i], sems.at[i]))
+        copies[-1].start()
+    return copies
+
+
+def table_scratch(n, lanes):
+    return [pltpu.SMEM((n, TABLE_ROWS, lanes), jnp.float32), pltpu.SemaphoreType.DMA((n,))]
+
+
+def pick_kernel(coef_dev, capacity, rows, begin, block, out, tables, sems):
+    (copy,) = start_tables([block], tables, sems)
+    out[capacity * rows :, :] = block[coef_dev * rows :, :]
+    copy.wait()
+    for e in range(capacity):
+        row = lax.div(tables[0, 0, begin[0] + e].astype(jnp.int32), coef_dev * M)
+        out[e * rows : (e + 1) * rows, :] = block[
+            pl.ds(pl.multiple_of(row * rows, rows), rows), :
+        ]
+
+
+def pick(block, device, coef_dev, capacity, rows):
+    size, lanes = block.shape
+    return pl.pallas_call(
+        functools.partial(pick_kernel, coef_dev, capacity, rows),
+        out_shape=jax.ShapeDtypeStruct((size - (coef_dev - capacity) * rows, lanes), jnp.float32),
+        in_specs=[SMEM, VMEM],
+        out_specs=VMEM,
+        scratch_shapes=table_scratch(1, lanes),
+        compiler_params=pltpu.CompilerParams(vmem_limit_bytes=8 << 20),
+        cost_estimate=cost(capacity, rows, lanes, 1),
+        name="pick",
+    )((device * capacity).astype(jnp.int32).reshape(1), block)
+
+
+def sum_kernel(picked, coef_dev, capacity, rows, slot_rows, more, where, *refs):
     refs = list(refs)
-    blocks = [refs.pop(0) for _ in range(n)]
+    blocks = [refs.pop(0) for _ in picked]
     so_far = refs.pop(0) if more else None
     out, tables, sems = refs
     targets = coef_dev * M
-    copies = [
-        pltpu.make_async_copy(
-            block.at[pl.ds(block.shape[0] - TABLE_ROWS, TABLE_ROWS)], tables.at[i], sems.at[i]
-        )
-        for i, block in enumerate(blocks)
-    ]
-    for copy in copies:
-        copy.start()
+    copies = start_tables(blocks, tables, sems)
     out[...] = so_far[...] if more else jnp.zeros_like(out)
     if slot_rows:
-        for i, block in enumerate(blocks):
+        for i, (block, few) in enumerate(zip(blocks, picked)):
             for k in range(M):
 
                 @pl.when(where[1 + k] == where[1 + M + i])
-                def _(block=block, k=k):
+                def _(block=block, k=k, few=few):
                     at = pl.ds(targets * rows + k * slot_rows, slot_rows)
-                    out[at, :] = block[pl.ds(coef_dev * rows, slot_rows), :]
+                    out[at, :] = block[pl.ds((capacity if few else coef_dev) * rows, slot_rows), :]
 
     begin = where[0] * capacity
-    for i, block in enumerate(blocks):
+    for i, (block, few) in enumerate(zip(blocks, picked)):
         copies[i].wait()
-
-        def listed(e, carry, i=i, block=block):
-            code, w = tables[i, 0, e].astype(jnp.int32), tables[i, 1, e]
-            row, target = lax.div(code, targets), lax.rem(code, targets)
+        for e in range(capacity):
+            code, w = tables[i, 0, begin + e].astype(jnp.int32), tables[i, 1, begin + e]
+            row, target = e if few else lax.div(code, targets), lax.rem(code, targets)
             at = pl.ds(pl.multiple_of(target * rows, rows), rows)
             src = block[pl.ds(pl.multiple_of(row * rows, rows), rows), :]
             out[at, :] = out[at, :] + w * src
-            return carry
-
-        lax.fori_loop(begin, begin + capacity, listed, 0)
-
-
-def sum_blocks(blocks, devices, me, mode_owner, coef_dev, capacity, rows, slot_rows, so_far):
+
+
+def sum_blocks(
+    blocks, picked, devices, me, mode_owner, coef_dev, capacity, rows, slot_rows, so_far
+):
     n, lanes = len(blocks), blocks[0].shape[1]
     size = coef_dev * M * rows + M * slot_rows
     where = jnp.stack([me] + [mode_owner[k] for k in range(M)] + devices).astype(jnp.int32)
     more = so_far is not None
     return pl.pallas_call(
-        functools.partial(
-            sum_kernel, n, coef_dev, capacity, rows, slot_rows, more
-        ),
+        functools.partial(sum_kernel, picked, coef_dev, capacity, rows, slot_rows, more),
         out_shape=jax.ShapeDtypeStruct((size, lanes), jnp.float32),
         in_specs=[SMEM] + [VMEM] * (n + more),
         out_specs=VMEM,
-        scratch_shapes=[
-            pltpu.SMEM((n, TABLE_ROWS, lanes), jnp.float32),
-            pltpu.SemaphoreType.DMA((n,)),
-        ],
+        scratch_shapes=table_scratch(n, lanes),
         compiler_params=pltpu.CompilerParams(vmem_limit_bytes=12 << 20),
         cost_estimate=cost(coef_dev * M, rows, lanes, 4),
     )(where, *blocks, *([so_far] if more else []))
@@ -204,7 +228,7 @@
 
 
 def unrolled(count):
-    return count % 2 == 0 and count <= 16
+    return count % 2 == 0 and 6 <= count <= 16
 
 
 def ring_order(count):
@@ -216,6 +240,14 @@
     return [
         (half, half - 1) if j == 0 else (half - 1, half) for j in range(CHUNKS)
     ]
+
+
+def sum_parts(count, chunk):
+    half = count // 2
+    middle = list(range(2, half - 1))
+    if chunk == 0:
+        return {"a": [0, 1], "b": middle + [half - 1]}
+    return {"a": [0, 1], "b": middle, "c": [half - 1, half]}
 
 
 def chaos_sums(chunks, coef_dev, capacity, rows_of, slot_rows, mode_owner):
@@ -239,7 +271,8 @@
             blocks = [lax.ppermute(b, "chaos", ring) for b in blocks]
             return blocks, jax.tree.map(jnp.add, sums, at_step(step, blocks))
 
-        return lax.fori_loop(1, count, body, (list(chunks), at_step(0, chunks)))[1]
+        found = lax.fori_loop(1, count, body, (list(chunks), at_step(0, chunks)))[1]
+        return found, None, jnp.int32(-1)
 
     order = ring_order(count)
     there = [(order[i], order[(i + 1) % count]) for i in range(count)]
@@ -251,23 +284,22 @@
         q = (place + shift) % count
         return jnp.where(q < half, 2 * q, 2 * (count - 1 - q) + 1)
 
-    gathered = []
-    for chunk, steps in zip(chunks, ring_steps(count)):
-        blocks = {0: chunk}
+    found, opposite = [], None
+    for j, (chunk, steps) in enumerate(zip(chunks, ring_steps(count))):
+        blocks = {0: (chunk, False)}
         for pairs, sign, n_steps in ((there, -1, steps[0]), (back, 1, steps[1])):
             block = chunk
             for step in range(1, n_steps + 1):
+                if step == n_steps:
+                    block = pick(block, device_at(-sign), coef_dev, capacity, rows_of[j])
                 block = lax.ppermute(block, "chaos", pairs)
-                blocks[sign * step] = block
-        gathered.append({shift % count: block for shift, block in blocks.items()})
-    early = [0] + [s for step in range(1, half - 1) for s in (step, count - step)]
-    late = [s for s in range(count) if s not in early]
-    found = []
-    for j, blocks in enumerate(gathered):
+                blocks[sign * step % count] = (block, step == n_steps)
         sums = None
-        for shifts in (early, late):
+        for distances in sum_parts(count, j).values():
+            shifts = sorted({s * d % count for d in distances for s in (1, -1)})
             sums = sum_blocks(
-                [blocks[s] for s in shifts],
+                [blocks[s][0] for s in shifts],
+                [blocks[s][1] for s in shifts],
                 [device_at(s) for s in shifts],
                 *fixed,
                 rows_of[j],
@@ -275,7 +307,9 @@
                 sums,
             )
         found.append(sums)
-    return found
+        if j == 0:
+            opposite = blocks[half][0]
+    return found, opposite, device_at(half)
 
 
 def depth_pair(values):
@@ -359,10 +393,22 @@
 
 
 def order_parts(trio, even, n, layers, summed, nx):
-    for part, slab in zip(trio, (1, jnp.where(even, 0, 2), jnp.where(even, 2, 0))):
+    slabs = (1, jnp.where(even, 0, 2), jnp.where(even, 2, 0))
+    for part, slab in zip(trio, slabs):
         for t in range(n):
             at = t * layers * nx
             summed[slab, t] = part[at : at + layers * nx].reshape(layers, nx, -1)
+    return slabs
+
+
+def add_picked(trio, slabs, begin, capacity, targets, layers, summed, table, nx):
+    rows = layers * nx
+    for e in range(capacity):
+        target = lax.rem(table[0, begin + e].astype(jnp.int32), targets)
+        w = table[1, begin + e]
+        for part, slab in zip(trio, slabs):
+            src = part[e * rows : (e + 1) * rows].reshape(layers, nx, -1)
+            summed[slab, target] = summed[slab, target] + w * src
 
 
 def coupled(l, depth, start, layers, coef_dev, summed, mode_face, visit):
@@ -395,20 +441,34 @@
     return True
 
 
-def begin_kernel(coef_dev, depth, layers, space_ref, known, own, other, pair, *refs):
-    rest, mode_face, summed, mode_ext = refs
+def begin_kernel(coef_dev, depth, layers, capacity, n_picked, where, known, own, other, pair, *refs):
+    picked = refs[:n_picked]
+    rest, mode_face, summed, mode_ext, tables, sems = refs[n_picked:]
     nx = known.shape[2]
     targets = coef_dev * M
-    even = lax.rem(space_ref[0], 2) == 0
-    order_parts((own, other, pair), even, targets, layers, summed, nx)
-    for part, slab in zip(
-        (own, other, pair), (1, jnp.where(even, 0, 2), jnp.where(even, 2, 0))
-    ):
+    copies = start_tables(picked[:1], tables, sems)
+    even = lax.rem(where[0], 2) == 0
+    slabs = order_parts((own, other, pair), even, targets, layers, summed, nx)
+    for part, slab in zip((own, other, pair), slabs):
         for k in range(M):
             at = (targets * layers + k * depth) * nx
             mode_ext[k, pl.ds(slab * depth, depth)] = part[at : at + depth * nx].reshape(
                 depth, nx, -1
             )
+    if picked:
+        at = capacity * layers * nx
+        for k in range(M):
+
+            @pl.when(where[2 + k] == where[2 + M])
+            def _(k=k):
+                for part, slab in zip(picked, slabs):
+                    mode_ext[k, pl.ds(slab * depth, depth)] = part[at : at + depth * nx].reshape(
+                        depth, nx, -1
+                    )
+
+        copies[0].wait()
+        begin = where[1] * capacity
+        add_picked(picked, slabs, begin, capacity, targets, layers, summed, tables.at[0], nx)
     last = 3 * depth - 1
 
     def mode_faces(l, carry):
@@ -501,7 +561,7 @@
     assert count * capacity <= ny
     chunks = pack(coeffs, mode_bank, links[0], capacity, rows_of)
 
-    sums = chaos_sums(
+    sums, opposite, opposite_device = chaos_sums(
         chunks, coef_dev, capacity, rows_of, slot_rows, mode_owner
     )
 
@@ -528,22 +588,30 @@
     )(index, coeffs, source, mean_field, other, pair)
 
     parts = [[own, *depth_pair(own)] for own in sums]
+    picked = [] if opposite is None else [opposite, *depth_pair(opposite)]
+    where = jnp.stack(
+        [index[0], lax.axis_index("chaos"), *(mode_owner[k] for k in range(M)), opposite_device]
+    ).astype(jnp.int32)
     layers = layer_counts[0]
     ordered = pltpu.VMEM((3, coef_dev * M, layers, nx, ny), jnp.float32)
     mode_faces = (M, 7, 3 * depth, nx, ny)
     rest, mode_face = pl.pallas_call(
-        functools.partial(begin_kernel, coef_dev, depth, layers),
+        functools.partial(begin_kernel, coef_dev, depth, layers, capacity, len(picked)),
         out_shape=(
             jax.ShapeDtypeStruct(wide, jnp.float32),
             jax.ShapeDtypeStruct(mode_faces, jnp.float32),
         ),
-        in_specs=[SMEM] + [VMEM] * 4,
+        in_specs=[SMEM] + [VMEM] * (4 + len(picked)),
         out_specs=(VMEM, VMEM),
-        scratch_shapes=[ordered, pltpu.VMEM((M, 3 * depth, nx, ny), jnp.float32)],
+        scratch_shapes=[
+            ordered,
+            pltpu.VMEM((M, 3 * depth, nx, ny), jnp.float32),
+            *table_scratch(1, ny),
+        ],
         compiler_params=pltpu.CompilerParams(vmem_limit_bytes=16 << 20),
         cost_estimate=cost(3 * depth * coef_dev, nx, ny, 40),
         name="begin",
-    )(index, known, *parts[0])
+    )(where, known, *parts[0], *picked)
     out = jax.ShapeDtypeStruct(coeffs.shape, jnp.float32)
     return pl.pallas_call(
         functools.partial(sweep_kernel, coef_dev, depth, depth - layers, layers),
@@ -567,6 +635,9 @@
         P("chaos", None, None),
     )
     out_specs = (P("chaos", "space", None, None), P("chaos", "space", None, None))
-    return jax.shard_map(
+    step = jax.shard_map(
         residual_and_correction, mesh=mesh, in_specs=in_specs, out_specs=out_specs, check_vma=False
     )
+    if not unrolled(mesh.shape["chaos"]):
+        return step
+    return step

time: 79.2 us -> 93.5 us (1.18)
  starting transfers between devices: 21.1 us -> 33.8 us
  waiting for transfers between devices: 28.3 us -> 18.9 us
  local copies, waits for them, and re-layouts: 3.09 us -> 7.93 us
  Pallas kernels: 23.1 us -> 27.5 us
    ppermute x14, waiting for transfers between devices: 27.4 us -> 11.6 us  [chaos_sums(): block = lax.ppermute(block, 'chaos', pairs)]
    ppermute x3 -> x4, starting transfers between devices: 11 us -> 20.5 us  [depth_pair(): other = lax.ppermute(values, 'space', second)]
    pallas_call x5 -> x10, Pallas kernels: 10.8 us -> 17.7 us  [the longest x5 8.68 us: sum_blocks(): pl.pallas_call(functools.partial(sum_kernel, picked, coef_dev, capacity,...]
    ppermute x3 -> x4, waiting for transfers between devices: 0.82 us -> 7.33 us  [depth_pair(): other = lax.ppermute(values, 'space', second)]
    unnamed x28 -> x32, local copies, waits for them, and re-layouts: 2.92 us -> 7.03 us
    ppermute x14, starting transfers between devices: 9.94 us -> 13.1 us  [chaos_sums(): block = lax.ppermute(block, 'chaos', pairs)]
    pallas_call x1, Pallas kernels: 3.53 us -> 2.34 us  [residual_and_correction(): pl.pallas_call(functools.partial(base_kernel, coef_dev, depth, n_space),...]
    pallas_call x1, Pallas kernels: 6.01 us -> 4.84 us  [residual_and_correction(): pl.pallas_call(functools.partial(sweep_kernel, coef_dev, depth, depth - l...]
  transfers between devices with their start and end apart: 20 -> 22, of which waited for: 9 -> 6; matrix products, arithmetic and copies ran while one was open for 3% -> 4% of each run, Pallas kernels for 18% -> 22%
where the time goes in v3:
time: 93.5 us; the launch traced here: 92.4 us
  starting transfers between devices  33.8 us (36%)
  Pallas kernels  27.5 us (29%)
  waiting for transfers between devices  18.9 us (20%)
  local copies, waits for them, and re-layouts  7.93 us (8%)
  other arithmetic  3.14 us (3%)
  between operations  1.03 us (1%)
    ppermute x4, starting transfers between devices, depth_pair(): other = lax.ppermute(values, 'space', second)  20.5 us
    ppermute x14, starting transfers between devices, chaos_sums(): block = lax.ppermute(block, 'chaos', pairs)  13.1 us
    ppermute x14, waiting for transfers between devices, chaos_sums(): block = lax.ppermute(block, 'chaos', pairs)  11.6 us
    pallas_call x5, Pallas kernels, sum_blocks(): pl.pallas_call(functools.partial(sum_kernel, picked, coef_dev, capacity,...  8.68 us
    ppermute x4, waiting for transfers between devices, depth_pair(): other = lax.ppermute(values, 'space', second)  7.33 us
    unnamed x32, local copies, waits for them, and re-layouts  7.03 us
    pallas_call x4, Pallas kernels, pick(): pl.pallas_call(functools.partial(pick_kernel, coef_dev, capacity, rows),...  5.25 us
    pallas_call x1, Pallas kernels, residual_and_correction(): pl.pallas_call(functools.partial(sweep_kernel, coef_dev, depth, depth - l...  4.84 us
  transfers between devices with their start and end apart: 22, of which 6 were waited for; matrix products, arithmetic and copies ran while one was open for 4% of the time, Pallas kernels for 22%

profile of v3, /device:TPU:1, one launch (start us, length us, event | category | flops | bytes accessed | tf_op | source)
XLA Modules:
  0.0 92.4 jit_solution(13221674917280273638)
XLA Ops:
  0.6 2.7 %pack.1 = (f32[648,128]{1,0:T(8,128)}, f32[520,128]{1,0:T(8,128)}) custom-call(s32[4,32]{1,0:T(4,128)} %bitcast.23, f32[8,128,128]{2,1,0:T(8,128)} %bitcast.19, f32[1,128,128]{2,1,0:T(8,128)} %bitcast.22), custom_call_target="tpu_custom_call" | custom-call | flops 131072 | bytes 1048576 | tf_op jit(solution)/shard_map/pack/pallas_call | solution.py:119
  3.3 2.1 %collective-permute-start.13 = (f32[520,128]{1,0:T(8,128)}, f32[520,128]{1,0:T(8,128)S(1)}, u32[]{:S(2)}, u32[]{:S(2)}) collective-permute-start(f32[520,128]{1,0:T(8,128)} %get-tuple-element.13.refs_0_), channel_id=1, source_target_pairs={{8,0},{16,8},{24,16},{28,24},{20,28},{12,20},{4,12},{0,4},{9,1},{1... | collective-permute-start | bytes 798728 | tf_op jit(solution)/shard_map/ppermute | solution.py:295
  5.5 1.3 %collective-permute-start.2 = (f32[648,128]{1,0:T(8,128)}, f32[648,128]{1,0:T(8,128)S(1)}, u32[]{:S(2)}, u32[]{:S(2)}) collective-permute-start(f32[648,128]{1,0:T(8,128)} %get-tuple-element.9.refs_0_), channel_id=1, source_target_pairs={{8,0},{16,8},{24,16},{28,24},{20,28},{12,20},{4,12},{0,4},{9,1},{1... | collective-permute-start | bytes 995336 | tf_op jit(solution)/shard_map/ppermute | solution.py:295
  7.0 2.3 %pad_maximum_fusion = f32[68,32,128]{2,1,0:T(8,128)} fusion(f32[4,32,128]{2,1,0:T(8,128)} %mean.1, f32[32,32,128]{2,1,0:T(8,128)} %bitcast.21, f32[32,32,128]{2,1,0:T(8,128)} %bitcast.20), kind=kLoop, calls=%fused_computation | loop fusion | flops 557056 | bytes 2228224 | tf_op jit(solution)/shard_map/concatenate | solution.py:568
  9.3 4.9 %collective-permute-start = (f32[68,32,128]{2,1,0:T(8,128)}, f32[68,32,128]{2,1,0:T(8,128)S(1)}, u32[]{:S(2)}, u32[]{:S(2)}) collective-permute-start(f32[68,32,128]{2,1,0:T(8,128)} %pad_maximum_fusion), channel_id=1, source_target_pairs={{1,2},{2,1},{5,6},{6,5},{9,10},{10,9},{13,14},{14,13},{17,18},{18,... | collective-permute-start | bytes 3342344 | tf_op jit(solution)/shard_map/ppermute | solution.py:324
  14.4 1.3 %collective-permute-start.6 = (f32[648,128]{1,0:T(8,128)S(1)}, f32[648,128]{1,0:T(8,128)}, u32[]{:S(2)}, u32[]{:S(2)}) collective-permute-start(f32[648,128]{1,0:T(8,128)S(1)} %collective-permute-done.5.refs_2_), channel_id=1, source_target_pairs={{0,8},{8,16},{16,24},{24,28},{28,20},{20,12},{12,4},{4,0},{1,9},{9... | collective-permute-start | bytes 995336 | tf_op jit(solution)/shard_map/ppermute | solution.py:295
  16.4 3.4 %collective-permute-done.17.refs_2_ = f32[520,128]{1,0:T(8,128)} collective-permute-done((f32[520,128]{1,0:T(8,128)}, f32[520,128]{1,0:T(8,128)}, u32[]{:S(2)}, u32[]{:S(2)}) %collective-permute-start.17) | collective-permute-done | bytes 266272 | tf_op jit(solution)/shard_map/ppermute | solution.py:295
  23.8 1.6 %collective-permute-done.14.refs_0_ = f32[520,128]{1,0:T(8,128)} collective-permute-done((f32[520,128]{1,0:T(8,128)S(1)}, f32[520,128]{1,0:T(8,128)}, u32[]{:S(2)}, u32[]{:S(2)}) %collective-permute-start.14) | collective-permute-done | bytes 266272 | tf_op jit(solution)/shard_map/ppermute | solution.py:295
  27.3 4.4 %collective-permute-done.3.block.refs_0_ = f32[648,128]{1,0:T(8,128)S(1)} collective-permute-done((f32[648,128]{1,0:T(8,128)S(1)}, f32[648,128]{1,0:T(8,128)S(1)}, u32[]{:S(2)}, u32[]{:S(2)}) %collective-permute-start.3) | collective-permute-done | bytes 331808 | tf_op jit(solution)/shard_map/ppermute | solution.py:295
  34.4 1.3 %collective-permute-start.4 = (f32[456,128]{1,0:T(8,128)}, f32[456,128]{1,0:T(8,128)}, u32[]{:S(2)}, u32[]{:S(2)}) collective-permute-start(f32[456,128]{1,0:T(8,128)} %pick.4), channel_id=1, source_target_pairs={{8,0},{16,8},{24,16},{28,24},{20,28},{12,20},{4,12},{0,4},{9,1},{1... | collective-permute-start | bytes 700424 | tf_op jit(solution)/shard_map/ppermute | solution.py:295
  38.6 1.3 %pick.6 = f32[328,128]{1,0:T(8,128)} custom-call(s32[1]{0:T(128)} %bitcast.13.begin, f32[520,128]{1,0:T(8,128)S(1)} %collective-permute-done.15.block.refs_0_), custom_call_target="tpu_custom_call" | custom-call | flops 40960 | bytes 327680 | tf_op jit(solution)/shard_map/pick/pallas_call | solution.py:156
  41.0 1.3 %pick.5 = f32[456,128]{1,0:T(8,128)} custom-call(s32[1]{0:T(128)} %bitcast.17.begin, f32[648,128]{1,0:T(8,128)S(1)} %collective-permute-done.7.refs_2_.block), custom_call_target="tpu_custom_call" | custom-call | flops 40960 | bytes 327680 | tf_op jit(solution)/shard_map/pick/pallas_call | solution.py:156
  46.0 1.3 %shard_map.77.refs_4_ = f32[1280,128]{1,0:T(8,128)S(1)} custom-call(s32[6]{0:T(128)S(1)} %stack.67.where, f32[648,128]{1,0:T(8,128)S(1)} %copy-done.6, f32[648,128]{1,0:T(8,128)S(1)} %copy-done.10, f32[648,128]{1,0:T(8,128)S(1)} %copy-done.8), custom_call_target="tpu_custom_call" | custom-call | flops 524288 | bytes 1048576 | tf_op jit(solution)/shard_map/pallas_call | solution.py:203
  47.3 2.0 %shard_map.78.own = f32[1280,128]{1,0:T(8,128)S(1)} custom-call(s32[7]{0:T(128)S(1)} %stack.63.where, f32[648,128]{1,0:T(8,128)S(1)} %collective-permute-done.3.block.refs_0_, f32[456,128]{1,0:T(8,128)} %collective-permute-done.4.refs_1_, f32[648,128]{1,0:T(8,128)S(1)} %collective-permute-done.7.refs_2_.block, f32[648,128]{1,0:T(8,128)} %collective-permute-done.6.refs_3_, ...), custom_call_target="tpu_custom_call" | custom-call | flops 524288 | bytes 1048576 | tf_op jit(solution)/shard_map/pallas_call | solution.py:203
  49.3 10.0 %collective-permute-start.8 = (f32[1280,128]{1,0:T(8,128)S(1)}, f32[1280,128]{1,0:T(8,128)}, u32[]{:S(2)}, u32[]{:S(2)}) collective-permute-start(f32[1280,128]{1,0:T(8,128)S(1)} %shard_map.78.own), channel_id=1, source_target_pairs={{1,2},{2,1},{5,6},{6,5},{9,10},{10,9},{13,14},{14,13},{17,18},{18,... | collective-permute-start | bytes 1966088 | tf_op jit(solution)/shard_map/ppermute | solution.py:324
  62.9 1.8 %shard_map.79.refs_2_ = f32[1024,128]{1,0:T(8,128)S(1)} custom-call(s32[6]{0:T(128)S(1)} %stack.67.where, f32[520,128]{1,0:T(8,128)S(1)} %copy-done.11, f32[520,128]{1,0:T(8,128)S(1)} %copy-done.13, f32[520,128]{1,0:T(8,128)} %collective-permute-done.17.refs_2_), custom_call_target="tpu_custom_call" | custom-call | flops 524288 | bytes 1048576 | tf_op jit(solution)/shard_map/pallas_call | solution.py:203
  64.7 1.7 %shard_map.80.refs_3_ = f32[1024,128]{1,0:T(8,128)S(1)} custom-call(s32[5]{0:T(128)S(1)} %get-tuple-element.14.where, f32[520,128]{1,0:T(8,128)} %collective-permute-done.14.refs_0_, f32[520,128]{1,0:T(8,128)S(1)} %copy-done.3, f32[1024,128]{1,0:T(8,128)S(1)} %shard_map.79.refs_2_), custom_call_target="tpu_custom_call" | custom-call | flops 524288 | bytes 1048576 | tf_op jit(solution)/shard_map/pallas_call | solution.py:203
  66.4 1.9 %shard_map.81.refs_0_ = f32[1024,128]{1,0:T(8,128)S(1)} custom-call(s32[6]{0:T(128)S(1)} %stack.68.where, f32[520,128]{1,0:T(8,128)S(1)} %copy-done.5, f32[328,128]{1,0:T(8,128)} %collective-permute-done.16.refs_1_, f32[328,128]{1,0:T(8,128)} %collective-permute-done.19.refs_2_, f32[1024,128]{1,0:T(8,128)S(1)} %shard_map.80.refs_3_), custom_call_target="tpu_custom_call" | custom-call | flops 524288 | bytes 1048576 | tf_op jit(solution)/shard_map/pallas_call | solution.py:203
  68.3 1.9 %collective-permute-start.20 = (f32[1024,128]{1,0:T(8,128)S(1)}, f32[1024,128]{1,0:T(8,128)S(1)}, u32[]{:S(2)}, u32[]{:S(2)}) collective-permute-start(f32[1024,128]{1,0:T(8,128)S(1)} %shard_map.81.refs_0_), channel_id=1, source_target_pairs={{1,2},{2,1},{5,6},{6,5},{9,10},{10,9},{13,14},{14,13},{17,18},{18,... | collective-permute-start | bytes 1572872 | tf_op jit(solution)/shard_map/ppermute | solution.py:324
  70.4 3.6 %collective-permute-start.11 = (f32[456,128]{1,0:T(8,128)}, f32[456,128]{1,0:T(8,128)S(1)}, u32[]{:S(2)}, u32[]{:S(2)}) collective-permute-start(f32[456,128]{1,0:T(8,128)} %collective-permute-done.10.refs_0_), channel_id=1, source_target_pairs={{1,2},{2,1},{5,6},{6,5},{9,10},{10,9},{13,14},{14,13},{17,18},{18,... | collective-permute-start | bytes 700424 | tf_op jit(solution)/shard_map/ppermute | solution.py:324
  74.0 7.3 %collective-permute-done.11.refs_1_ = f32[456,128]{1,0:T(8,128)S(1)} collective-permute-done((f32[456,128]{1,0:T(8,128)}, f32[456,128]{1,0:T(8,128)S(1)}, u32[]{:S(2)}, u32[]{:S(2)}) %collective-permute-start.11) | collective-permute-done | bytes 233504 | tf_op jit(solution)/shard_map/ppermute | solution.py:324
  81.4 2.3 %base.1 = (f32[8,12,32,128]{3,2,1,0:T(8,128)S(1)}, f32[7,12,32,128]{3,2,1,0:T(8,128)S(1)}) custom-call(s32[1]{0:T(128)} %bitcast.space_ref, f32[8,4,32,128]{3,2,1,0:T(8,128)S(1)} %copy-done, f32[8,4,32,128]{3,2,1,0:T(8,128)S(1)} %copy-done.1, f32[4,32,128]{2,1,0:T(8,128)S(1)} %copy-done.14, f32[68,32,128]{2,1,0:T(8,128)S(1)} %collective-permute-done.refs_0_, ...), custom_call_target="tpu_custom_call" | custom-call | flops 7864320 | bytes 3145728 | tf_op jit(solution)/shard_map/base/pallas_call | solution.py:573
  83.7 3.8 %begin.1 = (f32[8,12,32,128]{3,2,1,0:T(8,128)S(1)}, f32[2,7,12,32,128]{4,3,2,1,0:T(8,128)S(1)}) custom-call(s32[5]{0:T(128)S(1)} %get-tuple-element.15.where, f32[8,12,32,128]{3,2,1,0:T(8,128)S(1)} %get-tuple-element.8.known, f32[1280,128]{1,0:T(8,128)S(1)} %shard_map.78.own, f32[1280,128]{1,0:T(8,128)} %collective-permute-done.8.other, ...), custom_call_target="tpu_custom_call" | custom-call | flops 15728640 | bytes 3145728 | tf_op jit(solution)/shard_map/begin/pallas_call | solution.py:598
  87.6 4.8 %sweeps.1 = (f32[8,4,32,128]{3,2,1,0:T(8,128)}, f32[8,4,32,128]{3,2,1,0:T(8,128)}) custom-call(s32[1]{0:T(128)} %bitcast.space_ref, f32[8,12,32,128]{3,2,1,0:T(8,128)S(1)} %get-tuple-element.10.rest, f32[2,7,12,32,128]{4,3,2,1,0:T(8,128)S(1)} %get-tuple-element.11.mode_face, f32[7,12,32,128]{3,2,1,0:T(8,128)S(1)} %get-tuple-element.12.face, ...), custom_call_target="tpu_custom_call" | custom-call | flops 31457280 | bytes 6291456 | tf_op jit(solution)/shard_map/sweeps/pallas_call | solution.py:616
  (70 shorter events, 20.8 us)
Async XLA Ops:
  3.3 11.0 %collective-permute-start.13 = (f32[520,128]{1,0:T(8,128)}, f32[520,128]{1,0:T(8,128)S(1)}, u32[]{:S(2)}, u32[]{:S(2)}) collective-permute-start(f32[520,128]{1,0:T(8,128)} %get-tuple-element.13.refs_0_), channel_id=1, source_target_pairs={{8,0},{16,8},{24,16},{28,24},{20,28},{12,20},{4,12},{0,4},{9,1},{1... | collective-permute-start | bytes 798728 | tf_op jit(solution)/shard_map/ppermute | solution.py:295
  5.4 9.0 %collective-permute-start.5 = (f32[648,128]{1,0:T(8,128)}, f32[648,128]{1,0:T(8,128)S(1)}, u32[]{:S(2)}, u32[]{:S(2)}) collective-permute-start(f32[648,128]{1,0:T(8,128)} %get-tuple-element.9.refs_0_), channel_id=1, source_target_pairs={{0,8},{8,16},{16,24},{24,28},{28,20},{20,12},{12,4},{4,0},{1,9},{9... | collective-permute-start | bytes 995336 | tf_op jit(solution)/shard_map/ppermute | solution.py:295
  5.5 16.3 %collective-permute-start.2 = (f32[648,128]{1,0:T(8,128)}, f32[648,128]{1,0:T(8,128)S(1)}, u32[]{:S(2)}, u32[]{:S(2)}) collective-permute-start(f32[648,128]{1,0:T(8,128)} %get-tuple-element.9.refs_0_), channel_id=1, source_target_pairs={{8,0},{16,8},{24,16},{28,24},{20,28},{12,20},{4,12},{0,4},{9,1},{1... | collective-permute-start | bytes 995336 | tf_op jit(solution)/shard_map/ppermute | solution.py:295
  6.8 13.0 %collective-permute-start.17 = (f32[520,128]{1,0:T(8,128)}, f32[520,128]{1,0:T(8,128)}, u32[]{:S(2)}, u32[]{:S(2)}) collective-permute-start(f32[520,128]{1,0:T(8,128)} %get-tuple-element.13.refs_0_), channel_id=1, source_target_pairs={{0,8},{8,16},{16,24},{24,28},{28,20},{20,12},{12,4},{4,0},{1,9},{9... | collective-permute-start | bytes 798728 | tf_op jit(solution)/shard_map/ppermute | solution.py:295
  9.3 59.0 %collective-permute-start = (f32[68,32,128]{2,1,0:T(8,128)}, f32[68,32,128]{2,1,0:T(8,128)S(1)}, u32[]{:S(2)}, u32[]{:S(2)}) collective-permute-start(f32[68,32,128]{2,1,0:T(8,128)} %pad_maximum_fusion), channel_id=1, source_target_pairs={{1,2},{2,1},{5,6},{6,5},{9,10},{10,9},{13,14},{14,13},{17,18},{18,... | collective-permute-start | bytes 3342344 | tf_op jit(solution)/shard_map/ppermute | solution.py:324
  14.3 56.0 %collective-permute-start.1 = (f32[68,32,128]{2,1,0:T(8,128)}, f32[68,32,128]{2,1,0:T(8,128)S(1)}, u32[]{:S(2)}, u32[]{:S(2)}) collective-permute-start(f32[68,32,128]{2,1,0:T(8,128)} %pad_maximum_fusion), channel_id=1, source_target_pairs={{0,1},{1,0},{2,3},{3,2},{4,5},{5,4},{6,7},{7,6},{8,9},{9,8},{10,11... | collective-permute-start | bytes 3342344 | tf_op jit(solution)/shard_map/ppermute | solution.py:325
  14.4 12.6 %collective-permute-start.6 = (f32[648,128]{1,0:T(8,128)S(1)}, f32[648,128]{1,0:T(8,128)}, u32[]{:S(2)}, u32[]{:S(2)}) collective-permute-start(f32[648,128]{1,0:T(8,128)S(1)} %collective-permute-done.5.refs_2_), channel_id=1, source_target_pairs={{0,8},{8,16},{16,24},{24,28},{28,20},{20,12},{12,4},{4,0},{1,9},{9... | collective-permute-start | bytes 995336 | tf_op jit(solution)/shard_map/ppermute | solution.py:295
  19.8 5.7 %collective-permute-start.14 = (f32[520,128]{1,0:T(8,128)S(1)}, f32[520,128]{1,0:T(8,128)}, u32[]{:S(2)}, u32[]{:S(2)}) collective-permute-start(f32[520,128]{1,0:T(8,128)S(1)} %collective-permute-done.13.refs_1_), channel_id=1, source_target_pairs={{8,0},{16,8},{24,16},{28,24},{20,28},{12,20},{4,12},{0,4},{9,1},{1... | collective-permute-start | bytes 798728 | tf_op jit(solution)/shard_map/ppermute | solution.py:295
  21.8 9.9 %collective-permute-start.3 = (f32[648,128]{1,0:T(8,128)S(1)}, f32[648,128]{1,0:T(8,128)S(1)}, u32[]{:S(2)}, u32[]{:S(2)}) collective-permute-start(f32[648,128]{1,0:T(8,128)S(1)} %collective-permute-done.2.refs_1_), channel_id=1, source_target_pairs={{8,0},{16,8},{24,16},{28,24},{20,28},{12,20},{4,12},{0,4},{9,1},{1... | collective-permute-start | bytes 995336 | tf_op jit(solution)/shard_map/ppermute | solution.py:295
  25.5 8.9 %collective-permute-start.18 = (f32[520,128]{1,0:T(8,128)}, f32[520,128]{1,0:T(8,128)S(1)}, u32[]{:S(2)}, u32[]{:S(2)}) collective-permute-start(f32[520,128]{1,0:T(8,128)} %collective-permute-done.17.refs_2_), channel_id=1, source_target_pairs={{0,8},{8,16},{16,24},{24,28},{28,20},{20,12},{12,4},{4,0},{1,9},{9... | collective-permute-start | bytes 798728 | tf_op jit(solution)/shard_map/ppermute | solution.py:295
  26.9 13.0 %collective-permute-start.7 = (f32[648,128]{1,0:T(8,128)}, f32[648,128]{1,0:T(8,128)S(1)}, u32[]{:S(2)}, u32[]{:S(2)}) collective-permute-start(f32[648,128]{1,0:T(8,128)} %collective-permute-done.6.refs_3_), channel_id=1, source_target_pairs={{0,8},{8,16},{16,24},{24,28},{28,20},{20,12},{12,4},{4,0},{1,9},{9... | collective-permute-start | bytes 995336 | tf_op jit(solution)/shard_map/ppermute | solution.py:295
  31.7 6.4 %collective-permute-start.15 = (f32[520,128]{1,0:T(8,128)}, f32[520,128]{1,0:T(8,128)S(1)}, u32[]{:S(2)}, u32[]{:S(2)}) collective-permute-start(f32[520,128]{1,0:T(8,128)} %collective-permute-done.14.refs_0_), channel_id=1, source_target_pairs={{8,0},{16,8},{24,16},{28,24},{20,28},{12,20},{4,12},{0,4},{9,1},{1... | collective-permute-start | bytes 798728 | tf_op jit(solution)/shard_map/ppermute | solution.py:295
  34.4 8.0 %collective-permute-start.4 = (f32[456,128]{1,0:T(8,128)}, f32[456,128]{1,0:T(8,128)}, u32[]{:S(2)}, u32[]{:S(2)}) collective-permute-start(f32[456,128]{1,0:T(8,128)} %pick.4), channel_id=1, source_target_pairs={{8,0},{16,8},{24,16},{28,24},{20,28},{12,20},{4,12},{0,4},{9,1},{1... | collective-permute-start | bytes 700424 | tf_op jit(solution)/shard_map/ppermute | solution.py:295
  38.2 11.1 %collective-permute-start.19 = (f32[328,128]{1,0:T(8,128)}, f32[328,128]{1,0:T(8,128)}, u32[]{:S(2)}, u32[]{:S(2)}) collective-permute-start(f32[328,128]{1,0:T(8,128)} %pick.7), channel_id=1, source_target_pairs={{0,8},{8,16},{16,24},{24,28},{28,20},{20,12},{12,4},{4,0},{1,9},{9... | collective-permute-start | bytes 503816 | tf_op jit(solution)/shard_map/ppermute | solution.py:295
  40.0 19.4 %collective-permute-start.16 = (f32[328,128]{1,0:T(8,128)}, f32[328,128]{1,0:T(8,128)}, u32[]{:S(2)}, u32[]{:S(2)}) collective-permute-start(f32[328,128]{1,0:T(8,128)} %pick.6), channel_id=1, source_target_pairs={{8,0},{16,8},{24,16},{28,24},{20,28},{12,20},{4,12},{0,4},{9,1},{1... | collective-permute-start | bytes 503816 | tf_op jit(solution)/shard_map/ppermute | solution.py:295
  42.4 28.0 %collective-permute-start.10 = (f32[456,128]{1,0:T(8,128)}, f32[456,128]{1,0:T(8,128)}, u32[]{:S(2)}, u32[]{:S(2)}) collective-permute-start(f32[456,128]{1,0:T(8,128)} %pick.5), channel_id=1, source_target_pairs={{0,8},{8,16},{16,24},{24,28},{28,20},{20,12},{12,4},{4,0},{1,9},{9... | collective-permute-start | bytes 700424 | tf_op jit(solution)/shard_map/ppermute | solution.py:295
  49.3 15.4 %copy-start.3 = (f32[520,128]{1,0:T(8,128)S(1)}, f32[520,128]{1,0:T(8,128)}, u32[]{:S(2)}) copy-start(f32[520,128]{1,0:T(8,128)} %copy-done.2) | copy-start | bytes 798724
  49.3 34.4 %collective-permute-start.8 = (f32[1280,128]{1,0:T(8,128)S(1)}, f32[1280,128]{1,0:T(8,128)}, u32[]{:S(2)}, u32[]{:S(2)}) collective-permute-start(f32[1280,128]{1,0:T(8,128)S(1)} %shard_map.78.own), channel_id=1, source_target_pairs={{1,2},{2,1},{5,6},{6,5},{9,10},{10,9},{13,14},{14,13},{17,18},{18,... | collective-permute-start | bytes 1966088 | tf_op jit(solution)/shard_map/ppermute | solution.py:324
  59.3 24.4 %collective-permute-start.9 = (f32[1280,128]{1,0:T(8,128)S(1)}, f32[1280,128]{1,0:T(8,128)}, u32[]{:S(2)}, u32[]{:S(2)}) collective-permute-start(f32[1280,128]{1,0:T(8,128)S(1)} %shard_map.78.own), channel_id=1, source_target_pairs={{0,1},{1,0},{2,3},{3,2},{4,5},{5,4},{6,7},{7,6},{8,9},{9,8},{10,11... | collective-permute-start | bytes 1966088 | tf_op jit(solution)/shard_map/ppermute | solution.py:325
  66.4 14.9 %copy-start = (f32[8,4,32,128]{3,2,1,0:T(8,128)S(1)}, f32[8,4,32,128]{3,2,1,0:T(8,128)}, u32[]{:S(2)}) copy-start(f32[8,4,32,128]{3,2,1,0:T(8,128)} %coeffs.1) | copy-start | bytes 1572868
  68.3 19.2 %collective-permute-start.20 = (f32[1024,128]{1,0:T(8,128)S(1)}, f32[1024,128]{1,0:T(8,128)S(1)}, u32[]{:S(2)}, u32[]{:S(2)}) collective-permute-start(f32[1024,128]{1,0:T(8,128)S(1)} %shard_map.81.refs_0_), channel_id=1, source_target_pairs={{1,2},{2,1},{5,6},{6,5},{9,10},{10,9},{13,14},{14,13},{17,18},{18,... | collective-permute-start | bytes 1572872 | tf_op jit(solution)/shard_map/ppermute | solution.py:324
  70.3 17.3 %collective-permute-start.21 = (f32[1024,128]{1,0:T(8,128)S(1)}, f32[1024,128]{1,0:T(8,128)S(1)}, u32[]{:S(2)}, u32[]{:S(2)}) collective-permute-start(f32[1024,128]{1,0:T(8,128)S(1)} %shard_map.81.refs_0_), channel_id=1, source_target_pairs={{0,1},{1,0},{2,3},{3,2},{4,5},{5,4},{6,7},{7,6},{8,9},{9,8},{10,11... | collective-permute-start | bytes 1572872 | tf_op jit(solution)/shard_map/ppermute | solution.py:325
  70.4 11.0 %collective-permute-start.11 = (f32[456,128]{1,0:T(8,128)}, f32[456,128]{1,0:T(8,128)S(1)}, u32[]{:S(2)}, u32[]{:S(2)}) collective-permute-start(f32[456,128]{1,0:T(8,128)} %collective-permute-done.10.refs_0_), channel_id=1, source_target_pairs={{1,2},{2,1},{5,6},{6,5},{9,10},{10,9},{13,14},{14,13},{17,18},{18,... | collective-permute-start | bytes 700424 | tf_op jit(solution)/shard_map/ppermute | solution.py:324
  81.3 2.4 %collective-permute-start.12 = (f32[456,128]{1,0:T(8,128)}, f32[456,128]{1,0:T(8,128)S(1)}, u32[]{:S(2)}, u32[]{:S(2)}) collective-permute-start(f32[456,128]{1,0:T(8,128)} %collective-permute-done.10.refs_0_), channel_id=1, source_target_pairs={{0,1},{1,0},{2,3},{3,2},{4,5},{5,4},{6,7},{7,6},{8,9},{9,8},{10,11... | collective-permute-start | bytes 700424 | tf_op jit(solution)/shard_map/ppermute | solution.py:325
  (14 other events, 61.9 us)

commit v4 on v3

--- a/solution.py
+++ b/solution.py
@@ -159,7 +159,7 @@
         in_specs=[SMEM, VMEM],
         out_specs=VMEM,
         scratch_shapes=table_scratch(1, lanes),
-        compiler_params=pltpu.CompilerParams(vmem_limit_bytes=8 << 20),
+        compiler_params=pltpu.CompilerParams(vmem_limit_bytes=2 << 20),
         cost_estimate=cost(capacity, rows, lanes, 1),
         name="pick",
     )((device * capacity).astype(jnp.int32).reshape(1), block)
@@ -206,7 +206,7 @@
         in_specs=[SMEM] + [VMEM] * (n + more),
         out_specs=VMEM,
         scratch_shapes=table_scratch(n, lanes),
-        compiler_params=pltpu.CompilerParams(vmem_limit_bytes=12 << 20),
+        compiler_params=pltpu.CompilerParams(vmem_limit_bytes=5 << 20),
         cost_estimate=cost(coef_dev * M, rows, lanes, 4),
     )(where, *blocks, *([so_far] if more else []))
 
@@ -244,10 +244,10 @@
 
 def sum_parts(count, chunk):
     half = count // 2
-    middle = list(range(2, half - 1))
+    middle, last = list(range(2, half - 1)), [half - 1, half]
     if chunk == 0:
-        return {"a": [0, 1], "b": middle + [half - 1]}
-    return {"a": [0, 1], "b": middle, "c": [half - 1, half]}
+        return {"a": [0, 1], "c": middle + last}
+    return {"a": [0, 1], "b": middle, "c": last}
 
 
 def chaos_sums(chunks, coef_dev, capacity, rows_of, slot_rows, mode_owner):
@@ -271,8 +271,7 @@
             blocks = [lax.ppermute(b, "chaos", ring) for b in blocks]
             return blocks, jax.tree.map(jnp.add, sums, at_step(step, blocks))
 
-        found = lax.fori_loop(1, count, body, (list(chunks), at_step(0, chunks)))[1]
-        return found, None, jnp.int32(-1)
+        return lax.fori_loop(1, count, body, (list(chunks), at_step(0, chunks)))[1]
 
     order = ring_order(count)
     there = [(order[i], order[(i + 1) % count]) for i in range(count)]
@@ -284,7 +283,7 @@
         q = (place + shift) % count
         return jnp.where(q < half, 2 * q, 2 * (count - 1 - q) + 1)
 
-    found, opposite = [], None
+    found = []
     for j, (chunk, steps) in enumerate(zip(chunks, ring_steps(count))):
         blocks = {0: (chunk, False)}
         for pairs, sign, n_steps in ((there, -1, steps[0]), (back, 1, steps[1])):
@@ -307,12 +306,10 @@
                 sums,
             )
         found.append(sums)
-        if j == 0:
-            opposite = blocks[half][0]
-    return found, opposite, device_at(half)
-
-
-def depth_pair(values):
+    return found
+
+
+def depth_pair(to_other, to_pair):
     count = lax.axis_size("space")
     first = [(i, i ^ 1) for i in range(count) if i ^ 1 < count]
     second = [
@@ -321,8 +318,8 @@
         for j in [i - 1 if i % 2 == 0 else i + 1]
         if 0 <= j < count
     ]
-    other = lax.ppermute(values, "space", second)
-    pair = lax.ppermute(values, "space", first)
+    other = lax.ppermute(to_other, "space", second)
+    pair = lax.ppermute(to_pair, "space", first)
     return other, pair
 
 
@@ -330,53 +327,34 @@
     other, pair, known, face, coef_ext, mean_ext = refs
     index = space_ref[0]
     even = lax.rem(index, 2) == 0
-    pair_at = jnp.where(even, 2 * depth, 0)
-    other_at = jnp.where(even, 0, 2 * depth)
-    total_layers = 3 * depth
-    planes = coef_dev * depth
-
-    for at, part in ((pair_at, pair), (other_at, other)):
+    for part, below in ((pair, jnp.logical_not(even)), (other, even)):
+        at = jnp.where(below, 0, 2 * depth)
+        edge = jnp.where(below, 1, 0)
         for c in range(coef_dev):
-            coef_ext[c, pl.ds(at, depth)] = part[c * depth : (c + 1) * depth]
-        mean_ext[pl.ds(at, depth)] = part[2 * planes : 2 * planes + depth]
+            coef_ext[c, jnp.where(below, 0, depth + 1)] = part[2 * c + edge]
+        mean_ext[pl.ds(at, depth)] = part[2 * coef_dev : 2 * coef_dev + depth]
     for c in range(coef_dev):
-        coef_ext[c, depth : 2 * depth] = coeffs[c]
+        coef_ext[c, 1 : depth + 1] = coeffs[c]
     mean_ext[depth : 2 * depth] = mean[...]
 
-    def layer(l, source_of):
+    def layer(l, own):
         xm, xp, ym, yp, down, up, total = faces(mean_ext[l - 1], mean_ext[l], mean_ext[l + 1])
         diagonal = REACTION + total
         absolute = index * depth + l - depth
         inside = (absolute >= 0) & (absolute < n_space * depth)
-        face[0, l], face[1, l], face[2, l], face[3, l] = xm, xp, ym, yp
-        face[4, l], face[5, l] = down, up
-        face[6, l] = jnp.where(inside, 1.0 / diagonal, 0.0)
-
-        def coefficient(c, carry):
-            v = coef_ext[c, l]
-            spread = lateral(xm * v, xp * v, ym * v, yp * v)
-            spread = spread + down * coef_ext[c, l - 1] + up * coef_ext[c, l + 1]
-            known[c, l] = source_of(c) - (diagonal * v - spread)
-            return carry
-
-        for c in range(coef_dev):
-            coefficient(c, 0)
-
-    def from_part(part, at):
-        def body(l, carry):
-            layer(l, lambda c: part[planes + c * depth + l - at])
-            return carry
-
-        lax.fori_loop(jnp.maximum(at, 1), jnp.minimum(at + depth, total_layers - 1), body, 0)
-
-    from_part(pair, pair_at)
-    from_part(other, other_at)
-
-    def body(l, carry):
-        layer(l, lambda c: source[c, l - depth])
-        return carry
-
-    lax.fori_loop(depth, 2 * depth, body, 0)
+        inverse = jnp.where(inside, 1.0 / diagonal, 0.0)
+        for i, value in enumerate((xm, xp, ym, yp, down, up)):
+            face[i, l] = value * inverse
+        face[6, l] = inverse
+        if own:
+            at = l - depth
+            for c in range(coef_dev):
+                v = coef_ext[c, at + 1]
+                spread = lateral(xm * v, xp * v, ym * v, yp * v)
+                spread = spread + down * coef_ext[c, at] + up * coef_ext[c, at + 2]
+                known[c, at] = source[c, at] - (diagonal * v - spread)
+
+    over_layers(layer, depth, ITERS - 1)
 
 
 def sweep_constants():
@@ -392,34 +370,17 @@
     return midpoint, steps
 
 
-def order_parts(trio, even, n, layers, summed, nx):
-    slabs = (1, jnp.where(even, 0, 2), jnp.where(even, 2, 0))
-    for part, slab in zip(trio, slabs):
-        for t in range(n):
-            at = t * layers * nx
-            summed[slab, t] = part[at : at + layers * nx].reshape(layers, nx, -1)
-    return slabs
-
-
-def add_picked(trio, slabs, begin, capacity, targets, layers, summed, table, nx):
-    rows = layers * nx
-    for e in range(capacity):
-        target = lax.rem(table[0, begin + e].astype(jnp.int32), targets)
-        w = table[1, begin + e]
-        for part, slab in zip(trio, slabs):
-            src = part[e * rows : (e + 1) * rows].reshape(layers, nx, -1)
-            summed[slab, target] = summed[slab, target] + w * src
-
-
-def coupled(l, depth, start, layers, coef_dev, summed, mode_face, visit):
-    slab, at = divmod(l, depth)
-    near = {}
-    for offset in (-1, 0, 1):
-        s, i = divmod(l + offset, depth)
-        if 0 <= s < 3 and start <= i < start + layers:
-            near[offset] = (s, i - start)
-    if not near:
-        return False
+def plane(sums, layers, nx, target, l):
+    at = (target * layers + l % layers) * nx
+    return sums[l // layers][at : at + nx, :]
+
+
+def mode_plane(sums, layers, depth, nx, targets, k, l):
+    at = (targets * layers + k * depth + l) * nx
+    return sums[0][at : at + nx, :]
+
+
+def coupled(l, inside, coef_dev, read, mode_face, visit):
     for c in range(coef_dev):
         to, rest = [None] * 4, None
 
@@ -427,104 +388,159 @@
             return term if total is None else total + term
 
         for k in range(M):
-            if 0 in near:
-                s, i = near[0]
-                v = summed[s, c * M + k, i]
+            target = c * M + k
+            if l in inside:
+                v = read(target, l)
                 for q in range(4):
                     to[q] = add(to[q], mode_face[k, q, l] * v)
-                rest = add(rest, -(mode_face[k, 6, l] * v))
-            for offset, which in ((-1, 4), (1, 5)):
-                if offset in near:
-                    s, i = near[offset]
-                    rest = add(rest, mode_face[k, which, l] * summed[s, c * M + k, i])
-        visit(c, rest + lateral(*to) if 0 in near else rest)
-    return True
-
-
-def begin_kernel(coef_dev, depth, layers, capacity, n_picked, where, known, own, other, pair, *refs):
-    picked = refs[:n_picked]
-    rest, mode_face, summed, mode_ext, tables, sems = refs[n_picked:]
-    nx = known.shape[2]
+                rest = add(rest, mode_face[k, 6, l] * v)
+            for near, which in ((l - 1, 4), (l + 1, 5)):
+                if near in inside:
+                    rest = add(rest, mode_face[k, which, l] * read(target, near))
+        if rest is not None:
+            visit(c, rest + lateral(*to) if l in inside else rest)
+
+
+def begin_kernel(coef_dev, depth, layers, sums, rest, mode_face):
+    nx = rest.shape[2]
     targets = coef_dev * M
-    copies = start_tables(picked[:1], tables, sems)
-    even = lax.rem(where[0], 2) == 0
-    slabs = order_parts((own, other, pair), even, targets, layers, summed, nx)
-    for part, slab in zip((own, other, pair), slabs):
+    for k in range(M):
+        own = [mode_plane([sums], layers, depth, nx, targets, k, l) for l in range(depth)]
+        for l in range(depth):
+            below = own[l - 1] if l > 0 else -own[l]
+            above = own[l + 1] if l + 1 < depth else -own[l]
+            *got, total = faces(below, own[l], above)
+            for i, value in enumerate((*got, -total)):
+                mode_face[k, i, l] = value
+    for l in range(depth):
+        if l > layers:
+            for c in range(coef_dev):
+                rest[c, l] = jnp.zeros_like(rest[c, l])
+
+        def visit(c, value, l=l):
+            rest[c, l] = value
+
+        coupled(
+            l, range(layers), coef_dev,
+            lambda target, at: plane([sums], layers, nx, target, at), mode_face, visit,
+        )
+
+
+def couple_kernel(coef_dev, depth, layers, space_ref, known, part, mode_face, *refs):
+    sums, (rest, to_other, to_pair) = refs[: depth // layers], refs[depth // layers :]
+    nx = part.shape[2]
+    targets = coef_dev * M
+    halo = ITERS - 1
+
+    def read(target, l):
+        return plane(sums, layers, nx, target, l)
+
+    for l in range(depth):
+
+        def visit(c, value, l=l):
+            rest[c, l] = known[c, l] + part[c, l] + value
+
+        late = range(layers, depth)
+        if not {l - 1, l, l + 1} & set(late):
+            for c in range(coef_dev):
+                rest[c, l] = known[c, l] + part[c, l]
+        coupled(l, late, coef_dev, read, mode_face, visit)
+
+    even = lax.rem(space_ref[0], 2) == 0
+
+    def fill(message, first, edge):
+        for c in range(coef_dev):
+            message[c * halo : (c + 1) * halo] = rest[c, first : first + halo]
+        for t in range(targets):
+            message[coef_dev * halo + t] = read(t, edge)
         for k in range(M):
-            at = (targets * layers + k * depth) * nx
-            mode_ext[k, pl.ds(slab * depth, depth)] = part[at : at + depth * nx].reshape(
-                depth, nx, -1
+            message[coef_dev * halo + targets + k] = mode_plane(
+                sums, layers, depth, nx, targets, k, edge
             )
-    if picked:
-        at = capacity * layers * nx
-        for k in range(M):
-
-            @pl.when(where[2 + k] == where[2 + M])
-            def _(k=k):
-                for part, slab in zip(picked, slabs):
-                    mode_ext[k, pl.ds(slab * depth, depth)] = part[at : at + depth * nx].reshape(
-                        depth, nx, -1
-                    )
-
-        copies[0].wait()
-        begin = where[1] * capacity
-        add_picked(picked, slabs, begin, capacity, targets, layers, summed, tables.at[0], nx)
-    last = 3 * depth - 1
-
-    def mode_faces(l, carry):
-        for k in range(M):
-            got = faces(mode_ext[k, l - 1], mode_ext[k, l], mode_ext[k, l + 1])
-            for i, value in enumerate(got):
-                mode_face[k, i, l] = value
-        return carry
-
-    lax.fori_loop(1, last, mode_faces, 0)
-    for l in range(1, last):
-
-        def visit(c, value, l=l):
-            rest[c, l] = known[c, l] + value
-
-        if not coupled(l, depth, 0, layers, coef_dev, summed, mode_face, visit):
-            for c in range(coef_dev):
-                rest[c, l] = known[c, l]
-
-
-def sweep_kernel(coef_dev, depth, start, layers, space_ref, rest, mode_face, face, *refs):
-    own, other, pair, residual, correction, summed, scaled, first, second = refs
+
+    @pl.when(even)
+    def _():
+        fill(to_pair, depth - halo, depth - 1)
+        fill(to_other, 0, 0)
+
+    @pl.when(jnp.logical_not(even))
+    def _():
+        fill(to_pair, 0, 0)
+        fill(to_other, depth - halo, depth - 1)
+
+
+def sweep_kernel(coef_dev, depth, layers, space_ref, rest, face, other, pair, *refs):
+    sums = refs[: depth // layers]
+    residual, correction, edges, scaled, first, second = refs[depth // layers :]
     nx = rest.shape[2]
+    targets = coef_dev * M
+    halo = ITERS - 1
     even = lax.rem(space_ref[0], 2) == 0
-    order_parts((own, other, pair), even, coef_dev * M, layers, summed, nx)
-    last = 3 * depth - 1
+
+    def rows(c, l):
+        return pl.ds(pl.multiple_of((c * 3 * depth + l) * nx, nx), nx)
+
+    for part, below in ((pair, jnp.logical_not(even)), (other, even)):
+        at = jnp.where(below, depth - halo, 2 * depth)
+        for c in range(coef_dev):
+            for i in range(halo):
+                scaled[rows(c, at + i), :] = part[c * halo + i]
+        edges[jnp.where(below, 0, 1)] = part[coef_dev * halo :]
+    half_modes = [
+        [
+            0.5 * (mode_plane(sums, layers, depth, nx, targets, k, l) + edges[side, targets + k])
+            for k in range(M)
+        ]
+        for side, l in ((0, 0), (1, depth - 1))
+    ]
+    for c in range(coef_dev):
+        for l in range(depth):
+            total = rest[c, l]
+            for side, edge, beyond in ((0, 0, depth - 1), (1, depth - 1, 2 * depth)):
+                if l != edge:
+                    continue
+                flux = None
+                for k in range(M):
+                    target = c * M + k
+                    drop = plane(sums, layers, nx, target, l) - edges[side, target]
+                    term = half_modes[side][k] * drop
+                    flux = term if flux is None else flux + term
+                total = total - flux
+                scaled[rows(c, beyond), :] = scaled[rows(c, beyond), :] + flux
+            residual[c, l] = total
+            scaled[rows(c, depth + l), :] = total
+
     midpoint, steps = sweep_constants()
-    for l in range(1, last):
-
-        def visit(c, value, l=l):
-            total = rest[c, l] if value is None else rest[c, l] + value
-            w = total * face[6, l]
+
+    def start(l, own):
+        for c in range(coef_dev):
+            w = scaled[rows(c, l), :] * face[6, l]
             d = w * (1.0 / midpoint)
-            scaled[c, l] = w
-            first[c, l] = d
-            if depth <= l < 2 * depth:
-                residual[c, l - depth] = total
+            scaled[rows(c, l), :] = w
+            first[rows(c, l), :] = d
+            if own:
                 correction[c, l - depth] = d
 
-        if not coupled(l, depth, start, layers, coef_dev, summed, mode_face, visit):
-            for c in range(coef_dev):
-                visit(c, None)
+    over_layers(start, depth, halo)
 
     now, later = first, second
     for number, (keep, gain) in enumerate(steps):
 
         def swept(l, own, now=now, later=later, keep=keep, gain=gain, number=number):
             for c in range(coef_dev):
-                v = now[c, l]
-                spread = lateral(face[0, l] * v, face[1, l] * v, face[2, l] * v, face[3, l] * v)
-                spread = spread + face[4, l] * now[c, l - 1] + face[5, l] * now[c, l + 1]
-                w = scaled[c, l] - v + face[6, l] * spread
+                at = pl.multiple_of((c * 3 * depth + l) * nx, nx)
+                here = pl.ds(at, nx)
+                v = now[here, :]
+                w = scaled[here, :] - v
+                w = w + face[0, l] * now[pl.ds(at - 1, nx), :]
+                w = w + face[1, l] * now[pl.ds(at + 1, nx), :]
+                w = w + face[2, l] * shifted(v, 1, 1) + face[3, l] * shifted(v, 1, -1)
+                w = w + face[4, l] * now[pl.ds(at - nx, nx), :]
+                w = w + face[5, l] * now[pl.ds(at + nx, nx), :]
                 d = keep * v + gain * w
                 if number + 1 < len(steps):
-                    scaled[c, l] = w
-                    later[c, l] = d
+                    scaled[here, :] = w
+                    later[here, :] = d
                 if own:
                     correction[c, l - depth] = correction[c, l - depth] + d
 
@@ -561,68 +577,63 @@
     assert count * capacity <= ny
     chunks = pack(coeffs, mode_bank, links[0], capacity, rows_of)
 
-    sums, opposite, opposite_device = chaos_sums(
+    sums = chaos_sums(
         chunks, coef_dev, capacity, rows_of, slot_rows, mode_owner
     )
 
-    early = jnp.concatenate(
-        [coeffs.reshape(-1, nx, ny), source.reshape(-1, nx, ny), mean_field], axis=0
-    )
-    other, pair = depth_pair(early)
-    wide = (coef_dev, 3 * depth, nx, ny)
+    halo = ITERS - 1
+    assert halo < depth and depth == CHUNKS * per_chunk
+    ends = coeffs[:, :: depth - 1].reshape(-1, nx, ny)
+    early = jnp.concatenate([ends, mean_field], axis=0)
+    other, pair = depth_pair(early, early)
+    ext = (7, 3 * depth, nx, ny)
+    own = jax.ShapeDtypeStruct(coeffs.shape, jnp.float32)
     known, face = pl.pallas_call(
         functools.partial(base_kernel, coef_dev, depth, n_space),
-        out_shape=(
-            jax.ShapeDtypeStruct(wide, jnp.float32),
-            jax.ShapeDtypeStruct((7, 3 * depth, nx, ny), jnp.float32),
-        ),
+        out_shape=(own, jax.ShapeDtypeStruct(ext, jnp.float32)),
         in_specs=[SMEM] + [VMEM] * 5,
         out_specs=(VMEM, VMEM),
         scratch_shapes=[
-            pltpu.VMEM(wide, jnp.float32),
+            pltpu.VMEM((coef_dev, depth + 2, nx, ny), jnp.float32),
             pltpu.VMEM((3 * depth, nx, ny), jnp.float32),
         ],
-        cost_estimate=cost(3 * depth * coef_dev, nx, ny, 20),
-        compiler_params=pltpu.CompilerParams(vmem_limit_bytes=16 << 20),
+        compiler_params=pltpu.CompilerParams(vmem_limit_bytes=8 << 20),
+        cost_estimate=cost(depth * coef_dev, nx, ny, 20),
         name="base",
     )(index, coeffs, source, mean_field, other, pair)
 
-    parts = [[own, *depth_pair(own)] for own in sums]
-    picked = [] if opposite is None else [opposite, *depth_pair(opposite)]
-    where = jnp.stack(
-        [index[0], lax.axis_index("chaos"), *(mode_owner[k] for k in range(M)), opposite_device]
-    ).astype(jnp.int32)
-    layers = layer_counts[0]
-    ordered = pltpu.VMEM((3, coef_dev * M, layers, nx, ny), jnp.float32)
-    mode_faces = (M, 7, 3 * depth, nx, ny)
-    rest, mode_face = pl.pallas_call(
-        functools.partial(begin_kernel, coef_dev, depth, layers, capacity, len(picked)),
-        out_shape=(
-            jax.ShapeDtypeStruct(wide, jnp.float32),
-            jax.ShapeDtypeStruct(mode_faces, jnp.float32),
-        ),
-        in_specs=[SMEM] + [VMEM] * (4 + len(picked)),
+    layers = per_chunk
+    part, mode_face = pl.pallas_call(
+        functools.partial(begin_kernel, coef_dev, depth, layers),
+        out_shape=(own, jax.ShapeDtypeStruct((M, 7, depth, nx, ny), jnp.float32)),
+        in_specs=[VMEM],
         out_specs=(VMEM, VMEM),
-        scratch_shapes=[
-            ordered,
-            pltpu.VMEM((M, 3 * depth, nx, ny), jnp.float32),
-            *table_scratch(1, ny),
-        ],
-        compiler_params=pltpu.CompilerParams(vmem_limit_bytes=16 << 20),
-        cost_estimate=cost(3 * depth * coef_dev, nx, ny, 40),
+        compiler_params=pltpu.CompilerParams(vmem_limit_bytes=8 << 20),
+        cost_estimate=cost(depth * coef_dev, nx, ny, 20),
         name="begin",
-    )(where, known, *parts[0], *picked)
-    out = jax.ShapeDtypeStruct(coeffs.shape, jnp.float32)
+    )(sums[0])
+    message = jax.ShapeDtypeStruct((coef_dev * (halo + M) + M, nx, ny), jnp.float32)
+    rest, to_other, to_pair = pl.pallas_call(
+        functools.partial(couple_kernel, coef_dev, depth, layers),
+        out_shape=(own, message, message),
+        in_specs=[SMEM] + [VMEM] * (3 + len(sums)),
+        out_specs=(VMEM, VMEM, VMEM),
+        compiler_params=pltpu.CompilerParams(vmem_limit_bytes=8 << 20),
+        cost_estimate=cost(depth * coef_dev, nx, ny, 20),
+        name="couple",
+    )(index, known, part, mode_face, *sums)
+    other, pair = depth_pair(to_other, to_pair)
     return pl.pallas_call(
-        functools.partial(sweep_kernel, coef_dev, depth, depth - layers, layers),
-        out_shape=(out, out),
-        in_specs=[SMEM] + [VMEM] * 6,
+        functools.partial(sweep_kernel, coef_dev, depth, layers),
+        out_shape=(own, own),
+        in_specs=[SMEM] + [VMEM] * (4 + len(sums)),
         out_specs=(VMEM, VMEM),
-        scratch_shapes=[ordered] + [pltpu.VMEM(wide, jnp.float32)] * 3,
-        compiler_params=pltpu.CompilerParams(vmem_limit_bytes=20 << 20),
+        scratch_shapes=[pltpu.VMEM((2, coef_dev * M + M, nx, ny), jnp.float32)]
+        + [pltpu.VMEM((coef_dev * 3 * depth * nx, ny), jnp.float32)] * 3,
+        compiler_params=pltpu.CompilerParams(vmem_limit_bytes=12 << 20),
         cost_estimate=cost(6 * depth * coef_dev, nx, ny, 40),
         name="sweeps",
-    )(index, rest, mode_face, face, *parts[1])
+    )(index, rest, face, other, pair, *sums)
 
 
 def solution(mesh):

time: 93.5 us -> 81.5 us (0.87)
  starting transfers between devices: 33.8 us -> 27.5 us
  waiting for transfers between devices: 18.9 us -> 23.8 us
  local copies, waits for them, and re-layouts: 7.93 us -> 3.04 us
  Pallas kernels: 27.5 us -> 24 us
  other arithmetic: 3.14 us -> 1.7 us
    ppermute x8 -> x4, starting transfers between devices: 20.7 us -> 14.4 us  [the longest x2 11.4 us: depth_pair(): other = lax.ppermute(to_other, 'space', second)]
    unnamed x32 -> x16, local copies, waits for them, and re-layouts: 7.03 us -> 1.82 us
    ppermute x14, waiting for transfers between devices: 11.6 us -> 15.3 us  [chaos_sums(): block = lax.ppermute(block, 'chaos', pairs)]
    pallas_call x2 -> x3, Pallas kernels: 8.62 us -> 4.91 us  [the longest x1 4.02 us: residual_and_correction(): pl.pallas_call(functools.partial(sweep_kernel, coef_dev, depth, layers),...]
    ppermute x8 -> x4, waiting for transfers between devices: 7.34 us -> 8.53 us  [the longest x2 8.53 us: depth_pair(): other = lax.ppermute(to_other, 'space', second)]
    slice x0 -> x1, local copies, waits for them, and re-layouts: none -> 0.97 us  [residual_and_correction(): ends = coeffs[:, ::depth - 1].reshape(-1, nx, ny)]
  transfers between devices with their start and end apart: 22 -> 18, of which waited for: 6 -> 4; matrix products, arithmetic and copies ran while one was open for 4% -> 4% of each run, Pallas kernels for 22% -> 18%
where the time goes in v4:
time: 81.5 us; the launch traced here: 81.1 us
  starting transfers between devices  27.5 us (34%)
  Pallas kernels  24 us (29%)
  waiting for transfers between devices  23.8 us (29%)
  local copies, waits for them, and re-layouts  3.04 us (4%)
  other arithmetic  1.7 us (2%)
  between operations  0.97 us (1%)
    ppermute x14, waiting for transfers between devices, chaos_sums(): block = lax.ppermute(block, 'chaos', pairs)  15.3 us
    ppermute x14, starting transfers between devices, chaos_sums(): block = lax.ppermute(block, 'chaos', pairs)  13.1 us
    ppermute x2, starting transfers between devices, depth_pair(): other = lax.ppermute(to_other, 'space', second)  11.4 us
    pallas_call x5, Pallas kernels, sum_blocks(): pl.pallas_call(functools.partial(sum_kernel, picked, coef_dev, capacity,...  8.63 us
    ppermute x2, waiting for transfers between devices, depth_pair(): other = lax.ppermute(to_other, 'space', second)  8.53 us
    pallas_call x4, Pallas kernels, pick(): pl.pallas_call(functools.partial(pick_kernel, coef_dev, capacity, rows),...  5.25 us
    pallas_call x1, Pallas kernels, residual_and_correction(): pl.pallas_call(functools.partial(sweep_kernel, coef_dev, depth, layers),...  4.02 us
    ppermute x2, starting transfers between devices, depth_pair(): pair = lax.ppermute(to_pair, 'space', first)  3.02 us
  transfers between devices with their start and end apart: 18, of which 4 were waited for; matrix products, arithmetic and copies ran while one was open for 4% of the time, Pallas kernels for 18%

profile of v4, /device:TPU:1, one launch (start us, length us, event | category | flops | bytes accessed | tf_op | source)
XLA Modules:
  0.0 81.1 jit_solution(15015912030187413870)
XLA Ops:
  0.6 2.7 %pack.1 = (f32[648,128]{1,0:T(8,128)}, f32[520,128]{1,0:T(8,128)}) custom-call(s32[4,32]{1,0:T(4,128)} %bitcast.21, f32[8,128,128]{2,1,0:T(8,128)} %bitcast.18, f32[1,128,128]{2,1,0:T(8,128)} %bitcast.20), custom_call_target="tpu_custom_call" | custom-call | flops 131072 | bytes 1048576 | tf_op jit(solution)/shard_map/pack/pallas_call | solution.py:119
  3.3 2.2 %collective-permute-start.5 = (f32[648,128]{1,0:T(8,128)}, f32[648,128]{1,0:T(8,128)S(1)}, u32[]{:S(2)}, u32[]{:S(2)}) collective-permute-start(f32[648,128]{1,0:T(8,128)} %get-tuple-element.12.refs_0_), channel_id=1, source_target_pairs={{0,8},{8,16},{16,24},{24,28},{28,20},{20,12},{12,4},{4,0},{1,9},{9... | collective-permute-start | bytes 995336 | tf_op jit(solution)/shard_map/ppermute | solution.py:294
  5.5 1.4 %collective-permute-start.9 = (f32[520,128]{1,0:T(8,128)}, f32[520,128]{1,0:T(8,128)S(1)}, u32[]{:S(2)}, u32[]{:S(2)}) collective-permute-start(f32[520,128]{1,0:T(8,128)} %get-tuple-element.15.refs_0_), channel_id=1, source_target_pairs={{8,0},{16,8},{24,16},{28,24},{20,28},{12,20},{4,12},{0,4},{9,1},{1... | collective-permute-start | bytes 798728 | tf_op jit(solution)/shard_map/ppermute | solution.py:294
  6.8 6.2 %collective-permute-done.5.refs_2_ = f32[648,128]{1,0:T(8,128)S(1)} collective-permute-done((f32[648,128]{1,0:T(8,128)}, f32[648,128]{1,0:T(8,128)S(1)}, u32[]{:S(2)}, u32[]{:S(2)}) %collective-permute-start.5) | collective-permute-done | bytes 331808 | tf_op jit(solution)/shard_map/ppermute | solution.py:294
  14.3 1.3 %collective-permute-start.13 = (f32[520,128]{1,0:T(8,128)}, f32[520,128]{1,0:T(8,128)}, u32[]{:S(2)}, u32[]{:S(2)}) collective-permute-start(f32[520,128]{1,0:T(8,128)} %get-tuple-element.15.refs_0_), channel_id=1, source_target_pairs={{0,8},{8,16},{16,24},{24,28},{28,20},{20,12},{12,4},{4,0},{1,9},{9... | collective-permute-start | bytes 798728 | tf_op jit(solution)/shard_map/ppermute | solution.py:294
  15.6 4.1 %collective-permute-done.9.refs_1_ = f32[520,128]{1,0:T(8,128)S(1)} collective-permute-done((f32[520,128]{1,0:T(8,128)}, f32[520,128]{1,0:T(8,128)S(1)}, u32[]{:S(2)}, u32[]{:S(2)}) %collective-permute-start.9) | collective-permute-done | bytes 266272 | tf_op jit(solution)/shard_map/ppermute | solution.py:294
  22.1 4.9 %collective-permute-done.13.refs_2_ = f32[520,128]{1,0:T(8,128)} collective-permute-done((f32[520,128]{1,0:T(8,128)}, f32[520,128]{1,0:T(8,128)}, u32[]{:S(2)}, u32[]{:S(2)}) %collective-permute-start.13) | collective-permute-done | bytes 266272 | tf_op jit(solution)/shard_map/ppermute | solution.py:294
  28.0 1.3 %collective-permute-start.7 = (f32[648,128]{1,0:T(8,128)S(1)}, f32[648,128]{1,0:T(8,128)S(1)}, u32[]{:S(2)}, u32[]{:S(2)}) collective-permute-start(f32[648,128]{1,0:T(8,128)S(1)} %collective-permute-done.6.refs_4_), channel_id=1, source_target_pairs={{0,8},{8,16},{16,24},{24,28},{28,20},{20,12},{12,4},{4,0},{1,9},{9... | collective-permute-start | bytes 995336 | tf_op jit(solution)/shard_map/ppermute | solution.py:294
  29.3 1.6 %pad_maximum_fusion = f32[20,32,128]{2,1,0:T(8,128)} fusion(f32[4,32,128]{2,1,0:T(8,128)} %mean.1, f32[16,32,128]{2,1,0:T(8,128)S(1)} %bitcast.19), kind=kLoop, calls=%fused_computation | loop fusion | flops 81920 | bytes 655360 | tf_op jit(solution)/shard_map/concatenate | solution.py:587
  30.9 2.9 %collective-permute-start.1 = (f32[20,32,128]{2,1,0:T(8,128)}, f32[20,32,128]{2,1,0:T(8,128)}, u32[]{:S(2)}, u32[]{:S(2)}) collective-permute-start(f32[20,32,128]{2,1,0:T(8,128)} %pad_maximum_fusion), channel_id=1, source_target_pairs={{0,1},{1,0},{2,3},{3,2},{4,5},{5,4},{6,7},{7,6},{8,9},{9,8},{10,11... | collective-permute-start | bytes 983048 | tf_op jit(solution)/shard_map/ppermute | solution.py:322
  34.0 4.7 %collective-permute-start = (f32[20,32,128]{2,1,0:T(8,128)}, f32[20,32,128]{2,1,0:T(8,128)}, u32[]{:S(2)}, u32[]{:S(2)}) collective-permute-start(f32[20,32,128]{2,1,0:T(8,128)} %pad_maximum_fusion), channel_id=1, source_target_pairs={{1,2},{2,1},{5,6},{6,5},{9,10},{10,9},{13,14},{14,13},{17,18},{18,... | collective-permute-start | bytes 983048 | tf_op jit(solution)/shard_map/ppermute | solution.py:321
  38.8 1.3 %pick.4 = f32[456,128]{1,0:T(8,128)} custom-call(s32[1]{0:T(128)} %bitcast.12.begin, f32[648,128]{1,0:T(8,128)S(1)} %collective-permute-done.3.block.refs_0_), custom_call_target="tpu_custom_call" | custom-call | flops 40960 | bytes 327680 | tf_op jit(solution)/shard_map/pick/pallas_call | solution.py:156
  40.8 1.3 %pick.5 = f32[456,128]{1,0:T(8,128)} custom-call(s32[1]{0:T(128)} %bitcast.13.begin, f32[648,128]{1,0:T(8,128)S(1)} %collective-permute-done.7.block.refs_3_), custom_call_target="tpu_custom_call" | custom-call | flops 40960 | bytes 327680 | tf_op jit(solution)/shard_map/pick/pallas_call | solution.py:156
  43.1 1.3 %pick.7 = f32[328,128]{1,0:T(8,128)} custom-call(s32[1]{0:T(128)} %bitcast.13.begin, f32[520,128]{1,0:T(8,128)S(1)} %collective-permute-done.14.block.refs_1_), custom_call_target="tpu_custom_call" | custom-call | flops 40960 | bytes 327680 | tf_op jit(solution)/shard_map/pick/pallas_call | solution.py:156
  44.4 1.3 %collective-permute-start.15 = (f32[328,128]{1,0:T(8,128)}, f32[328,128]{1,0:T(8,128)}, u32[]{:S(2)}, u32[]{:S(2)}) collective-permute-start(f32[328,128]{1,0:T(8,128)} %pick.7), channel_id=1, source_target_pairs={{0,8},{8,16},{16,24},{24,28},{28,20},{20,12},{12,4},{4,0},{1,9},{9... | collective-permute-start | bytes 503816 | tf_op jit(solution)/shard_map/ppermute | solution.py:294
  48.6 1.8 %shard_map.79.refs_2_ = f32[1024,128]{1,0:T(8,128)S(1)} custom-call(s32[6]{0:T(128)S(1)} %stack.62.where, f32[520,128]{1,0:T(8,128)S(1)} %copy-done.3, f32[520,128]{1,0:T(8,128)S(1)} %copy-done.5, f32[520,128]{1,0:T(8,128)} %collective-permute-done.13.refs_2_), custom_call_target="tpu_custom_call" | custom-call | flops 524288 | bytes 1048576 | tf_op jit(solution)/shard_map/pallas_call | solution.py:203
  51.3 2.6 %base.1 = (f32[8,4,32,128]{3,2,1,0:T(8,128)S(1)}, f32[7,12,32,128]{3,2,1,0:T(8,128)S(1)}) custom-call(s32[1]{0:T(128)} %bitcast.space_ref, f32[8,4,32,128]{3,2,1,0:T(8,128)S(1)} %copy-done, f32[8,4,32,128]{3,2,1,0:T(8,128)S(1)} %copy-done.1, f32[4,32,128]{2,1,0:T(8,128)S(1)} %copy-done.6, f32[20,32,128]{2,1,0:T(8,128)} %collective-permute-done.refs_0_, ...), custom_call_target="tpu_custom_call" | custom-call | flops 2621440 | bytes 1048576 | tf_op jit(solution)/shard_map/base/pallas_call | solution.py:591
  53.9 1.3 %shard_map.77.refs_5_ = f32[1280,128]{1,0:T(8,128)S(1)} custom-call(s32[6]{0:T(128)S(1)} %stack.62.where, f32[648,128]{1,0:T(8,128)S(1)} %copy-done.2, f32[648,128]{1,0:T(8,128)S(1)} %collective-permute-done.2.refs_1_, f32[648,128]{1,0:T(8,128)S(1)} %collective-permute-done.5.refs_2_), custom_call_target="tpu_custom_call" | custom-call | flops 524288 | bytes 1048576 | tf_op jit(solution)/shard_map/pallas_call | solution.py:203
  55.2 1.7 %shard_map.80.refs_3_ = f32[1024,128]{1,0:T(8,128)S(1)} custom-call(s32[5]{0:T(128)S(1)} %pad_add_fusion.where, f32[520,128]{1,0:T(8,128)} %collective-permute-done.10.refs_0_, f32[520,128]{1,0:T(8,128)S(1)} %collective-permute-done.14.block.refs_1_, f32[1024,128]{1,0:T(8,128)S(1)} %shard_map.79.refs_2_), custom_call_target="tpu_custom_call" | custom-call | flops 524288 | bytes 1048576 | tf_op jit(solution)/shard_map/pallas_call | solution.py:203
  56.9 1.8 %shard_map.81.refs_1_ = f32[1024,128]{1,0:T(8,128)S(1)} custom-call(s32[6]{0:T(128)S(1)} %stack.63.where, f32[520,128]{1,0:T(8,128)S(1)} %collective-permute-done.11.block.refs_0_, f32[328,128]{1,0:T(8,128)} %collective-permute-done.12.refs_1_, f32[328,128]{1,0:T(8,128)} %collective-permute-done.15.refs_2_, f32[1024,128]{1,0:T(8,128)S(1)} %shard_map.80.refs_3_), custom_call_target="tpu_custom_call" | custom-call | flops 524288 | bytes 1048576 | tf_op jit(solution)/shard_map/pallas_call | solution.py:203
  58.7 2.0 %shard_map.78.sums.refs_0_ = f32[1280,128]{1,0:T(8,128)S(1)} custom-call(s32[8]{0:T(128)S(1)} %stack.58.where, f32[648,128]{1,0:T(8,128)S(1)} %collective-permute-done.3.block.refs_0_, f32[456,128]{1,0:T(8,128)} %collective-permute-done.4.refs_1_, f32[456,128]{1,0:T(8,128)} %collective-permute-done.8.refs_2_, ...), custom_call_target="tpu_custom_call" | custom-call | flops 524288 | bytes 1048576 | tf_op jit(solution)/shard_map/pallas_call | solution.py:203
  61.7 6.8 %collective-permute-start.16 = (f32[42,32,128]{2,1,0:T(8,128)S(1)}, f32[42,32,128]{2,1,0:T(8,128)S(1)}, u32[]{:S(2)}, u32[]{:S(2)}) collective-permute-start(f32[42,32,128]{2,1,0:T(8,128)S(1)} %get-tuple-element.18), channel_id=1, source_target_pairs={{1,2},{2,1},{5,6},{6,5},{9,10},{10,9},{13,14},{14,13},{17,18},{18,... | collective-permute-start | bytes 2064392 | tf_op jit(solution)/shard_map/ppermute | solution.py:321
  68.5 8.5 %collective-permute-done.16.other = f32[42,32,128]{2,1,0:T(8,128)S(1)} collective-permute-done((f32[42,32,128]{2,1,0:T(8,128)S(1)}, f32[42,32,128]{2,1,0:T(8,128)S(1)}, u32[]{:S(2)}, u32[]{:S(2)}) %collective-permute-start.16) | collective-permute-done | bytes 688160 | tf_op jit(solution)/shard_map/ppermute | solution.py:321
  77.0 4.0 %sweeps.1 = (f32[8,4,32,128]{3,2,1,0:T(8,128)}, f32[8,4,32,128]{3,2,1,0:T(8,128)}) custom-call(s32[1]{0:T(128)} %bitcast.space_ref, f32[8,4,32,128]{3,2,1,0:T(8,128)S(1)} %get-tuple-element.16.rest, f32[7,12,32,128]{3,2,1,0:T(8,128)S(1)} %get-tuple-element.17.face, f32[42,32,128]{2,1,0:T(8,128)S(1)} %collective-permute-done.16.other, ...), custom_call_target="tpu_custom_call" | custom-call | flops 31457280 | bytes 6291456 | tf_op jit(solution)/shard_map/sweeps/pallas_call | solution.py:626
  (48 shorter events, 11.0 us)
Async XLA Ops:
  3.3 9.8 %collective-permute-start.5 = (f32[648,128]{1,0:T(8,128)}, f32[648,128]{1,0:T(8,128)S(1)}, u32[]{:S(2)}, u32[]{:S(2)}) collective-permute-start(f32[648,128]{1,0:T(8,128)} %get-tuple-element.12.refs_0_), channel_id=1, source_target_pairs={{0,8},{8,16},{16,24},{24,28},{28,20},{20,12},{12,4},{4,0},{1,9},{9... | collective-permute-start | bytes 995336 | tf_op jit(solution)/shard_map/ppermute | solution.py:294
  5.5 14.6 %collective-permute-start.2 = (f32[648,128]{1,0:T(8,128)}, f32[648,128]{1,0:T(8,128)S(1)}, u32[]{:S(2)}, u32[]{:S(2)}) collective-permute-start(f32[648,128]{1,0:T(8,128)} %get-tuple-element.12.refs_0_), channel_id=1, source_target_pairs={{8,0},{16,8},{24,16},{28,24},{20,28},{12,20},{4,12},{0,4},{9,1},{1... | collective-permute-start | bytes 995336 | tf_op jit(solution)/shard_map/ppermute | solution.py:294
  5.5 14.3 %collective-permute-start.9 = (f32[520,128]{1,0:T(8,128)}, f32[520,128]{1,0:T(8,128)S(1)}, u32[]{:S(2)}, u32[]{:S(2)}) collective-permute-start(f32[520,128]{1,0:T(8,128)} %get-tuple-element.15.refs_0_), channel_id=1, source_target_pairs={{8,0},{16,8},{24,16},{28,24},{20,28},{12,20},{4,12},{0,4},{9,1},{1... | collective-permute-start | bytes 798728 | tf_op jit(solution)/shard_map/ppermute | solution.py:294
  13.1 14.9 %collective-permute-start.6 = (f32[648,128]{1,0:T(8,128)S(1)}, f32[648,128]{1,0:T(8,128)S(1)}, u32[]{:S(2)}, u32[]{:S(2)}) collective-permute-start(f32[648,128]{1,0:T(8,128)S(1)} %collective-permute-done.5.refs_2_), channel_id=1, source_target_pairs={{0,8},{8,16},{16,24},{24,28},{28,20},{20,12},{12,4},{4,0},{1,9},{9... | collective-permute-start | bytes 995336 | tf_op jit(solution)/shard_map/ppermute | solution.py:294
  14.3 12.7 %collective-permute-start.13 = (f32[520,128]{1,0:T(8,128)}, f32[520,128]{1,0:T(8,128)}, u32[]{:S(2)}, u32[]{:S(2)}) collective-permute-start(f32[520,128]{1,0:T(8,128)} %get-tuple-element.15.refs_0_), channel_id=1, source_target_pairs={{0,8},{8,16},{16,24},{24,28},{28,20},{20,12},{12,4},{4,0},{1,9},{9... | collective-permute-start | bytes 798728 | tf_op jit(solution)/shard_map/ppermute | solution.py:294
  19.8 14.1 %copy-start.4 = (f32[520,128]{1,0:T(8,128)}, f32[520,128]{1,0:T(8,128)S(1)}, u32[]{:S(2)}) copy-start(f32[520,128]{1,0:T(8,128)S(1)} %collective-permute-done.9.refs_1_) | copy-start | bytes 798724
  19.8 14.1 %collective-permute-start.10 = (f32[520,128]{1,0:T(8,128)S(1)}, f32[520,128]{1,0:T(8,128)}, u32[]{:S(2)}, u32[]{:S(2)}) collective-permute-start(f32[520,128]{1,0:T(8,128)S(1)} %collective-permute-done.9.refs_1_), channel_id=1, source_target_pairs={{8,0},{16,8},{24,16},{28,24},{20,28},{12,20},{4,12},{0,4},{9,1},{1... | collective-permute-start | bytes 798728 | tf_op jit(solution)/shard_map/ppermute | solution.py:294
  20.1 14.0 %collective-permute-start.3 = (f32[648,128]{1,0:T(8,128)S(1)}, f32[648,128]{1,0:T(8,128)S(1)}, u32[]{:S(2)}, u32[]{:S(2)}) collective-permute-start(f32[648,128]{1,0:T(8,128)S(1)} %collective-permute-done.2.refs_1_), channel_id=1, source_target_pairs={{8,0},{16,8},{24,16},{28,24},{20,28},{12,20},{4,12},{0,4},{9,1},{1... | collective-permute-start | bytes 995336 | tf_op jit(solution)/shard_map/ppermute | solution.py:294
  27.0 15.2 %collective-permute-start.14 = (f32[520,128]{1,0:T(8,128)}, f32[520,128]{1,0:T(8,128)S(1)}, u32[]{:S(2)}, u32[]{:S(2)}) collective-permute-start(f32[520,128]{1,0:T(8,128)} %collective-permute-done.13.refs_2_), channel_id=1, source_target_pairs={{0,8},{8,16},{16,24},{24,28},{28,20},{20,12},{12,4},{4,0},{1,9},{9... | collective-permute-start | bytes 798728 | tf_op jit(solution)/shard_map/ppermute | solution.py:294
  28.0 12.2 %collective-permute-start.7 = (f32[648,128]{1,0:T(8,128)S(1)}, f32[648,128]{1,0:T(8,128)S(1)}, u32[]{:S(2)}, u32[]{:S(2)}) collective-permute-start(f32[648,128]{1,0:T(8,128)S(1)} %collective-permute-done.6.refs_4_), channel_id=1, source_target_pairs={{0,8},{8,16},{16,24},{24,28},{28,20},{20,12},{12,4},{4,0},{1,9},{9... | collective-permute-start | bytes 995336 | tf_op jit(solution)/shard_map/ppermute | solution.py:294
  29.3 18.0 %copy-start.7 = (s32[2]{0:T(128)S(1)}, s32[2]{0:T(128)}, u32[]{:S(2)}) copy-start(s32[2]{0:T(128)} %param.10) | copy-start | bytes 28
  29.3 18.3 %copy-start.3 = (f32[520,128]{1,0:T(8,128)S(1)}, f32[520,128]{1,0:T(8,128)}, u32[]{:S(2)}) copy-start(f32[520,128]{1,0:T(8,128)} %get-tuple-element.15.refs_0_) | copy-start | bytes 798724
  30.9 16.1 %collective-permute-start.1 = (f32[20,32,128]{2,1,0:T(8,128)}, f32[20,32,128]{2,1,0:T(8,128)}, u32[]{:S(2)}, u32[]{:S(2)}) collective-permute-start(f32[20,32,128]{2,1,0:T(8,128)} %pad_maximum_fusion), channel_id=1, source_target_pairs={{0,1},{1,0},{2,3},{3,2},{4,5},{5,4},{6,7},{7,6},{8,9},{9,8},{10,11... | collective-permute-start | bytes 983048 | tf_op jit(solution)/shard_map/ppermute | solution.py:322
  33.9 10.5 %collective-permute-start.11 = (f32[520,128]{1,0:T(8,128)}, f32[520,128]{1,0:T(8,128)S(1)}, u32[]{:S(2)}, u32[]{:S(2)}) collective-permute-start(f32[520,128]{1,0:T(8,128)} %collective-permute-done.10.refs_0_), channel_id=1, source_target_pairs={{8,0},{16,8},{24,16},{28,24},{20,28},{12,20},{4,12},{0,4},{9,1},{1... | collective-permute-start | bytes 798728 | tf_op jit(solution)/shard_map/ppermute | solution.py:294
  34.0 16.4 %collective-permute-start = (f32[20,32,128]{2,1,0:T(8,128)}, f32[20,32,128]{2,1,0:T(8,128)}, u32[]{:S(2)}, u32[]{:S(2)}) collective-permute-start(f32[20,32,128]{2,1,0:T(8,128)} %pad_maximum_fusion), channel_id=1, source_target_pairs={{1,2},{2,1},{5,6},{6,5},{9,10},{10,9},{13,14},{14,13},{17,18},{18,... | collective-permute-start | bytes 983048 | tf_op jit(solution)/shard_map/ppermute | solution.py:321
  40.2 18.6 %collective-permute-start.4 = (f32[456,128]{1,0:T(8,128)}, f32[456,128]{1,0:T(8,128)}, u32[]{:S(2)}, u32[]{:S(2)}) collective-permute-start(f32[456,128]{1,0:T(8,128)} %pick.4), channel_id=1, source_target_pairs={{8,0},{16,8},{24,16},{28,24},{20,28},{12,20},{4,12},{0,4},{9,1},{1... | collective-permute-start | bytes 700424 | tf_op jit(solution)/shard_map/ppermute | solution.py:294
  42.1 8.3 %copy-start = (f32[8,4,32,128]{3,2,1,0:T(8,128)S(1)}, f32[8,4,32,128]{3,2,1,0:T(8,128)}, u32[]{:S(2)}) copy-start(f32[8,4,32,128]{3,2,1,0:T(8,128)} %coeffs.1) | copy-start | bytes 1572868
  42.1 8.3 %copy-start.1 = (f32[8,4,32,128]{3,2,1,0:T(8,128)S(1)}, f32[8,4,32,128]{3,2,1,0:T(8,128)}, u32[]{:S(2)}) copy-start(f32[8,4,32,128]{3,2,1,0:T(8,128)} %source.1) | copy-start | bytes 1572868
  42.2 16.6 %collective-permute-start.8 = (f32[456,128]{1,0:T(8,128)}, f32[456,128]{1,0:T(8,128)}, u32[]{:S(2)}, u32[]{:S(2)}) collective-permute-start(f32[456,128]{1,0:T(8,128)} %pick.5), channel_id=1, source_target_pairs={{0,8},{8,16},{16,24},{24,28},{28,20},{20,12},{12,4},{4,0},{1,9},{9... | collective-permute-start | bytes 700424 | tf_op jit(solution)/shard_map/ppermute | solution.py:294
  44.4 12.5 %collective-permute-start.15 = (f32[328,128]{1,0:T(8,128)}, f32[328,128]{1,0:T(8,128)}, u32[]{:S(2)}, u32[]{:S(2)}) collective-permute-start(f32[328,128]{1,0:T(8,128)} %pick.7), channel_id=1, source_target_pairs={{0,8},{8,16},{16,24},{24,28},{28,20},{20,12},{12,4},{4,0},{1,9},{9... | collective-permute-start | bytes 503816 | tf_op jit(solution)/shard_map/ppermute | solution.py:294
  47.1 9.8 %collective-permute-start.12 = (f32[328,128]{1,0:T(8,128)}, f32[328,128]{1,0:T(8,128)}, u32[]{:S(2)}, u32[]{:S(2)}) collective-permute-start(f32[328,128]{1,0:T(8,128)} %pick.6), channel_id=1, source_target_pairs={{8,0},{16,8},{24,16},{28,24},{20,28},{12,20},{4,12},{0,4},{9,1},{1... | collective-permute-start | bytes 503816 | tf_op jit(solution)/shard_map/ppermute | solution.py:294
  48.6 5.3 %copy-start.2 = (f32[648,128]{1,0:T(8,128)S(1)}, f32[648,128]{1,0:T(8,128)}, u32[]{:S(2)}) copy-start(f32[648,128]{1,0:T(8,128)} %get-tuple-element.12.refs_0_) | copy-start | bytes 995332
  61.7 15.4 %collective-permute-start.16 = (f32[42,32,128]{2,1,0:T(8,128)S(1)}, f32[42,32,128]{2,1,0:T(8,128)S(1)}, u32[]{:S(2)}, u32[]{:S(2)}) collective-permute-start(f32[42,32,128]{2,1,0:T(8,128)S(1)} %get-tuple-element.18), channel_id=1, source_target_pairs={{1,2},{2,1},{5,6},{6,5},{9,10},{10,9},{13,14},{14,13},{17,18},{18,... | collective-permute-start | bytes 2064392 | tf_op jit(solution)/shard_map/ppermute | solution.py:321
  68.4 8.6 %collective-permute-start.17 = (f32[42,32,128]{2,1,0:T(8,128)S(1)}, f32[42,32,128]{2,1,0:T(8,128)S(1)}, u32[]{:S(2)}, u32[]{:S(2)}) collective-permute-start(f32[42,32,128]{2,1,0:T(8,128)S(1)} %get-tuple-element.19), channel_id=1, source_target_pairs={{0,1},{1,0},{2,3},{3,2},{4,5},{5,4},{6,7},{7,6},{8,9},{9,8},{10,11... | collective-permute-start | bytes 2064392 | tf_op jit(solution)/shard_map/ppermute | solution.py:322
  (2 other events, 1.8 us)

commit v5 on v4

--- a/solution.py
+++ b/solution.py
@@ -16,6 +16,7 @@
 BOUND_HIGH = 2.0
 
 CHUNKS = 2
+PARTS = 2
 TABLE_ROWS = 8
 
 
@@ -136,25 +137,34 @@
     return copies
 
 
+def device_at(me, shift, count):
+    half = count // 2
+    up = lax.div(me, 2)
+    place = jnp.where(lax.rem(me, 2) == 0, up, count - 1 - up)
+    q = lax.rem(place + shift % count, count)
+    return jnp.where(q < half, 2 * q, 2 * (count - 1 - q) + 1)
+
+
 def table_scratch(n, lanes):
     return [pltpu.SMEM((n, TABLE_ROWS, lanes), jnp.float32), pltpu.SemaphoreType.DMA((n,))]
 
 
-def pick_kernel(coef_dev, capacity, rows, begin, block, out, tables, sems):
+def pick_kernel(coef_dev, capacity, rows, shift, count, me, block, out, tables, sems):
     (copy,) = start_tables([block], tables, sems)
     out[capacity * rows :, :] = block[coef_dev * rows :, :]
+    begin = device_at(me[0], shift, count) * capacity
     copy.wait()
     for e in range(capacity):
-        row = lax.div(tables[0, 0, begin[0] + e].astype(jnp.int32), coef_dev * M)
+        row = lax.div(tables[0, 0, begin + e].astype(jnp.int32), coef_dev * M)
         out[e * rows : (e + 1) * rows, :] = block[
             pl.ds(pl.multiple_of(row * rows, rows), rows), :
         ]
 
 
-def pick(block, device, coef_dev, capacity, rows):
+def pick(block, shift, count, me, coef_dev, capacity, rows):
     size, lanes = block.shape
     return pl.pallas_call(
-        functools.partial(pick_kernel, coef_dev, capacity, rows),
+        functools.partial(pick_kernel, coef_dev, capacity, rows, shift, count),
         out_shape=jax.ShapeDtypeStruct((size - (coef_dev - capacity) * rows, lanes), jnp.float32),
         in_specs=[SMEM, VMEM],
         out_specs=VMEM,
@@ -162,10 +172,12 @@
         compiler_params=pltpu.CompilerParams(vmem_limit_bytes=2 << 20),
         cost_estimate=cost(capacity, rows, lanes, 1),
         name="pick",
-    )((device * capacity).astype(jnp.int32).reshape(1), block)
-
-
-def sum_kernel(picked, coef_dev, capacity, rows, slot_rows, more, where, *refs):
+    )(me, block)
+
+
+def sum_kernel(
+    picked, shifts, count, coef_dev, capacity, rows, slot_rows, more, me_ref, owner_ref, *refs
+):
     refs = list(refs)
     blocks = [refs.pop(0) for _ in picked]
     so_far = refs.pop(0) if more else None
@@ -173,16 +185,17 @@
     targets = coef_dev * M
     copies = start_tables(blocks, tables, sems)
     out[...] = so_far[...] if more else jnp.zeros_like(out)
+    me = me_ref[0]
     if slot_rows:
         for i, (block, few) in enumerate(zip(blocks, picked)):
             for k in range(M):
 
-                @pl.when(where[1 + k] == where[1 + M + i])
+                @pl.when(owner_ref[k] == device_at(me, shifts[i], count))
                 def _(block=block, k=k, few=few):
                     at = pl.ds(targets * rows + k * slot_rows, slot_rows)
                     out[at, :] = block[pl.ds((capacity if few else coef_dev) * rows, slot_rows), :]
 
-    begin = where[0] * capacity
+    begin = me * capacity
     for i, (block, few) in enumerate(zip(blocks, picked)):
         copies[i].wait()
         for e in range(capacity):
@@ -194,21 +207,22 @@
 
 
 def sum_blocks(
-    blocks, picked, devices, me, mode_owner, coef_dev, capacity, rows, slot_rows, so_far
+    blocks, picked, shifts, count, me, owner, coef_dev, capacity, rows, slot_rows, so_far
 ):
     n, lanes = len(blocks), blocks[0].shape[1]
     size = coef_dev * M * rows + M * slot_rows
-    where = jnp.stack([me] + [mode_owner[k] for k in range(M)] + devices).astype(jnp.int32)
     more = so_far is not None
     return pl.pallas_call(
-        functools.partial(sum_kernel, picked, coef_dev, capacity, rows, slot_rows, more),
+        functools.partial(
+            sum_kernel, picked, shifts, count, coef_dev, capacity, rows, slot_rows, more
+        ),
         out_shape=jax.ShapeDtypeStruct((size, lanes), jnp.float32),
-        in_specs=[SMEM] + [VMEM] * (n + more),
+        in_specs=[SMEM, SMEM] + [VMEM] * (n + more),
         out_specs=VMEM,
         scratch_shapes=table_scratch(n, lanes),
         compiler_params=pltpu.CompilerParams(vmem_limit_bytes=5 << 20),
         cost_estimate=cost(coef_dev * M, rows, lanes, 4),
-    )(where, *blocks, *([so_far] if more else []))
+    )(me, owner, *blocks, *([so_far] if more else []))
 
 
 def plain_sums(block, table, mode_slot, device, me, mode_owner, coef_dev, capacity, rows):
@@ -276,13 +290,7 @@
     order = ring_order(count)
     there = [(order[i], order[(i + 1) % count]) for i in range(count)]
     back = [(b, a) for a, b in there]
-    half = count // 2
-    place = jnp.where(me % 2 == 0, me // 2, count - 1 - me // 2)
-
-    def device_at(shift):
-        q = (place + shift) % count
-        return jnp.where(q < half, 2 * q, 2 * (count - 1 - q) + 1)
-
+    me = me.astype(jnp.int32).reshape(1)
     found = []
     for j, (chunk, steps) in enumerate(zip(chunks, ring_steps(count))):
         blocks = {0: (chunk, False)}
@@ -290,7 +298,7 @@
             block = chunk
             for step in range(1, n_steps + 1):
                 if step == n_steps:
-                    block = pick(block, device_at(-sign), coef_dev, capacity, rows_of[j])
+                    block = pick(block, -sign, count, me, coef_dev, capacity, rows_of[j])
                 block = lax.ppermute(block, "chaos", pairs)
                 blocks[sign * step % count] = (block, step == n_steps)
         sums = None
@@ -299,8 +307,12 @@
             sums = sum_blocks(
                 [blocks[s][0] for s in shifts],
                 [blocks[s][1] for s in shifts],
-                [device_at(s) for s in shifts],
-                *fixed,
+                shifts,
+                count,
+                me,
+                mode_owner,
+                coef_dev,
+                capacity,
                 rows_of[j],
                 slot_rows if j == 0 else 0,
                 sums,
@@ -427,7 +439,7 @@
 
 
 def couple_kernel(coef_dev, depth, layers, space_ref, known, part, mode_face, *refs):
-    sums, (rest, to_other, to_pair) = refs[: depth // layers], refs[depth // layers :]
+    sums, (rest, *messages) = refs[: depth // layers], refs[depth // layers :]
     nx = part.shape[2]
     targets = coef_dev * M
     halo = ITERS - 1
@@ -448,15 +460,20 @@
 
     even = lax.rem(space_ref[0], 2) == 0
 
-    def fill(message, first, edge):
-        for c in range(coef_dev):
-            message[c * halo : (c + 1) * halo] = rest[c, first : first + halo]
-        for t in range(targets):
-            message[coef_dev * halo + t] = read(t, edge)
-        for k in range(M):
-            message[coef_dev * halo + targets + k] = mode_plane(
-                sums, layers, depth, nx, targets, k, edge
-            )
+    few = coef_dev // PARTS
+
+    def fill(messages, first, edge):
+        for part, message in enumerate(messages):
+            for c in range(few):
+                message[c * halo : (c + 1) * halo] = rest[part * few + c, first : first + halo]
+            for t in range(few * M):
+                message[few * halo + t] = read(part * few * M + t, edge)
+            for k in range(M):
+                message[few * (halo + M) + k] = mode_plane(
+                    sums, layers, depth, nx, targets, k, edge
+                )
+
+    to_other, to_pair = messages[:PARTS], messages[PARTS:]
 
     @pl.when(even)
     def _():
@@ -469,41 +486,41 @@
         fill(to_other, depth - halo, depth - 1)
 
 
-def sweep_kernel(coef_dev, depth, layers, space_ref, rest, face, other, pair, *refs):
+def sweep_kernel(part, coef_dev, depth, layers, space_ref, rest, face, other, pair, *refs):
     sums = refs[: depth // layers]
-    residual, correction, edges, scaled, first, second = refs[depth // layers :]
+    residual, correction, edges, scaled, first, second = refs[-6:]
     nx = rest.shape[2]
     targets = coef_dev * M
     halo = ITERS - 1
+    few = coef_dev // PARTS
     even = lax.rem(space_ref[0], 2) == 0
 
     def rows(c, l):
         return pl.ds(pl.multiple_of((c * 3 * depth + l) * nx, nx), nx)
 
-    for part, below in ((pair, jnp.logical_not(even)), (other, even)):
+    for message, below in ((pair, jnp.logical_not(even)), (other, even)):
         at = jnp.where(below, depth - halo, 2 * depth)
-        for c in range(coef_dev):
+        for c in range(few):
             for i in range(halo):
-                scaled[rows(c, at + i), :] = part[c * halo + i]
-        edges[jnp.where(below, 0, 1)] = part[coef_dev * halo :]
+                scaled[rows(c, at + i), :] = message[c * halo + i]
+        edges[jnp.where(below, 0, 1)] = message[few * halo :]
     half_modes = [
         [
-            0.5 * (mode_plane(sums, layers, depth, nx, targets, k, l) + edges[side, targets + k])
+            0.5 * (mode_plane(sums, layers, depth, nx, targets, k, l) + edges[side, few * M + k])
             for k in range(M)
         ]
         for side, l in ((0, 0), (1, depth - 1))
     ]
-    for c in range(coef_dev):
+    for c in range(few):
         for l in range(depth):
-            total = rest[c, l]
+            total = rest[part * few + c, l]
             for side, edge, beyond in ((0, 0, depth - 1), (1, depth - 1, 2 * depth)):
                 if l != edge:
                     continue
                 flux = None
                 for k in range(M):
-                    target = c * M + k
-                    drop = plane(sums, layers, nx, target, l) - edges[side, target]
-                    term = half_modes[side][k] * drop
+                    own = plane(sums, layers, nx, (part * few + c) * M + k, l)
+                    term = half_modes[side][k] * (own - edges[side, c * M + k])
                     flux = term if flux is None else flux + term
                 total = total - flux
                 scaled[rows(c, beyond), :] = scaled[rows(c, beyond), :] + flux
@@ -513,7 +530,7 @@
     midpoint, steps = sweep_constants()
 
     def start(l, own):
-        for c in range(coef_dev):
+        for c in range(few):
             w = scaled[rows(c, l), :] * face[6, l]
             d = w * (1.0 / midpoint)
             scaled[rows(c, l), :] = w
@@ -527,7 +544,7 @@
     for number, (keep, gain) in enumerate(steps):
 
         def swept(l, own, now=now, later=later, keep=keep, gain=gain, number=number):
-            for c in range(coef_dev):
+            for c in range(few):
                 at = pl.multiple_of((c * 3 * depth + l) * nx, nx)
                 here = pl.ds(at, nx)
                 v = now[here, :]
@@ -549,17 +566,20 @@
 
 
 def over_layers(visit, depth, halo):
-    def own(l, carry):
-        visit(l, True)
+    def own(i, carry):
+        for l in range(2):
+            visit(depth + 2 * i + l, True)
         return carry
 
     def outside(i, carry):
-        visit(jnp.where(i < halo, depth - halo + i, 2 * depth - halo + i), False)
+        visit(depth - halo + i, False)
+        visit(2 * depth + i, False)
         return carry
 
-    lax.fori_loop(depth, 2 * depth, own, 0)
+    assert depth % 2 == 0
+    lax.fori_loop(0, depth // 2, own, 0)
     if halo:
-        lax.fori_loop(0, 2 * halo, outside, 0)
+        lax.fori_loop(0, halo, outside, 0)
 
 
 def residual_and_correction(coeffs, source, mean_field, mode_bank, mode_owner, links):
@@ -612,28 +632,36 @@
         cost_estimate=cost(depth * coef_dev, nx, ny, 20),
         name="begin",
     )(sums[0])
-    message = jax.ShapeDtypeStruct((coef_dev * (halo + M) + M, nx, ny), jnp.float32)
-    rest, to_other, to_pair = pl.pallas_call(
+    few = coef_dev // PARTS
+    message = jax.ShapeDtypeStruct((few * (halo + M) + M, nx, ny), jnp.float32)
+    rest, *messages = pl.pallas_call(
         functools.partial(couple_kernel, coef_dev, depth, layers),
-        out_shape=(own, message, message),
+        out_shape=[own] + [message] * (2 * PARTS),
         in_specs=[SMEM] + [VMEM] * (3 + len(sums)),
-        out_specs=(VMEM, VMEM, VMEM),
+        out_specs=[VMEM] * (1 + 2 * PARTS),
         compiler_params=pltpu.CompilerParams(vmem_limit_bytes=8 << 20),
         cost_estimate=cost(depth * coef_dev, nx, ny, 20),
         name="couple",
     )(index, known, part, mode_face, *sums)
-    other, pair = depth_pair(to_other, to_pair)
-    return pl.pallas_call(
-        functools.partial(sweep_kernel, coef_dev, depth, layers),
-        out_shape=(own, own),
-        in_specs=[SMEM] + [VMEM] * (4 + len(sums)),
-        out_specs=(VMEM, VMEM),
-        scratch_shapes=[pltpu.VMEM((2, coef_dev * M + M, nx, ny), jnp.float32)]
-        + [pltpu.VMEM((coef_dev * 3 * depth * nx, ny), jnp.float32)] * 3,
-        compiler_params=pltpu.CompilerParams(vmem_limit_bytes=12 << 20),
-        cost_estimate=cost(6 * depth * coef_dev, nx, ny, 40),
-        name="sweeps",
-    )(index, rest, face, other, pair, *sums)
+    found = []
+    for h in range(PARTS):
+        other, pair = depth_pair(messages[h], messages[PARTS + h])
+        first = 5 + len(sums)
+        found = pl.pallas_call(
+            functools.partial(sweep_kernel, h, coef_dev, depth, layers),
+            grid=(1,),
+            out_shape=(own, own),
+            in_specs=[SMEM]
+            + [VMEM] * (first - 1)
+            + [pl.BlockSpec(memory_space=pl.ANY)] * len(found),
+            out_specs=[pl.BlockSpec((few, depth, nx, ny), lambda i, h=h: (h, 0, 0, 0))] * 2,
+            scratch_shapes=[pltpu.VMEM((2, few * M + M, nx, ny), jnp.float32)]
+            + [pltpu.VMEM((few * 3 * depth * nx, ny), jnp.float32)] * 3,
+            input_output_aliases={first + i: i for i in range(len(found))},
+            compiler_params=pltpu.CompilerParams(vmem_limit_bytes=12 << 20),
+            cost_estimate=cost(3 * depth * coef_dev, nx, ny, 40),
+        )(index, rest, face, other, pair, *sums, *found)
+    return tuple(found)
 
 
 def solution(mesh):

time: 81.5 us -> 79.5 us (0.975)
  waiting for transfers between devices: 23.8 us -> 19.9 us
  starting transfers between devices: 27.5 us -> 29.6 us
    ppermute x2 -> x3, waiting for transfers between devices: 8.53 us -> 4.53 us  [depth_pair(): other = lax.ppermute(to_other, 'space', second)]
    ppermute x2 -> x3, starting transfers between devices: 11.4 us -> 13.4 us  [depth_pair(): other = lax.ppermute(to_other, 'space', second)]
    pallas_call x10 -> x11, Pallas kernels: 17.9 us -> 18.5 us  [the longest x5 8.64 us: sum_blocks(): pl.pallas_call(functools.partial(sum_kernel, picked, shifts, count, coef_...]
    ppermute x2 -> x3, starting transfers between devices: 3.02 us -> 3.09 us  [depth_pair(): pair = lax.ppermute(to_pair, 'space', first)]
  transfers between devices with their start and end apart: 18 -> 20, of which waited for: 4 -> 6; matrix products, arithmetic and copies ran while one was open for 4% -> 3% of each run, Pallas kernels for 18% -> 21%
where the time goes in v5:
time: 79.5 us; the launch traced here: 79 us
  starting transfers between devices  29.6 us (37%)
  Pallas kernels  24.3 us (31%)
  waiting for transfers between devices  19.9 us (25%)
  local copies, waits for them, and re-layouts  2.79 us (4%)
  other arithmetic  1.58 us (2%)
  between operations  0.92 us (1%)
    ppermute x14, waiting for transfers between devices, chaos_sums(): block = lax.ppermute(block, 'chaos', pairs)  15.3 us
    ppermute x3, starting transfers between devices, depth_pair(): other = lax.ppermute(to_other, 'space', second)  13.4 us
    ppermute x14, starting transfers between devices, chaos_sums(): block = lax.ppermute(block, 'chaos', pairs)  13 us
    pallas_call x5, Pallas kernels, sum_blocks(): pl.pallas_call(functools.partial(sum_kernel, picked, shifts, count, coef_...  8.64 us
    pallas_call x4, Pallas kernels, pick(): pl.pallas_call(functools.partial(pick_kernel, coef_dev, capacity, rows, s...  5.23 us
    pallas_call x2, Pallas kernels, residual_and_correction(): pl.pallas_call(functools.partial(sweep_kernel, h, coef_dev, depth, layers...  4.67 us
    ppermute x3, waiting for transfers between devices, depth_pair(): other = lax.ppermute(to_other, 'space', second)  4.53 us
    ppermute x3, starting transfers between devices, depth_pair(): pair = lax.ppermute(to_pair, 'space', first)  3.09 us
  transfers between devices with their start and end apart: 20, of which 6 were waited for; matrix products, arithmetic and copies ran while one was open for 3% of the time, Pallas kernels for 21%

profile of v5, /device:TPU:1, one launch (start us, length us, event | category | flops | bytes accessed | tf_op | source)
XLA Modules:
  0.0 79.0 jit_solution(2043797383064389960)
XLA Ops:
  0.6 2.7 %pack.1 = (f32[648,128]{1,0:T(8,128)}, f32[520,128]{1,0:T(8,128)}) custom-call(s32[4,32]{1,0:T(4,128)} %bitcast.11, f32[8,128,128]{2,1,0:T(8,128)} %bitcast.8, f32[1,128,128]{2,1,0:T(8,128)} %bitcast.10), custom_call_target="tpu_custom_call" | custom-call | flops 131072 | bytes 1048576 | tf_op jit(solution)/shard_map/pack/pallas_call | solution.py:120
  3.3 2.2 %collective-permute-start.5 = (f32[648,128]{1,0:T(8,128)}, f32[648,128]{1,0:T(8,128)S(1)}, u32[]{:S(2)}, u32[]{:S(2)}) collective-permute-start(f32[648,128]{1,0:T(8,128)} %get-tuple-element.16.refs_0_), channel_id=1, source_target_pairs={{0,8},{8,16},{16,24},{24,28},{28,20},{20,12},{12,4},{4,0},{1,9},{9... | collective-permute-start | bytes 995336 | tf_op jit(solution)/shard_map/ppermute | solution.py:302
  5.5 1.4 %collective-permute-start.9 = (f32[520,128]{1,0:T(8,128)}, f32[520,128]{1,0:T(8,128)S(1)}, u32[]{:S(2)}, u32[]{:S(2)}) collective-permute-start(f32[520,128]{1,0:T(8,128)} %get-tuple-element.19.refs_0_), channel_id=1, source_target_pairs={{8,0},{16,8},{24,16},{28,24},{20,28},{12,20},{4,12},{0,4},{9,1},{1... | collective-permute-start | bytes 798728 | tf_op jit(solution)/shard_map/ppermute | solution.py:302
  6.9 6.2 %collective-permute-done.5.refs_2_ = f32[648,128]{1,0:T(8,128)S(1)} collective-permute-done((f32[648,128]{1,0:T(8,128)}, f32[648,128]{1,0:T(8,128)S(1)}, u32[]{:S(2)}, u32[]{:S(2)}) %collective-permute-start.5) | collective-permute-done | bytes 331808 | tf_op jit(solution)/shard_map/ppermute | solution.py:302
  15.7 4.1 %collective-permute-done.9.refs_1_ = f32[520,128]{1,0:T(8,128)S(1)} collective-permute-done((f32[520,128]{1,0:T(8,128)}, f32[520,128]{1,0:T(8,128)S(1)}, u32[]{:S(2)}, u32[]{:S(2)}) %collective-permute-start.9) | collective-permute-done | bytes 266272 | tf_op jit(solution)/shard_map/ppermute | solution.py:302
  22.2 4.8 %collective-permute-done.13.refs_2_ = f32[520,128]{1,0:T(8,128)} collective-permute-done((f32[520,128]{1,0:T(8,128)}, f32[520,128]{1,0:T(8,128)}, u32[]{:S(2)}, u32[]{:S(2)}) %collective-permute-start.13) | collective-permute-done | bytes 266272 | tf_op jit(solution)/shard_map/ppermute | solution.py:302
  29.3 1.6 %pad_maximum_fusion = f32[20,32,128]{2,1,0:T(8,128)} fusion(f32[4,32,128]{2,1,0:T(8,128)} %mean.1, f32[16,32,128]{2,1,0:T(8,128)S(1)} %bitcast.9), kind=kLoop, calls=%fused_computation | loop fusion | flops 81920 | bytes 655360 | tf_op jit(solution)/shard_map/concatenate | solution.py:607
  30.9 2.9 %collective-permute-start.1 = (f32[20,32,128]{2,1,0:T(8,128)}, f32[20,32,128]{2,1,0:T(8,128)}, u32[]{:S(2)}, u32[]{:S(2)}) collective-permute-start(f32[20,32,128]{2,1,0:T(8,128)} %pad_maximum_fusion), channel_id=1, source_target_pairs={{0,1},{1,0},{2,3},{3,2},{4,5},{5,4},{6,7},{7,6},{8,9},{9,8},{10,11... | collective-permute-start | bytes 983048 | tf_op jit(solution)/shard_map/ppermute | solution.py:334
  34.0 4.7 %collective-permute-start = (f32[20,32,128]{2,1,0:T(8,128)}, f32[20,32,128]{2,1,0:T(8,128)}, u32[]{:S(2)}, u32[]{:S(2)}) collective-permute-start(f32[20,32,128]{2,1,0:T(8,128)} %pad_maximum_fusion), channel_id=1, source_target_pairs={{1,2},{2,1},{5,6},{6,5},{9,10},{10,9},{13,14},{14,13},{17,18},{18,... | collective-permute-start | bytes 983048 | tf_op jit(solution)/shard_map/ppermute | solution.py:333
  38.7 1.3 %pick.4 = f32[456,128]{1,0:T(8,128)} custom-call(s32[1]{0:T(128)} %bitcast.2.me.me_ref, f32[648,128]{1,0:T(8,128)S(1)} %collective-permute-done.3.block.refs_0_), custom_call_target="tpu_custom_call" | custom-call | flops 40960 | bytes 327680 | tf_op jit(solution)/shard_map/pick/pallas_call | solution.py:166
  40.8 1.3 %pick.5 = f32[456,128]{1,0:T(8,128)} custom-call(s32[1]{0:T(128)} %bitcast.2.me.me_ref, f32[648,128]{1,0:T(8,128)S(1)} %collective-permute-done.7.block.refs_3_), custom_call_target="tpu_custom_call" | custom-call | flops 40960 | bytes 327680 | tf_op jit(solution)/shard_map/pick/pallas_call | solution.py:166
  44.4 1.3 %collective-permute-start.15 = (f32[328,128]{1,0:T(8,128)}, f32[328,128]{1,0:T(8,128)}, u32[]{:S(2)}, u32[]{:S(2)}) collective-permute-start(f32[328,128]{1,0:T(8,128)} %pick.7), channel_id=1, source_target_pairs={{0,8},{8,16},{16,24},{24,28},{28,20},{20,12},{12,4},{4,0},{1,9},{9... | collective-permute-start | bytes 503816 | tf_op jit(solution)/shard_map/ppermute | solution.py:302
  48.2 1.8 %shard_map.79.refs_2_ = f32[1024,128]{1,0:T(8,128)S(1)} custom-call(s32[1]{0:T(128)} %bitcast.2.me.me_ref, s32[2]{0:T(128)S(1)} %copy-done.7, f32[520,128]{1,0:T(8,128)S(1)} %copy-done.3, f32[520,128]{1,0:T(8,128)S(1)} %copy-done.5, f32[520,128]{1,0:T(8,128)} %collective-permute-done.13.refs_2_), custom_call_target="tpu_custom_call" | custom-call | flops 524288 | bytes 1048576 | tf_op jit(solution)/shard_map/pallas_call | solution.py:215
  50.9 2.2 %base.1 = (f32[8,4,32,128]{3,2,1,0:T(8,128)S(1)}, f32[7,12,32,128]{3,2,1,0:T(8,128)S(1)}) custom-call(s32[1]{0:T(128)} %bitcast.space_ref, f32[8,4,32,128]{3,2,1,0:T(8,128)S(1)} %copy-done, f32[8,4,32,128]{3,2,1,0:T(8,128)S(1)} %copy-done.1, f32[4,32,128]{2,1,0:T(8,128)S(1)} %copy-done.6, f32[20,32,128]{2,1,0:T(8,128)} %collective-permute-done.refs_0_, ...), custom_call_target="tpu_custom_call" | custom-call | flops 2621440 | bytes 1048576 | tf_op jit(solution)/shard_map/base/pallas_call | solution.py:611
  53.1 1.3 %shard_map.77.refs_5_ = f32[1280,128]{1,0:T(8,128)S(1)} custom-call(s32[1]{0:T(128)} %bitcast.2.me.me_ref, s32[2]{0:T(128)S(1)} %copy-done.7, f32[648,128]{1,0:T(8,128)S(1)} %copy-done.2, f32[648,128]{1,0:T(8,128)S(1)} %collective-permute-done.2.refs_1_, f32[648,128]{1,0:T(8,128)S(1)} %collective-permute-done.5.refs_2_), custom_call_target="tpu_custom_call" | custom-call | flops 524288 | bytes 1048576 | tf_op jit(solution)/shard_map/pallas_call | solution.py:215
  54.4 1.7 %shard_map.80.refs_3_ = f32[1024,128]{1,0:T(8,128)S(1)} custom-call(s32[1]{0:T(128)} %bitcast.2.me.me_ref, s32[2]{0:T(128)S(1)} %copy-done.7, f32[520,128]{1,0:T(8,128)} %collective-permute-done.10.refs_0_, f32[520,128]{1,0:T(8,128)S(1)} %collective-permute-done.14.block.refs_1_, f32[1024,128]{1,0:T(8,128)S(1)} %shard_map.79.refs_2_), custom_call_target="tpu_custom_call" | custom-call | flops 524288 | bytes 1048576 | tf_op jit(solution)/shard_map/pallas_call | solution.py:215
  56.1 1.8 %shard_map.81.refs_1_ = f32[1024,128]{1,0:T(8,128)S(1)} custom-call(s32[1]{0:T(128)} %bitcast.2.me.me_ref, s32[2]{0:T(128)S(1)} %copy-done.7, f32[520,128]{1,0:T(8,128)S(1)} %collective-permute-done.11.block.refs_0_, f32[328,128]{1,0:T(8,128)} %collective-permute-done.12.refs_1_, f32[328,128]{1,0:T(8,128)} %collective-permute-done.15.refs_2_, ...), custom_call_target="tpu_custom_call" | custom-call | flops 524288 | bytes 1048576 | tf_op jit(solution)/shard_map/pallas_call | solution.py:215
  57.9 2.0 %shard_map.78.sums.refs_0_ = f32[1280,128]{1,0:T(8,128)S(1)} custom-call(s32[1]{0:T(128)} %bitcast.2.me.me_ref, s32[2]{0:T(128)S(1)} %copy-done.7, f32[648,128]{1,0:T(8,128)S(1)} %collective-permute-done.3.block.refs_0_, f32[456,128]{1,0:T(8,128)} %collective-permute-done.4.refs_1_, f32[456,128]{1,0:T(8,128)} %collective-permute-done.8.refs_2_, ...), custom_call_target="tpu_custom_call" | custom-call | flops 524288 | bytes 1048576 | tf_op jit(solution)/shard_map/pallas_call | solution.py:215
  60.9 6.8 %collective-permute-start.18 = (f32[22,32,128]{2,1,0:T(8,128)S(1)}, f32[22,32,128]{2,1,0:T(8,128)S(1)}, u32[]{:S(2)}, u32[]{:S(2)}) collective-permute-start(f32[22,32,128]{2,1,0:T(8,128)S(1)} %get-tuple-element.24), channel_id=1, source_target_pairs={{1,2},{2,1},{5,6},{6,5},{9,10},{10,9},{13,14},{14,13},{17,18},{18,... | collective-permute-start | bytes 1081352 | tf_op jit(solution)/shard_map/ppermute | solution.py:333
  67.8 1.9 %collective-permute-start.16 = (f32[22,32,128]{2,1,0:T(8,128)S(1)}, f32[22,32,128]{2,1,0:T(8,128)S(1)}, u32[]{:S(2)}, u32[]{:S(2)}) collective-permute-start(f32[22,32,128]{2,1,0:T(8,128)S(1)} %get-tuple-element.22), channel_id=1, source_target_pairs={{1,2},{2,1},{5,6},{6,5},{9,10},{10,9},{13,14},{14,13},{17,18},{18,... | collective-permute-start | bytes 1081352 | tf_op jit(solution)/shard_map/ppermute | solution.py:333
  69.8 3.0 %collective-permute-done.18.other = f32[22,32,128]{2,1,0:T(8,128)S(1)} collective-permute-done((f32[22,32,128]{2,1,0:T(8,128)S(1)}, f32[22,32,128]{2,1,0:T(8,128)S(1)}, u32[]{:S(2)}, u32[]{:S(2)}) %collective-permute-start.18) | collective-permute-done | bytes 360480 | tf_op jit(solution)/shard_map/ppermute | solution.py:333
  72.8 2.3 %shard_map.82 = (f32[8,4,32,128]{3,2,1,0:T(8,128)}, f32[8,4,32,128]{3,2,1,0:T(8,128)}) custom-call(s32[1]{0:T(128)} %bitcast.space_ref, f32[8,4,32,128]{3,2,1,0:T(8,128)S(1)} %get-tuple-element.20.rest, f32[7,12,32,128]{3,2,1,0:T(8,128)S(1)} %get-tuple-element.21.face, f32[22,32,128]{2,1,0:T(8,128)S(1)} %collective-permute-done.18.other, ...), custom_call_target="tpu_custom_call" | custom-call | flops 15728640 | bytes 3145728 | tf_op jit(solution)/shard_map/pallas_call | solution.py:650
  75.1 1.5 %collective-permute-done.16.other = f32[22,32,128]{2,1,0:T(8,128)S(1)} collective-permute-done((f32[22,32,128]{2,1,0:T(8,128)S(1)}, f32[22,32,128]{2,1,0:T(8,128)S(1)}, u32[]{:S(2)}, u32[]{:S(2)}) %collective-permute-start.16) | collective-permute-done | bytes 360480 | tf_op jit(solution)/shard_map/ppermute | solution.py:333
  76.6 2.3 %shard_map.83 = (f32[8,4,32,128]{3,2,1,0:T(8,128)}, f32[8,4,32,128]{3,2,1,0:T(8,128)}) custom-call(s32[1]{0:T(128)} %bitcast.space_ref, f32[8,4,32,128]{3,2,1,0:T(8,128)S(1)} %get-tuple-element.20.rest, f32[7,12,32,128]{3,2,1,0:T(8,128)S(1)} %get-tuple-element.21.face, ...), custom_call_target="tpu_custom_call", output_to_operand_aliasing={{0}: (7, {}), {1}: (8, {})} | custom-call | flops 15728640 | bytes 3145728 | tf_op jit(solution)/shard_map/pallas_call | solution.py:650
  (49 shorter events, 14.7 us)
Async XLA Ops:
  3.3 9.8 %collective-permute-start.5 = (f32[648,128]{1,0:T(8,128)}, f32[648,128]{1,0:T(8,128)S(1)}, u32[]{:S(2)}, u32[]{:S(2)}) collective-permute-start(f32[648,128]{1,0:T(8,128)} %get-tuple-element.16.refs_0_), channel_id=1, source_target_pairs={{0,8},{8,16},{16,24},{24,28},{28,20},{20,12},{12,4},{4,0},{1,9},{9... | collective-permute-start | bytes 995336 | tf_op jit(solution)/shard_map/ppermute | solution.py:302
  5.5 14.6 %collective-permute-start.2 = (f32[648,128]{1,0:T(8,128)}, f32[648,128]{1,0:T(8,128)S(1)}, u32[]{:S(2)}, u32[]{:S(2)}) collective-permute-start(f32[648,128]{1,0:T(8,128)} %get-tuple-element.16.refs_0_), channel_id=1, source_target_pairs={{8,0},{16,8},{24,16},{28,24},{20,28},{12,20},{4,12},{0,4},{9,1},{1... | collective-permute-start | bytes 995336 | tf_op jit(solution)/shard_map/ppermute | solution.py:302
  5.5 14.3 %collective-permute-start.9 = (f32[520,128]{1,0:T(8,128)}, f32[520,128]{1,0:T(8,128)S(1)}, u32[]{:S(2)}, u32[]{:S(2)}) collective-permute-start(f32[520,128]{1,0:T(8,128)} %get-tuple-element.19.refs_0_), channel_id=1, source_target_pairs={{8,0},{16,8},{24,16},{28,24},{20,28},{12,20},{4,12},{0,4},{9,1},{1... | collective-permute-start | bytes 798728 | tf_op jit(solution)/shard_map/ppermute | solution.py:302
  13.1 14.9 %collective-permute-start.6 = (f32[648,128]{1,0:T(8,128)S(1)}, f32[648,128]{1,0:T(8,128)S(1)}, u32[]{:S(2)}, u32[]{:S(2)}) collective-permute-start(f32[648,128]{1,0:T(8,128)S(1)} %collective-permute-done.5.refs_2_), channel_id=1, source_target_pairs={{0,8},{8,16},{16,24},{24,28},{28,20},{20,12},{12,4},{4,0},{1,9},{9... | collective-permute-start | bytes 995336 | tf_op jit(solution)/shard_map/ppermute | solution.py:302
  14.4 12.7 %collective-permute-start.13 = (f32[520,128]{1,0:T(8,128)}, f32[520,128]{1,0:T(8,128)}, u32[]{:S(2)}, u32[]{:S(2)}) collective-permute-start(f32[520,128]{1,0:T(8,128)} %get-tuple-element.19.refs_0_), channel_id=1, source_target_pairs={{0,8},{8,16},{16,24},{24,28},{28,20},{20,12},{12,4},{4,0},{1,9},{9... | collective-permute-start | bytes 798728 | tf_op jit(solution)/shard_map/ppermute | solution.py:302
  19.8 14.0 %copy-start.4 = (f32[520,128]{1,0:T(8,128)}, f32[520,128]{1,0:T(8,128)S(1)}, u32[]{:S(2)}) copy-start(f32[520,128]{1,0:T(8,128)S(1)} %collective-permute-done.9.refs_1_) | copy-start | bytes 798724
  19.8 14.0 %collective-permute-start.10 = (f32[520,128]{1,0:T(8,128)S(1)}, f32[520,128]{1,0:T(8,128)}, u32[]{:S(2)}, u32[]{:S(2)}) collective-permute-start(f32[520,128]{1,0:T(8,128)S(1)} %collective-permute-done.9.refs_1_), channel_id=1, source_target_pairs={{8,0},{16,8},{24,16},{28,24},{20,28},{12,20},{4,12},{0,4},{9,1},{1... | collective-permute-start | bytes 798728 | tf_op jit(solution)/shard_map/ppermute | solution.py:302
  20.1 13.9 %collective-permute-start.3 = (f32[648,128]{1,0:T(8,128)S(1)}, f32[648,128]{1,0:T(8,128)S(1)}, u32[]{:S(2)}, u32[]{:S(2)}) collective-permute-start(f32[648,128]{1,0:T(8,128)S(1)} %collective-permute-done.2.refs_1_), channel_id=1, source_target_pairs={{8,0},{16,8},{24,16},{28,24},{20,28},{12,20},{4,12},{0,4},{9,1},{1... | collective-permute-start | bytes 995336 | tf_op jit(solution)/shard_map/ppermute | solution.py:302
  22.1 25.1 %copy-start.3 = (f32[520,128]{1,0:T(8,128)S(1)}, f32[520,128]{1,0:T(8,128)}, u32[]{:S(2)}) copy-start(f32[520,128]{1,0:T(8,128)} %get-tuple-element.19.refs_0_) | copy-start | bytes 798724
  22.2 25.1 %copy-start.7 = (s32[2]{0:T(128)S(1)}, s32[2]{0:T(128)}, u32[]{:S(2)}) copy-start(s32[2]{0:T(128)} %owner_ref.9) | copy-start | bytes 28
  27.0 15.1 %collective-permute-start.14 = (f32[520,128]{1,0:T(8,128)}, f32[520,128]{1,0:T(8,128)S(1)}, u32[]{:S(2)}, u32[]{:S(2)}) collective-permute-start(f32[520,128]{1,0:T(8,128)} %collective-permute-done.13.refs_2_), channel_id=1, source_target_pairs={{0,8},{8,16},{16,24},{24,28},{28,20},{20,12},{12,4},{4,0},{1,9},{9... | collective-permute-start | bytes 798728 | tf_op jit(solution)/shard_map/ppermute | solution.py:302
  28.0 12.2 %collective-permute-start.7 = (f32[648,128]{1,0:T(8,128)S(1)}, f32[648,128]{1,0:T(8,128)S(1)}, u32[]{:S(2)}, u32[]{:S(2)}) collective-permute-start(f32[648,128]{1,0:T(8,128)S(1)} %collective-permute-done.6.refs_4_), channel_id=1, source_target_pairs={{0,8},{8,16},{16,24},{24,28},{28,20},{20,12},{12,4},{4,0},{1,9},{9... | collective-permute-start | bytes 995336 | tf_op jit(solution)/shard_map/ppermute | solution.py:302
  30.9 16.1 %collective-permute-start.1 = (f32[20,32,128]{2,1,0:T(8,128)}, f32[20,32,128]{2,1,0:T(8,128)}, u32[]{:S(2)}, u32[]{:S(2)}) collective-permute-start(f32[20,32,128]{2,1,0:T(8,128)} %pad_maximum_fusion), channel_id=1, source_target_pairs={{0,1},{1,0},{2,3},{3,2},{4,5},{5,4},{6,7},{7,6},{8,9},{9,8},{10,11... | collective-permute-start | bytes 983048 | tf_op jit(solution)/shard_map/ppermute | solution.py:334
  33.8 10.5 %collective-permute-start.11 = (f32[520,128]{1,0:T(8,128)}, f32[520,128]{1,0:T(8,128)S(1)}, u32[]{:S(2)}, u32[]{:S(2)}) collective-permute-start(f32[520,128]{1,0:T(8,128)} %collective-permute-done.10.refs_0_), channel_id=1, source_target_pairs={{8,0},{16,8},{24,16},{28,24},{20,28},{12,20},{4,12},{0,4},{9,1},{1... | collective-permute-start | bytes 798728 | tf_op jit(solution)/shard_map/ppermute | solution.py:302
  34.0 16.0 %collective-permute-start = (f32[20,32,128]{2,1,0:T(8,128)}, f32[20,32,128]{2,1,0:T(8,128)}, u32[]{:S(2)}, u32[]{:S(2)}) collective-permute-start(f32[20,32,128]{2,1,0:T(8,128)} %pad_maximum_fusion), channel_id=1, source_target_pairs={{1,2},{2,1},{5,6},{6,5},{9,10},{10,9},{13,14},{14,13},{17,18},{18,... | collective-permute-start | bytes 983048 | tf_op jit(solution)/shard_map/ppermute | solution.py:333
  40.1 9.9 %copy-start = (f32[8,4,32,128]{3,2,1,0:T(8,128)S(1)}, f32[8,4,32,128]{3,2,1,0:T(8,128)}, u32[]{:S(2)}) copy-start(f32[8,4,32,128]{3,2,1,0:T(8,128)} %coeffs.1) | copy-start | bytes 1572868
  40.2 17.7 %collective-permute-start.4 = (f32[456,128]{1,0:T(8,128)}, f32[456,128]{1,0:T(8,128)}, u32[]{:S(2)}, u32[]{:S(2)}) collective-permute-start(f32[456,128]{1,0:T(8,128)} %pick.4), channel_id=1, source_target_pairs={{8,0},{16,8},{24,16},{28,24},{20,28},{12,20},{4,12},{0,4},{9,1},{1... | collective-permute-start | bytes 700424 | tf_op jit(solution)/shard_map/ppermute | solution.py:302
  42.2 15.8 %collective-permute-start.8 = (f32[456,128]{1,0:T(8,128)}, f32[456,128]{1,0:T(8,128)}, u32[]{:S(2)}, u32[]{:S(2)}) collective-permute-start(f32[456,128]{1,0:T(8,128)} %pick.5), channel_id=1, source_target_pairs={{0,8},{8,16},{16,24},{24,28},{28,20},{20,12},{12,4},{4,0},{1,9},{9... | collective-permute-start | bytes 700424 | tf_op jit(solution)/shard_map/ppermute | solution.py:302
  44.4 11.7 %collective-permute-start.15 = (f32[328,128]{1,0:T(8,128)}, f32[328,128]{1,0:T(8,128)}, u32[]{:S(2)}, u32[]{:S(2)}) collective-permute-start(f32[328,128]{1,0:T(8,128)} %pick.7), channel_id=1, source_target_pairs={{0,8},{8,16},{16,24},{24,28},{28,20},{20,12},{12,4},{4,0},{1,9},{9... | collective-permute-start | bytes 503816 | tf_op jit(solution)/shard_map/ppermute | solution.py:302
  47.0 9.1 %collective-permute-start.12 = (f32[328,128]{1,0:T(8,128)}, f32[328,128]{1,0:T(8,128)}, u32[]{:S(2)}, u32[]{:S(2)}) collective-permute-start(f32[328,128]{1,0:T(8,128)} %pick.6), channel_id=1, source_target_pairs={{8,0},{16,8},{24,16},{28,24},{20,28},{12,20},{4,12},{0,4},{9,1},{1... | collective-permute-start | bytes 503816 | tf_op jit(solution)/shard_map/ppermute | solution.py:302
  60.9 11.9 %collective-permute-start.18 = (f32[22,32,128]{2,1,0:T(8,128)S(1)}, f32[22,32,128]{2,1,0:T(8,128)S(1)}, u32[]{:S(2)}, u32[]{:S(2)}) collective-permute-start(f32[22,32,128]{2,1,0:T(8,128)S(1)} %get-tuple-element.24), channel_id=1, source_target_pairs={{1,2},{2,1},{5,6},{6,5},{9,10},{10,9},{13,14},{14,13},{17,18},{18,... | collective-permute-start | bytes 1081352 | tf_op jit(solution)/shard_map/ppermute | solution.py:333
  67.7 5.1 %collective-permute-start.19 = (f32[22,32,128]{2,1,0:T(8,128)S(1)}, f32[22,32,128]{2,1,0:T(8,128)S(1)}, u32[]{:S(2)}, u32[]{:S(2)}) collective-permute-start(f32[22,32,128]{2,1,0:T(8,128)S(1)} %get-tuple-element.25), channel_id=1, source_target_pairs={{0,1},{1,0},{2,3},{3,2},{4,5},{5,4},{6,7},{7,6},{8,9},{9,8},{10,11... | collective-permute-start | bytes 1081352 | tf_op jit(solution)/shard_map/ppermute | solution.py:334
  67.8 8.9 %collective-permute-start.16 = (f32[22,32,128]{2,1,0:T(8,128)S(1)}, f32[22,32,128]{2,1,0:T(8,128)S(1)}, u32[]{:S(2)}, u32[]{:S(2)}) collective-permute-start(f32[22,32,128]{2,1,0:T(8,128)S(1)} %get-tuple-element.22), channel_id=1, source_target_pairs={{1,2},{2,1},{5,6},{6,5},{9,10},{10,9},{13,14},{14,13},{17,18},{18,... | collective-permute-start | bytes 1081352 | tf_op jit(solution)/shard_map/ppermute | solution.py:333
  69.7 7.0 %collective-permute-start.17 = (f32[22,32,128]{2,1,0:T(8,128)S(1)}, f32[22,32,128]{2,1,0:T(8,128)S(1)}, u32[]{:S(2)}, u32[]{:S(2)}) collective-permute-start(f32[22,32,128]{2,1,0:T(8,128)S(1)} %get-tuple-element.23), channel_id=1, source_target_pairs={{0,1},{1,0},{2,3},{3,2},{4,5},{5,4},{6,7},{7,6},{8,9},{9,8},{10,11... | collective-permute-start | bytes 1081352 | tf_op jit(solution)/shard_map/ppermute | solution.py:334
  (4 other events, 16.6 us)

commit v6 on v5

--- a/solution.py
+++ b/solution.py
@@ -62,7 +62,9 @@
 
 
 def pack_kernel(coef_dev, capacity, rows_of, slot_rows, links, coeffs, bank, *refs):
-    blocks, (sems,) = refs[: len(rows_of)], refs[len(rows_of) :]
+    blocks, (listed, sems, link_sem) = refs[: len(rows_of)], refs[len(rows_of) :]
+    link_copy = pltpu.make_async_copy(links, listed, link_sem)
+    link_copy.start()
     slot = blocks[0].at[pl.ds(coef_dev * rows_of[0], slot_rows)]
     copies = [pltpu.make_async_copy(bank.at[0], slot, sems.at[len(rows_of) * coef_dev])]
     start = 0
@@ -79,8 +81,9 @@
     for copy in copies:
         copy.start()
     entries, lanes = links.shape[1], blocks[0].shape[1]
-    listed = links[...].astype(jnp.float32)
-    s, p, k, level = (listed[i : i + 1] for i in range(4))
+    link_copy.wait()
+    values = listed[...].astype(jnp.float32)
+    s, p, k, level = (values[i : i + 1] for i in range(4))
     device = jnp.floor((p + 0.5) * (1.0 / coef_dev))
     code = (s * coef_dev + p - device * coef_dev) * M + k
     square = (entries, entries)
@@ -120,9 +123,13 @@
     return pl.pallas_call(
         functools.partial(pack_kernel, coef_dev, capacity, rows_of, slot_rows),
         out_shape=[jax.ShapeDtypeStruct((size, lanes), jnp.float32) for size in sizes],
-        in_specs=[VMEM, hbm, hbm],
+        in_specs=[hbm, hbm, hbm],
         out_specs=[VMEM] * len(sizes),
-        scratch_shapes=[pltpu.SemaphoreType.DMA((len(sizes) * coef_dev + 1,))],
+        scratch_shapes=[
+            pltpu.VMEM((links.shape[1], links.shape[0]), jnp.int32),
+            pltpu.SemaphoreType.DMA((len(sizes) * coef_dev + 1,)),
+            pltpu.SemaphoreType.DMA(()),
+        ],
         cost_estimate=cost(coef_dev, sum(rows_of), lanes, 1),
         name="pack",
     )(links.T, whole_rows, slot)
@@ -260,8 +267,8 @@
     half = count // 2
     middle, last = list(range(2, half - 1)), [half - 1, half]
     if chunk == 0:
-        return {"a": [0, 1], "c": middle + last}
-    return {"a": [0, 1], "b": middle, "c": last}
+        return {"a": [0, 1], "b": middle, "c": last}
+    return {"a": [0, 1], "b": middle + last[:1], "c": last[1:]}
 
 
 def chaos_sums(chunks, coef_dev, capacity, rows_of, slot_rows, mode_owner):
@@ -468,10 +475,11 @@
                 message[c * halo : (c + 1) * halo] = rest[part * few + c, first : first + halo]
             for t in range(few * M):
                 message[few * halo + t] = read(part * few * M + t, edge)
-            for k in range(M):
-                message[few * (halo + M) + k] = mode_plane(
-                    sums, layers, depth, nx, targets, k, edge
-                )
+            if part == 0:
+                for k in range(M):
+                    message[few * (halo + M) + k] = mode_plane(
+                        sums, layers, depth, nx, targets, k, edge
+                    )
 
     to_other, to_pair = messages[:PARTS], messages[PARTS:]
 
@@ -487,7 +495,7 @@
 
 
 def sweep_kernel(part, coef_dev, depth, layers, space_ref, rest, face, other, pair, *refs):
-    sums = refs[: depth // layers]
+    first_other, first_pair, *sums = refs[: 2 + depth // layers]
     residual, correction, edges, scaled, first, second = refs[-6:]
     nx = rest.shape[2]
     targets = coef_dev * M
@@ -498,12 +506,17 @@
     def rows(c, l):
         return pl.ds(pl.multiple_of((c * 3 * depth + l) * nx, nx), nx)
 
-    for message, below in ((pair, jnp.logical_not(even)), (other, even)):
+    for message, modes, below in (
+        (pair, first_pair, jnp.logical_not(even)),
+        (other, first_other, even),
+    ):
         at = jnp.where(below, depth - halo, 2 * depth)
         for c in range(few):
             for i in range(halo):
                 scaled[rows(c, at + i), :] = message[c * halo + i]
-        edges[jnp.where(below, 0, 1)] = message[few * halo :]
+        side = jnp.where(below, 0, 1)
+        edges[side, : few * M] = message[few * halo : few * (halo + M)]
+        edges[side, few * M :] = modes[few * (halo + M) :]
     half_modes = [
         [
             0.5 * (mode_plane(sums, layers, depth, nx, targets, k, l) + edges[side, few * M + k])
@@ -633,10 +646,13 @@
         name="begin",
     )(sums[0])
     few = coef_dev // PARTS
-    message = jax.ShapeDtypeStruct((few * (halo + M) + M, nx, ny), jnp.float32)
+    message = [
+        jax.ShapeDtypeStruct((few * (halo + M) + (M if h == 0 else 0), nx, ny), jnp.float32)
+        for h in range(PARTS)
+    ]
     rest, *messages = pl.pallas_call(
         functools.partial(couple_kernel, coef_dev, depth, layers),
-        out_shape=[own] + [message] * (2 * PARTS),
+        out_shape=[own] + message * 2,
         in_specs=[SMEM] + [VMEM] * (3 + len(sums)),
         out_specs=[VMEM] * (1 + 2 * PARTS),
         compiler_params=pltpu.CompilerParams(vmem_limit_bytes=8 << 20),
@@ -646,7 +662,9 @@
     found = []
     for h in range(PARTS):
         other, pair = depth_pair(messages[h], messages[PARTS + h])
-        first = 5 + len(sums)
+        if h == 0:
+            modes = (other, pair)
+        first = 7 + len(sums)
         found = pl.pallas_call(
             functools.partial(sweep_kernel, h, coef_dev, depth, layers),
             grid=(1,),
@@ -660,7 +678,7 @@
             input_output_aliases={first + i: i for i in range(len(found))},
             compiler_params=pltpu.CompilerParams(vmem_limit_bytes=12 << 20),
             cost_estimate=cost(3 * depth * coef_dev, nx, ny, 40),
-        )(index, rest, face, other, pair, *sums, *found)
+        )(index, rest, face, other, pair, *modes, *sums, *found)
     return tuple(found)
 
 

time: 79.5 us -> 80.5 us (1.013)
  local copies, waits for them, and re-layouts: 2.79 us -> 3.73 us
    pallas_call x5 -> x6, Pallas kernels: 8.64 us -> 9.63 us  [sum_blocks(): pl.pallas_call(functools.partial(sum_kernel, picked, shifts, count, coef_...]
    unnamed x16, local copies, waits for them, and re-layouts: 1.82 us -> 2.76 us
  transfers between devices with their start and end apart: 20 -> 20, of which waited for: 6 -> 6; matrix products, arithmetic and copies ran while one was open for 3% -> 3% of each run, Pallas kernels for 21% -> 22%
where the time goes in v6:
time: 80.5 us; the launch traced here: 80 us
  starting transfers between devices  29.6 us (37%)
  Pallas kernels  24.7 us (31%)
  waiting for transfers between devices  19.5 us (24%)
  local copies, waits for them, and re-layouts  3.73 us (5%)
  other arithmetic  1.58 us (2%)
  between operations  0.92 us (1%)
    ppermute x14, waiting for transfers between devices, chaos_sums(): block = lax.ppermute(block, 'chaos', pairs)  15.3 us
    ppermute x3, starting transfers between devices, depth_pair(): other = lax.ppermute(to_other, 'space', second)  13.4 us
    ppermute x14, starting transfers between devices, chaos_sums(): block = lax.ppermute(block, 'chaos', pairs)  13 us
    pallas_call x6, Pallas kernels, sum_blocks(): pl.pallas_call(functools.partial(sum_kernel, picked, shifts, count, coef_...  9.63 us
    pallas_call x4, Pallas kernels, pick(): pl.pallas_call(functools.partial(pick_kernel, coef_dev, capacity, rows, s...  5.26 us
    pallas_call x2, Pallas kernels, residual_and_correction(): pl.pallas_call(functools.partial(sweep_kernel, h, coef_dev, depth, layers...  4.67 us
    ppermute x3, waiting for transfers between devices, depth_pair(): other = lax.ppermute(to_other, 'space', second)  4.18 us
    ppermute x3, starting transfers between devices, depth_pair(): pair = lax.ppermute(to_pair, 'space', first)  3.09 us
  transfers between devices with their start and end apart: 20, of which 6 were waited for; matrix products, arithmetic and copies ran while one was open for 3% of the time, Pallas kernels for 22%

profile of v6, /device:TPU:1, one launch (start us, length us, event | category | flops | bytes accessed | tf_op | source)
XLA Modules:
  0.0 80.0 jit_solution(4414977596600117209)
XLA Ops:
  0.6 2.1 %pack.1 = (f32[648,128]{1,0:T(8,128)}, f32[520,128]{1,0:T(8,128)}) custom-call(s32[4,32]{1,0:T(4,128)} %bitcast.11, f32[8,128,128]{2,1,0:T(8,128)} %bitcast.8, f32[1,128,128]{2,1,0:T(8,128)} %bitcast.10), custom_call_target="tpu_custom_call" | custom-call | flops 131072 | bytes 1048576 | tf_op jit(solution)/shard_map/pack/pallas_call | solution.py:123
  2.7 2.2 %collective-permute-start.5 = (f32[648,128]{1,0:T(8,128)}, f32[648,128]{1,0:T(8,128)S(1)}, u32[]{:S(2)}, u32[]{:S(2)}) collective-permute-start(f32[648,128]{1,0:T(8,128)} %get-tuple-element.16.refs_0_), channel_id=1, source_target_pairs={{0,8},{8,16},{16,24},{24,28},{28,20},{20,12},{12,4},{4,0},{1,9},{9... | collective-permute-start | bytes 995336 | tf_op jit(solution)/shard_map/ppermute | solution.py:309
  4.9 1.4 %collective-permute-start.9 = (f32[520,128]{1,0:T(8,128)}, f32[520,128]{1,0:T(8,128)S(1)}, u32[]{:S(2)}, u32[]{:S(2)}) collective-permute-start(f32[520,128]{1,0:T(8,128)} %get-tuple-element.19.refs_0_), channel_id=1, source_target_pairs={{8,0},{16,8},{24,16},{28,24},{20,28},{12,20},{4,12},{0,4},{9,1},{1... | collective-permute-start | bytes 798728 | tf_op jit(solution)/shard_map/ppermute | solution.py:309
  6.3 6.2 %collective-permute-done.5.refs_2_ = f32[648,128]{1,0:T(8,128)S(1)} collective-permute-done((f32[648,128]{1,0:T(8,128)}, f32[648,128]{1,0:T(8,128)S(1)}, u32[]{:S(2)}, u32[]{:S(2)}) %collective-permute-start.5) | collective-permute-done | bytes 331808 | tf_op jit(solution)/shard_map/ppermute | solution.py:309
  15.1 4.1 %collective-permute-done.9.refs_1_ = f32[520,128]{1,0:T(8,128)S(1)} collective-permute-done((f32[520,128]{1,0:T(8,128)}, f32[520,128]{1,0:T(8,128)S(1)}, u32[]{:S(2)}, u32[]{:S(2)}) %collective-permute-start.9) | collective-permute-done | bytes 266272 | tf_op jit(solution)/shard_map/ppermute | solution.py:309
  21.6 4.9 %collective-permute-done.13.refs_2_ = f32[520,128]{1,0:T(8,128)} collective-permute-done((f32[520,128]{1,0:T(8,128)}, f32[520,128]{1,0:T(8,128)}, u32[]{:S(2)}, u32[]{:S(2)}) %collective-permute-start.13) | collective-permute-done | bytes 266272 | tf_op jit(solution)/shard_map/ppermute | solution.py:309
  28.7 1.6 %pad_maximum_fusion = f32[20,32,128]{2,1,0:T(8,128)} fusion(f32[4,32,128]{2,1,0:T(8,128)} %mean.1, f32[16,32,128]{2,1,0:T(8,128)S(1)} %bitcast.9), kind=kLoop, calls=%fused_computation | loop fusion | flops 81920 | bytes 655360 | tf_op jit(solution)/shard_map/concatenate | solution.py:620
  30.3 2.9 %collective-permute-start.1 = (f32[20,32,128]{2,1,0:T(8,128)}, f32[20,32,128]{2,1,0:T(8,128)}, u32[]{:S(2)}, u32[]{:S(2)}) collective-permute-start(f32[20,32,128]{2,1,0:T(8,128)} %pad_maximum_fusion), channel_id=1, source_target_pairs={{0,1},{1,0},{2,3},{3,2},{4,5},{5,4},{6,7},{7,6},{8,9},{9,8},{10,11... | collective-permute-start | bytes 983048 | tf_op jit(solution)/shard_map/ppermute | solution.py:341
  33.5 4.7 %collective-permute-start = (f32[20,32,128]{2,1,0:T(8,128)}, f32[20,32,128]{2,1,0:T(8,128)}, u32[]{:S(2)}, u32[]{:S(2)}) collective-permute-start(f32[20,32,128]{2,1,0:T(8,128)} %pad_maximum_fusion), channel_id=1, source_target_pairs={{1,2},{2,1},{5,6},{6,5},{9,10},{10,9},{13,14},{14,13},{17,18},{18,... | collective-permute-start | bytes 983048 | tf_op jit(solution)/shard_map/ppermute | solution.py:340
  38.2 1.3 %pick.4 = f32[456,128]{1,0:T(8,128)} custom-call(s32[1]{0:T(128)} %bitcast.2.me.me_ref, f32[648,128]{1,0:T(8,128)S(1)} %collective-permute-done.3.block.refs_0_), custom_call_target="tpu_custom_call" | custom-call | flops 40960 | bytes 327680 | tf_op jit(solution)/shard_map/pick/pallas_call | solution.py:173
  40.2 1.3 %pick.5 = f32[456,128]{1,0:T(8,128)} custom-call(s32[1]{0:T(128)} %bitcast.2.me.me_ref, f32[648,128]{1,0:T(8,128)S(1)} %collective-permute-done.7.block.refs_2_), custom_call_target="tpu_custom_call" | custom-call | flops 40960 | bytes 327680 | tf_op jit(solution)/shard_map/pick/pallas_call | solution.py:173
  42.5 1.3 %pick.7 = f32[328,128]{1,0:T(8,128)} custom-call(s32[1]{0:T(128)} %bitcast.2.me.me_ref, f32[520,128]{1,0:T(8,128)S(1)} %collective-permute-done.14.block.refs_3_), custom_call_target="tpu_custom_call" | custom-call | flops 40960 | bytes 327680 | tf_op jit(solution)/shard_map/pick/pallas_call | solution.py:173
  43.8 1.3 %collective-permute-start.15 = (f32[328,128]{1,0:T(8,128)}, f32[328,128]{1,0:T(8,128)}, u32[]{:S(2)}, u32[]{:S(2)}) collective-permute-start(f32[328,128]{1,0:T(8,128)} %pick.7), channel_id=1, source_target_pairs={{0,8},{8,16},{16,24},{24,28},{28,20},{20,12},{12,4},{4,0},{1,9},{9... | collective-permute-start | bytes 503816 | tf_op jit(solution)/shard_map/ppermute | solution.py:309
  48.6 1.8 %shard_map.80.refs_4_ = f32[1024,128]{1,0:T(8,128)S(1)} custom-call(s32[1]{0:T(128)} %bitcast.2.me.me_ref, s32[2]{0:T(128)S(1)} %copy-done.7, f32[520,128]{1,0:T(8,128)S(1)} %copy-done.3, f32[520,128]{1,0:T(8,128)S(1)} %copy-done.5, f32[520,128]{1,0:T(8,128)} %collective-permute-done.13.refs_2_), custom_call_target="tpu_custom_call" | custom-call | flops 524288 | bytes 1048576 | tf_op jit(solution)/shard_map/pallas_call | solution.py:222
  51.3 2.2 %base.1 = (f32[8,4,32,128]{3,2,1,0:T(8,128)S(1)}, f32[7,12,32,128]{3,2,1,0:T(8,128)S(1)}) custom-call(s32[1]{0:T(128)} %bitcast.space_ref, f32[8,4,32,128]{3,2,1,0:T(8,128)S(1)} %copy-done, f32[8,4,32,128]{3,2,1,0:T(8,128)S(1)} %copy-done.1, f32[4,32,128]{2,1,0:T(8,128)S(1)} %copy-done.6, f32[20,32,128]{2,1,0:T(8,128)} %collective-permute-done.refs_0_, ...), custom_call_target="tpu_custom_call" | custom-call | flops 2621440 | bytes 1048576 | tf_op jit(solution)/shard_map/base/pallas_call | solution.py:624
  53.5 1.3 %shard_map.77.refs_2_ = f32[1280,128]{1,0:T(8,128)S(1)} custom-call(s32[1]{0:T(128)} %bitcast.2.me.me_ref, s32[2]{0:T(128)S(1)} %copy-done.7, f32[648,128]{1,0:T(8,128)S(1)} %copy-done.2, f32[648,128]{1,0:T(8,128)S(1)} %collective-permute-done.2.refs_1_, f32[648,128]{1,0:T(8,128)S(1)} %collective-permute-done.5.refs_2_), custom_call_target="tpu_custom_call" | custom-call | flops 524288 | bytes 1048576 | tf_op jit(solution)/shard_map/pallas_call | solution.py:222
  56.1 1.8 %shard_map.81.refs_1_ = f32[1024,128]{1,0:T(8,128)S(1)} custom-call(s32[1]{0:T(128)} %bitcast.2.me.me_ref, s32[2]{0:T(128)S(1)} %copy-done.7, f32[520,128]{1,0:T(8,128)S(1)} %collective-permute-done.10.refs_0_, f32[520,128]{1,0:T(8,128)S(1)} %collective-permute-done.11.block.refs_1_, f32[328,128]{1,0:T(8,128)} %collective-permute-done.15.refs_2_, ...), custom_call_target="tpu_custom_call" | custom-call | flops 524288 | bytes 1048576 | tf_op jit(solution)/shard_map/pallas_call | solution.py:222
  57.9 1.6 %shard_map.82.refs_1_.refs_3_ = f32[1024,128]{1,0:T(8,128)S(1)} custom-call(s32[1]{0:T(128)} %bitcast.2.me.me_ref, s32[2]{0:T(128)S(1)} %copy-done.7, f32[328,128]{1,0:T(8,128)} %collective-permute-done.12.refs_0_, f32[1024,128]{1,0:T(8,128)S(1)} %shard_map.81.refs_1_), custom_call_target="tpu_custom_call" | custom-call | flops 524288 | bytes 1048576 | tf_op jit(solution)/shard_map/pallas_call | solution.py:222
  59.5 1.9 %shard_map.79.sums.refs_0_.refs_2_ = f32[1280,128]{1,0:T(8,128)S(1)} custom-call(s32[1]{0:T(128)} %bitcast.2.me.me_ref, s32[2]{0:T(128)S(1)} %copy-done.7, f32[456,128]{1,0:T(8,128)} %collective-permute-done.4.refs_0_, f32[456,128]{1,0:T(8,128)} %collective-permute-done.8.refs_1_, f32[648,128]{1,0:T(8,128)S(1)} %collective-permute-done.7.block.refs_2_, ...), custom_call_target="tpu_custom_call" | custom-call | flops 524288 | bytes 1048576 | tf_op jit(solution)/shard_map/pallas_call | solution.py:222
  62.3 6.8 %collective-permute-start.18 = (f32[22,32,128]{2,1,0:T(8,128)S(1)}, f32[22,32,128]{2,1,0:T(8,128)S(1)}, u32[]{:S(2)}, u32[]{:S(2)}) collective-permute-start(f32[22,32,128]{2,1,0:T(8,128)S(1)} %get-tuple-element.24), channel_id=1, source_target_pairs={{1,2},{2,1},{5,6},{6,5},{9,10},{10,9},{13,14},{14,13},{17,18},{18,... | collective-permute-start | bytes 1081352 | tf_op jit(solution)/shard_map/ppermute | solution.py:340
  69.2 1.9 %collective-permute-start.16 = (f32[20,32,128]{2,1,0:T(8,128)S(1)}, f32[20,32,128]{2,1,0:T(8,128)S(1)}, u32[]{:S(2)}, u32[]{:S(2)}) collective-permute-start(f32[20,32,128]{2,1,0:T(8,128)S(1)} %get-tuple-element.22), channel_id=1, source_target_pairs={{1,2},{2,1},{5,6},{6,5},{9,10},{10,9},{13,14},{14,13},{17,18},{18,... | collective-permute-start | bytes 983048 | tf_op jit(solution)/shard_map/ppermute | solution.py:340
  71.2 3.0 %collective-permute-done.18.other.refs_0_ = f32[22,32,128]{2,1,0:T(8,128)S(1)} collective-permute-done((f32[22,32,128]{2,1,0:T(8,128)S(1)}, f32[22,32,128]{2,1,0:T(8,128)S(1)}, u32[]{:S(2)}, u32[]{:S(2)}) %collective-permute-start.18) | collective-permute-done | bytes 360480 | tf_op jit(solution)/shard_map/ppermute | solution.py:340
  74.2 2.3 %shard_map.83 = (f32[8,4,32,128]{3,2,1,0:T(8,128)}, f32[8,4,32,128]{3,2,1,0:T(8,128)}) custom-call(s32[1]{0:T(128)} %bitcast.space_ref, f32[8,4,32,128]{3,2,1,0:T(8,128)S(1)} %get-tuple-element.20.rest, f32[7,12,32,128]{3,2,1,0:T(8,128)S(1)} %get-tuple-element.21.face, f32[22,32,128]{2,1,0:T(8,128)S(1)} %collective-permute-done.18.other.refs_0_, ...), custom_call_target="tpu_custom_call" | custom-call | flops 15728640 | bytes 3145728 | tf_op jit(solution)/shard_map/pallas_call | solution.py:668
  77.7 2.3 %shard_map.84 = (f32[8,4,32,128]{3,2,1,0:T(8,128)}, f32[8,4,32,128]{3,2,1,0:T(8,128)}) custom-call(s32[1]{0:T(128)} %bitcast.space_ref, f32[8,4,32,128]{3,2,1,0:T(8,128)S(1)} %get-tuple-element.20.rest, f32[7,12,32,128]{3,2,1,0:T(8,128)S(1)} %get-tuple-element.21.face, ...), custom_call_target="tpu_custom_call", output_to_operand_aliasing={{0}: (9, {}), {1}: (10, {})} | custom-call | flops 15728640 | bytes 3145728 | tf_op jit(solution)/shard_map/pallas_call | solution.py:668
  (50 shorter events, 16.8 us)
Async XLA Ops:
  2.7 9.8 %collective-permute-start.5 = (f32[648,128]{1,0:T(8,128)}, f32[648,128]{1,0:T(8,128)S(1)}, u32[]{:S(2)}, u32[]{:S(2)}) collective-permute-start(f32[648,128]{1,0:T(8,128)} %get-tuple-element.16.refs_0_), channel_id=1, source_target_pairs={{0,8},{8,16},{16,24},{24,28},{28,20},{20,12},{12,4},{4,0},{1,9},{9... | collective-permute-start | bytes 995336 | tf_op jit(solution)/shard_map/ppermute | solution.py:309
  4.9 14.6 %collective-permute-start.2 = (f32[648,128]{1,0:T(8,128)}, f32[648,128]{1,0:T(8,128)S(1)}, u32[]{:S(2)}, u32[]{:S(2)}) collective-permute-start(f32[648,128]{1,0:T(8,128)} %get-tuple-element.16.refs_0_), channel_id=1, source_target_pairs={{8,0},{16,8},{24,16},{28,24},{20,28},{12,20},{4,12},{0,4},{9,1},{1... | collective-permute-start | bytes 995336 | tf_op jit(solution)/shard_map/ppermute | solution.py:309
  4.9 14.3 %collective-permute-start.9 = (f32[520,128]{1,0:T(8,128)}, f32[520,128]{1,0:T(8,128)S(1)}, u32[]{:S(2)}, u32[]{:S(2)}) collective-permute-start(f32[520,128]{1,0:T(8,128)} %get-tuple-element.19.refs_0_), channel_id=1, source_target_pairs={{8,0},{16,8},{24,16},{28,24},{20,28},{12,20},{4,12},{0,4},{9,1},{1... | collective-permute-start | bytes 798728 | tf_op jit(solution)/shard_map/ppermute | solution.py:309
  12.5 14.9 %collective-permute-start.6 = (f32[648,128]{1,0:T(8,128)S(1)}, f32[648,128]{1,0:T(8,128)S(1)}, u32[]{:S(2)}, u32[]{:S(2)}) collective-permute-start(f32[648,128]{1,0:T(8,128)S(1)} %collective-permute-done.5.refs_2_), channel_id=1, source_target_pairs={{0,8},{8,16},{16,24},{24,28},{28,20},{20,12},{12,4},{4,0},{1,9},{9... | collective-permute-start | bytes 995336 | tf_op jit(solution)/shard_map/ppermute | solution.py:309
  13.8 12.7 %collective-permute-start.13 = (f32[520,128]{1,0:T(8,128)}, f32[520,128]{1,0:T(8,128)}, u32[]{:S(2)}, u32[]{:S(2)}) collective-permute-start(f32[520,128]{1,0:T(8,128)} %get-tuple-element.19.refs_0_), channel_id=1, source_target_pairs={{0,8},{8,16},{16,24},{24,28},{28,20},{20,12},{12,4},{4,0},{1,9},{9... | collective-permute-start | bytes 798728 | tf_op jit(solution)/shard_map/ppermute | solution.py:309
  19.2 14.0 %copy-start.4 = (f32[520,128]{1,0:T(8,128)}, f32[520,128]{1,0:T(8,128)S(1)}, u32[]{:S(2)}) copy-start(f32[520,128]{1,0:T(8,128)S(1)} %collective-permute-done.9.refs_1_) | copy-start | bytes 798724
  19.2 14.0 %collective-permute-start.10 = (f32[520,128]{1,0:T(8,128)S(1)}, f32[520,128]{1,0:T(8,128)S(1)}, u32[]{:S(2)}, u32[]{:S(2)}) collective-permute-start(f32[520,128]{1,0:T(8,128)S(1)} %collective-permute-done.9.refs_1_), channel_id=1, source_target_pairs={{8,0},{16,8},{24,16},{28,24},{20,28},{12,20},{4,12},{0,4},{9,1},{1... | collective-permute-start | bytes 798728 | tf_op jit(solution)/shard_map/ppermute | solution.py:309
  19.5 13.9 %collective-permute-start.3 = (f32[648,128]{1,0:T(8,128)S(1)}, f32[648,128]{1,0:T(8,128)S(1)}, u32[]{:S(2)}, u32[]{:S(2)}) collective-permute-start(f32[648,128]{1,0:T(8,128)S(1)} %collective-permute-done.2.refs_1_), channel_id=1, source_target_pairs={{8,0},{16,8},{24,16},{28,24},{20,28},{12,20},{4,12},{0,4},{9,1},{1... | collective-permute-start | bytes 995336 | tf_op jit(solution)/shard_map/ppermute | solution.py:309
  21.6 25.1 %copy-start.7 = (s32[2]{0:T(128)S(1)}, s32[2]{0:T(128)}, u32[]{:S(2)}) copy-start(s32[2]{0:T(128)} %owner_ref.11) | copy-start | bytes 28
  26.5 15.1 %collective-permute-start.14 = (f32[520,128]{1,0:T(8,128)}, f32[520,128]{1,0:T(8,128)S(1)}, u32[]{:S(2)}, u32[]{:S(2)}) collective-permute-start(f32[520,128]{1,0:T(8,128)} %collective-permute-done.13.refs_2_), channel_id=1, source_target_pairs={{0,8},{8,16},{16,24},{24,28},{28,20},{20,12},{12,4},{4,0},{1,9},{9... | collective-permute-start | bytes 798728 | tf_op jit(solution)/shard_map/ppermute | solution.py:309
  27.4 12.2 %collective-permute-start.7 = (f32[648,128]{1,0:T(8,128)S(1)}, f32[648,128]{1,0:T(8,128)S(1)}, u32[]{:S(2)}, u32[]{:S(2)}) collective-permute-start(f32[648,128]{1,0:T(8,128)S(1)} %collective-permute-done.6.refs_1_), channel_id=1, source_target_pairs={{0,8},{8,16},{16,24},{24,28},{28,20},{20,12},{12,4},{4,0},{1,9},{9... | collective-permute-start | bytes 995336 | tf_op jit(solution)/shard_map/ppermute | solution.py:309
  30.3 16.1 %collective-permute-start.1 = (f32[20,32,128]{2,1,0:T(8,128)}, f32[20,32,128]{2,1,0:T(8,128)}, u32[]{:S(2)}, u32[]{:S(2)}) collective-permute-start(f32[20,32,128]{2,1,0:T(8,128)} %pad_maximum_fusion), channel_id=1, source_target_pairs={{0,1},{1,0},{2,3},{3,2},{4,5},{5,4},{6,7},{7,6},{8,9},{9,8},{10,11... | collective-permute-start | bytes 983048 | tf_op jit(solution)/shard_map/ppermute | solution.py:341
  33.3 10.5 %collective-permute-start.11 = (f32[520,128]{1,0:T(8,128)S(1)}, f32[520,128]{1,0:T(8,128)S(1)}, u32[]{:S(2)}, u32[]{:S(2)}) collective-permute-start(f32[520,128]{1,0:T(8,128)S(1)} %collective-permute-done.10.refs_0_), channel_id=1, source_target_pairs={{8,0},{16,8},{24,16},{28,24},{20,28},{12,20},{4,12},{0,4},{9,1},{1... | collective-permute-start | bytes 798728 | tf_op jit(solution)/shard_map/ppermute | solution.py:309
  33.5 17.0 %collective-permute-start = (f32[20,32,128]{2,1,0:T(8,128)}, f32[20,32,128]{2,1,0:T(8,128)}, u32[]{:S(2)}, u32[]{:S(2)}) collective-permute-start(f32[20,32,128]{2,1,0:T(8,128)} %pad_maximum_fusion), channel_id=1, source_target_pairs={{1,2},{2,1},{5,6},{6,5},{9,10},{10,9},{13,14},{14,13},{17,18},{18,... | collective-permute-start | bytes 983048 | tf_op jit(solution)/shard_map/ppermute | solution.py:340
  39.5 10.9 %copy-start = (f32[8,4,32,128]{3,2,1,0:T(8,128)S(1)}, f32[8,4,32,128]{3,2,1,0:T(8,128)}, u32[]{:S(2)}) copy-start(f32[8,4,32,128]{3,2,1,0:T(8,128)} %coeffs.1) | copy-start | bytes 1572868
  39.5 10.9 %copy-start.1 = (f32[8,4,32,128]{3,2,1,0:T(8,128)S(1)}, f32[8,4,32,128]{3,2,1,0:T(8,128)}, u32[]{:S(2)}) copy-start(f32[8,4,32,128]{3,2,1,0:T(8,128)} %source.1) | copy-start | bytes 1572868
  39.6 19.9 %collective-permute-start.4 = (f32[456,128]{1,0:T(8,128)}, f32[456,128]{1,0:T(8,128)}, u32[]{:S(2)}, u32[]{:S(2)}) collective-permute-start(f32[456,128]{1,0:T(8,128)} %pick.4), channel_id=1, source_target_pairs={{8,0},{16,8},{24,16},{28,24},{20,28},{12,20},{4,12},{0,4},{9,1},{1... | collective-permute-start | bytes 700424 | tf_op jit(solution)/shard_map/ppermute | solution.py:309
  41.6 17.9 %collective-permute-start.8 = (f32[456,128]{1,0:T(8,128)}, f32[456,128]{1,0:T(8,128)}, u32[]{:S(2)}, u32[]{:S(2)}) collective-permute-start(f32[456,128]{1,0:T(8,128)} %pick.5), channel_id=1, source_target_pairs={{0,8},{8,16},{16,24},{24,28},{28,20},{20,12},{12,4},{4,0},{1,9},{9... | collective-permute-start | bytes 700424 | tf_op jit(solution)/shard_map/ppermute | solution.py:309
  43.8 12.3 %collective-permute-start.15 = (f32[328,128]{1,0:T(8,128)}, f32[328,128]{1,0:T(8,128)}, u32[]{:S(2)}, u32[]{:S(2)}) collective-permute-start(f32[328,128]{1,0:T(8,128)} %pick.7), channel_id=1, source_target_pairs={{0,8},{8,16},{16,24},{24,28},{28,20},{20,12},{12,4},{4,0},{1,9},{9... | collective-permute-start | bytes 503816 | tf_op jit(solution)/shard_map/ppermute | solution.py:309
  46.5 11.4 %collective-permute-start.12 = (f32[328,128]{1,0:T(8,128)}, f32[328,128]{1,0:T(8,128)}, u32[]{:S(2)}, u32[]{:S(2)}) collective-permute-start(f32[328,128]{1,0:T(8,128)} %pick.6), channel_id=1, source_target_pairs={{8,0},{16,8},{24,16},{28,24},{20,28},{12,20},{4,12},{0,4},{9,1},{1... | collective-permute-start | bytes 503816 | tf_op jit(solution)/shard_map/ppermute | solution.py:309
  62.3 11.9 %collective-permute-start.18 = (f32[22,32,128]{2,1,0:T(8,128)S(1)}, f32[22,32,128]{2,1,0:T(8,128)S(1)}, u32[]{:S(2)}, u32[]{:S(2)}) collective-permute-start(f32[22,32,128]{2,1,0:T(8,128)S(1)} %get-tuple-element.24), channel_id=1, source_target_pairs={{1,2},{2,1},{5,6},{6,5},{9,10},{10,9},{13,14},{14,13},{17,18},{18,... | collective-permute-start | bytes 1081352 | tf_op jit(solution)/shard_map/ppermute | solution.py:340
  69.1 5.1 %collective-permute-start.19 = (f32[22,32,128]{2,1,0:T(8,128)S(1)}, f32[22,32,128]{2,1,0:T(8,128)S(1)}, u32[]{:S(2)}, u32[]{:S(2)}) collective-permute-start(f32[22,32,128]{2,1,0:T(8,128)S(1)} %get-tuple-element.25), channel_id=1, source_target_pairs={{0,1},{1,0},{2,3},{3,2},{4,5},{5,4},{6,7},{7,6},{8,9},{9,8},{10,11... | collective-permute-start | bytes 1081352 | tf_op jit(solution)/shard_map/ppermute | solution.py:341
  69.2 8.5 %collective-permute-start.16 = (f32[20,32,128]{2,1,0:T(8,128)S(1)}, f32[20,32,128]{2,1,0:T(8,128)S(1)}, u32[]{:S(2)}, u32[]{:S(2)}) collective-permute-start(f32[20,32,128]{2,1,0:T(8,128)S(1)} %get-tuple-element.22), channel_id=1, source_target_pairs={{1,2},{2,1},{5,6},{6,5},{9,10},{10,9},{13,14},{14,13},{17,18},{18,... | collective-permute-start | bytes 983048 | tf_op jit(solution)/shard_map/ppermute | solution.py:340
  71.1 6.6 %collective-permute-start.17 = (f32[20,32,128]{2,1,0:T(8,128)S(1)}, f32[20,32,128]{2,1,0:T(8,128)S(1)}, u32[]{:S(2)}, u32[]{:S(2)}) collective-permute-start(f32[20,32,128]{2,1,0:T(8,128)S(1)} %get-tuple-element.23), channel_id=1, source_target_pairs={{0,1},{1,0},{2,3},{3,2},{4,5},{5,4},{6,7},{7,6},{8,9},{9,8},{10,11... | collective-permute-start | bytes 983048 | tf_op jit(solution)/shard_map/ppermute | solution.py:341
  (4 other events, 7.6 us)
